TPU v7x, 32 devices: a whole 2x2x4 slice. The times are simulated.
32 devices in a mesh: parts: 2 (over x), blk: 16 (over z, y, core).
Axes of the slice: x: 2, y: 2, z: 4, core: 2. Of those that a mesh axis runs over, the one named last changes fastest.
Arguments:
- particles: bfloat16 [4096, 4608], P(('parts', 'blk')), parts along dimension 0, may hold values from -24 to 24
- references: bfloat16 [64, 4608], P(('parts', 'blk')), parts along dimension 0, may hold values from -0.5 to 0.5
- inv_noise: float32 [4096], P(('parts', 'blk')), parts along dimension 0, may hold values from 1 to 4
- assign: int32 [4096, 2], P(('parts', 'blk')), parts along dimension 0, may hold values from 0 to 31, all different within a row; in each aligned block of 128 rows (0 to 127, 128 to 255, ...) at most 16 rows name the same one
Outputs:
- class_sums: float32 [64, 4608], P(('parts', 'blk')), parts along dimension 0
- class_mass: float32 [64], P(('parts', 'blk')), parts along dimension 0
- log_evidence: float32 [4096], P(('parts', 'blk')), parts along dimension 0
There are 2 independent parts, one for each index of `parts`. A program takes and returns all parts, laid end to end along the dimension named above; each array names one. Nothing has to cross between parts.
Inputs may be any that keep to these rules, and one draw needn't show every extreme that they name: `assign`: among the rows of one device, at most 16 name any one class; in every draw some device's block reaches this bound.
All inputs are finite; a program needn't handle non-finite values.
Results may differ from a plain program's by a relative error of at most 0.0039.
Values may be sent and summed in bfloat16 or wider, within the bound.
No kernel may reach another device: no remote copies, remote signals or barrier semaphores. Data moves between devices by JAX's collectives and lax.ppermute only.
A program may use at most 128 MiB of HBM per device.

v0:
```python
import jax
import jax.numpy as jnp
from jax import lax
from jax.sharding import PartitionSpec as P

ROT = 12
TOPK = 2
CYCLES = 12
ANGLES = 384


def local(particles, references, inv_noise, assign):
    local_rows = particles.shape[0]
    width = particles.shape[1]
    owned = references.shape[0]
    devices = lax.axis_size("blk")
    classes = owned * devices
    step = ANGLES // ROT
    piece = lax.all_gather(references, "blk", axis=0, tiled=True)
    count = piece.shape[0]
    cube = piece.reshape(count, CYCLES, ANGLES)
    turned = jnp.stack([jnp.roll(cube, r * step, axis=2) for r in range(ROT)], axis=1)
    turned = turned.reshape(count * ROT, width)
    dots = lax.dot_general(
        particles, turned, (((1,), (1,)), ((), ())), preferred_element_type=jnp.float32
    )
    energy = jnp.sum(jnp.square(piece.astype(jnp.float32)), axis=1)
    logits = inv_noise[:, None] * (dots - 0.5 * jnp.repeat(energy, ROT)[None, :])
    top = jnp.max(logits, axis=1, keepdims=True)
    total = jnp.sum(jnp.exp(logits - top), axis=1, keepdims=True)
    log_evidence = top + jnp.log(total)
    post = jnp.exp(logits - log_evidence).reshape(local_rows, classes, ROT)
    picked = jnp.take_along_axis(post, assign[:, :, None], axis=1)
    blocks_b = jnp.arange(ROT, dtype=jnp.int32)[:, None, None]
    blocks_c = jnp.arange(ROT, dtype=jnp.int32)[None, :, None]
    shifts = jnp.arange(ROT, dtype=jnp.int32)[None, None, :]
    circulant = ((blocks_c - blocks_b) % ROT == shifts).astype(jnp.float32)
    mixing = jnp.einsum("pjr,bcr->pjbc", picked, circulant, precision=lax.Precision.HIGHEST)
    blocked = particles.reshape(local_rows, CYCLES, ROT, step).transpose(0, 2, 1, 3)
    blocked = blocked.reshape(local_rows, ROT, CYCLES * step).astype(jnp.float32)
    summed = jnp.einsum("pjbc,pcm->pjbm", mixing, blocked, precision=lax.Precision.HIGHEST)
    summed = summed.astype(jnp.bfloat16).reshape(local_rows, TOPK, ROT, CYCLES, step)
    flat_rows = summed.transpose(0, 1, 3, 2, 4).reshape(local_rows * TOPK, width)
    flat_weights = jnp.sum(picked, axis=2).astype(jnp.bfloat16).reshape(local_rows * TOPK)
    flat_class = assign.reshape(local_rows * TOPK)
    selector = (flat_class[:, None] == jnp.arange(classes, dtype=jnp.int32)[None, :]).astype(
        jnp.bfloat16
    )
    partial_sums = lax.dot_general(
        selector, flat_rows, (((0,), (0,)), ((), ())), preferred_element_type=jnp.float32
    )
    partial_mass = lax.dot_general(
        selector,
        flat_weights[:, None],
        (((0,), (0,)), ((), ())),
        preferred_element_type=jnp.float32,
    )[:, 0]
    class_sums, class_mass = (
        lax.psum_scatter(partial_sums, "blk", scatter_dimension=0, tiled=True),
        lax.psum_scatter(partial_mass, "blk", scatter_dimension=0, tiled=True),
    )
    return (class_sums, class_mass, log_evidence[:, 0])


def solution(mesh):
    placed = (
        P(("parts", "blk"), None),
        P(("parts", "blk"), None),
        P(("parts", "blk")),
        P(("parts", "blk"), None),
    )
    return jax.shard_map(
        local,
        mesh=mesh,
        in_specs=placed,
        out_specs=(P(("parts", "blk"), None), P(("parts", "blk")), P(("parts", "blk"))),
        check_vma=False,
    )
```

profile of v0, /device:TPU:0, one launch (start us, length us, event | category | flops | bytes accessed | tf_op | source)
XLA Modules:
  0.0 207.3 jit_solution(18054935562386416470)
XLA Ops:
  7.2 24.1 %all-gather = bf16[16,2,4608]{2,1,0:T(2,128)(2,1)S(1)} all-gather(bf16[1,2,4608]{2,1,0:T(2,128)(2,1)} %bitcast.89), channel_id=1, replica_groups=mesh['parts'=2,'blk'=16] {'blk'}, dimensions={0}, use_global_device_ids=true | all-gather | bytes 313344 | tf_op jit(solution)/shard_map/all_gather | solution.py:19
  40.6 1.2 fusion.1
  41.8 1.1 fusion.2
  42.9 1.1 fusion.3
  44.1 1.1 fusion.4
  45.1 1.2 fusion.5
  46.7 1.1 fusion.8
  47.8 1.0 fusion.9
  48.8 1.0 fusion.10
  50.9 2.8 %copy.47 = bf16[48,8,12,384]{3,1,2,0:T(8,128)(2,1)} copy(bf16[48,8,12,384]{3,2,1,0:T(8,128)(2,1)S(1)} %bitcast.83) | data formatting | bytes 7077888
  54.0 1.0 copy.36
  55.0 3.1 %fusion.38 = (f32[128]{0:T(128)S(1)}, f32[384,128]{1,0:T(8,128)S(1)}) fusion(f32[384]{0:T(512)S(1)} %mul.27, bf16[384,4608]{1,0:T(8,128)(2,1)} %bitcast.87, bf16[128,4608]{1,0:T(8,128)(2,1)S(1)} %copy-done, f32[128]{0:T(128)S(1)} %copy-done.10), kind=kOutput, calls=%fused_computation.67 | convolution fusion | flops 453132160 | bytes 4917760 | tf_op jit(solution)/shard_map/dot_general | solution.py:24
  58.8 1.8 copy.34
  60.8 1.9 gather_fusion
  63.8 2.9 %copy.38 = f32[128,2,12,12]{3,2,1,0:T(8,128)} copy(f32[128,2,12,12]{0,3,2,1:T(8,128)S(1)} %fusion.14) | data formatting | bytes 294912 | tf_op jit(solution)/shard_map/pjr,bcr->pjbc/dot_general | solution.py:38
  66.9 2.1 %copy.44 = bf16[128,12,384,1]{2,1,3,0:T(8,128)(2,1)} copy(bf16[128,12,384,1]{0,2,1,3:T(8,128)(2,1)S(1)} %bitcast.86) | data formatting | bytes 2359296 | tf_op jit(solution)/shard_map/reshape | solution.py:40
  69.0 4.6 %convolution_convert_fusion = bf16[128,2,12,384]{3,2,1,0:T(8,128)(2,1)S(1)} fusion(f32[128,2,12,12]{3,2,1,0:T(8,128)} %copy.38, bf16[128,12,384,1]{2,1,3,0:T(8,128)(2,1)} %copy.44), kind=kOutput, calls=%fused_computation.1 | convolution fusion | flops 171048960 | bytes 3686400 | tf_op jit(solution)/shard_map/pjbc,pcm->pjbm/dot_general | solution.py:41
  73.7 3.2 %copy.40 = bf16[128,2,12,384]{0,3,2,1:T(8,128)(2,1)} copy(bf16[128,2,12,384]{3,2,1,0:T(8,128)(2,1)S(1)} %convolution_convert_fusion) | data formatting | bytes 4718592 | tf_op jit(solution)/shard_map/convert_element_type | solution.py:42
  76.9 18.2 %copy.41 = bf16[128,2,12,12,32]{4,3,2,1,0:T(8,128)(2,1)} copy(bf16[128,2,12,12,32]{0,4,2,3,1:T(8,128)(2,1)} %bitcast.84) | data formatting | bytes 4718592 | tf_op jit(solution)/shard_map/transpose | solution.py:43
  95.1 13.2 %reshape.95 = bf16[256,4608]{1,0:T(8,128)(2,1)S(1)} reshape(bf16[128,2,12,12,32]{4,3,2,1,0:T(8,128)(2,1)} %copy.41) | data formatting | bytes 4718592 | tf_op jit(solution)/shard_map/reshape | solution.py:43
  108.4 1.4 fusion.12
  111.7 30.0 %all-reduce.1 = f32[32]{0:T(128)S(1)} all-reduce(f32[32]{0:T(128)S(1)} %convolution_bitcast_fusion), channel_id=3, replica_groups=mesh['parts'=2,'blk'=16] {'blk'}, use_global_device_ids=true, to_apply=%region_5.6.clone | all-reduce | flops 32 | bytes 256
  142.3 56.6 %all-reduce.4.cloned.1.call-done = f32[32,4608]{1,0:T(8,128)} async-done(((f32[32,4608]{1,0:T(8,128)}), f32[32,4608]{1,0:T(8,128)}) %all-reduce.4.cloned.1.call-update) | async-done | bytes 589840
  198.9 1.5 constant_dynamic-slice_fusion
  (69 shorter events, 14.9 us)
Async XLA Ops:
  7.2 191.7 %all-reduce.4.cloned.1.call-start = ((), (), s32[]{:S(2)}) async-start(), calls=%async_computation | async-start | bytes 1179648
  32.7 6.5 %copy-start.7 = (s32[128,2]{0,1:T(2,128)S(1)}, s32[128,2]{0,1:T(2,128)}, u32[]{:S(2)}) copy-start(s32[128,2]{0,1:T(2,128)} %param.7) | copy-start | bytes 3076
  38.9 7.7 %copy-start.1 = (bf16[32,12,224]{2,1,0:T(8,128)(2,1)S(1)}, bf16[32,12,224]{2,1,0:T(8,128)(2,1)}, u32[]{:S(2)}) copy-start(bf16[32,12,224]{2,1,0:T(8,128)(2,1)} %get-tuple-element.19) | copy-start | bytes 516100
  39.3 7.3 %copy-start.2 = (bf16[32,12,160]{2,1,0:T(8,128)(2,1)S(1)}, bf16[32,12,160]{2,1,0:T(8,128)(2,1)}, u32[]{:S(2)}) copy-start(bf16[32,12,160]{2,1,0:T(8,128)(2,1)} %get-tuple-element.21) | copy-start | bytes 368644
  40.5 5.8 %copy-start.3 = (bf16[32,12,192]{2,1,0:T(8,128)(2,1)S(1)}, bf16[32,12,192]{2,1,0:T(8,128)(2,1)}, u32[]{:S(2)}) copy-start(bf16[32,12,192]{2,1,0:T(8,128)(2,1)} %get-tuple-element.23) | copy-start | bytes 442372
  40.5 5.8 %copy-start.4 = (bf16[32,12,192]{2,1,0:T(8,128)(2,1)S(1)}, bf16[32,12,192]{2,1,0:T(8,128)(2,1)}, u32[]{:S(2)}) copy-start(bf16[32,12,192]{2,1,0:T(8,128)(2,1)} %get-tuple-element.24) | copy-start | bytes 442372
  40.5 9.3 %copy-start.5 = (bf16[32,12,32]{2,1,0:T(8,128)(2,1)S(1)}, bf16[32,12,32]{2,1,0:T(8,128)(2,1)}, u32[]{:S(2)}) copy-start(bf16[32,12,32]{2,1,0:T(8,128)(2,1)} %get-tuple-element.5) | copy-start | bytes 73732
  50.9 3.1 %copy-start = (bf16[128,4608]{1,0:T(8,128)(2,1)S(1)}, bf16[128,4608]{1,0:T(8,128)(2,1)}, u32[]{:S(2)}) copy-start(bf16[128,4608]{1,0:T(8,128)(2,1)} %param.4) | copy-start | bytes 3538948
  50.9 4.1 %copy-start.10 = (f32[128]{0:T(128)S(1)}, f32[128]{0:T(128)}, u32[]{:S(2)}) copy-start(f32[128]{0:T(128)} %param.6) | copy-start | bytes 1540
  58.2 0.5 copy-start.9
  95.1 13.2 %copy-start.6 = (s32[128,2]{1,0:T(8,128)S(1)}, s32[128,2]{1,0:T(8,128)}, u32[]{:S(2)}) copy-start(s32[128,2]{1,0:T(8,128)} %copy.31) | copy-start | bytes 3076
  95.1 14.9 %copy-start.8 = (pred[128,2]{0,1:T(4,128)(4,1)S(1)}, pred[128,2]{0,1:T(4,128)(4,1)}, u32[]{:S(2)}) copy-start(pred[128,2]{0,1:T(4,128)(4,1)} %compare_and_fusion) | copy-start | bytes 772
  95.1 15.2 %copy-start.11 = (u32[32]{0:T(128)S(1)}, u32[32]{0:T(128)}, u32[]{:S(2)}) copy-start(u32[32]{0:T(128)} %constant.47) | copy-start | bytes 388
Sparse Core Ops, SparseCore 0:
  110.0 88.8 all-reduce.3
where the time goes:
time: 208 us; the launch traced here: 207 us
  local copies, waits for them, and re-layouts  60.8 us (29%)
  waiting for transfers between devices  56.6 us (27%)
  blocking collectives  54.2 us (26%)
  between operations  14.9 us (7%)
  other arithmetic  10.5 us (5%)
  matrix products  10.3 us (5%)
    unnamed x2, waiting for transfers between devices  56.6 us
    unnamed x1, blocking collectives  30 us
    all_gather x1, blocking collectives, local(): piece = lax.all_gather(references, 'blk', axis=0, tiled=True)  24.1 us
    transpose x1, local copies, waits for them, and re-layouts, local(): summed.transpose(0, 1, 3, 2, 4).reshape(local_rows * TOPK, width)  18.2 us
    reshape x1, local copies, waits for them, and re-layouts, local(): summed.transpose(0, 1, 3, 2, 4).reshape(local_rows * TOPK, width)  13.2 us
    unnamed x10, other arithmetic  9.24 us
    unnamed x31, local copies, waits for them, and re-layouts  7.83 us
    slice x11, local copies, waits for them, and re-layouts, local(): jnp.roll(cube, r * step, axis=2)  7.09 us
  transfers between devices with their start and end apart: 1, of which 1 were waited for; matrix products, arithmetic and copies ran while one was open for 1% of the time, Pallas kernels for 0%

commit v1 on v0

v1 whole, which is shorter than its diff:
```python
import functools

import jax
import jax.numpy as jnp
from jax import lax
from jax.experimental import pallas as pl
from jax.experimental.pallas import tpu as pltpu
from jax.sharding import PartitionSpec as P

ROT = 12
CYCLES = 12
ANGLES = 384
LANES = 128
STEP = ANGLES // ROT
FINE = LANES // STEP
COARSE = ROT // FINE


def assign_kernel(bits, p_ref, refs_ref, noise_ref, assign_ref, keep_ref, send_ref, log_ref, turned_ref):
    classes = refs_ref.shape[0]
    owned = classes >> bits
    half = classes // 2
    group = FINE * classes
    me = lax.axis_index("blk")

    energy = jnp.zeros((classes, LANES), jnp.float32)
    for c in range(CYCLES):
        cube = refs_ref[:, c * ANGLES:(c + 1) * ANGLES].astype(jnp.float32)
        for v in range(COARSE):
            piece = cube[:, v * LANES:(v + 1) * LANES]
            energy = energy + piece * piece
        for s in range(FINE):
            moved = (cube if s == 0 else pltpu.roll(cube, s * STEP, 1)).astype(jnp.bfloat16)
            for q in range(COARSE):
                for v in range(COARSE):
                    at = c * ANGLES + (v + q) % COARSE * LANES
                    turned_ref[q * group + s * classes:q * group + (s + 1) * classes, at:at + LANES] = (
                        moved[:, v * LANES:(v + 1) * LANES]
                    )
    energy = jnp.sum(energy, axis=1, keepdims=True)

    dots = lax.dot_general(
        turned_ref[...], p_ref[...], (((1,), (1,)), ((), ())), preferred_element_type=jnp.float32
    )
    rows = dots.shape[1]
    dots = dots.reshape(ROT, classes, rows)
    logits = noise_ref[...][None] * (dots - 0.5 * energy[None])
    top = jnp.max(jnp.max(logits, axis=0), axis=0, keepdims=True)
    grown = jnp.exp(logits - top[None])
    total = jnp.sum(jnp.sum(grown, axis=0), axis=0, keepdims=True)
    log_ref[...] = top + jnp.log(total)

    row = lax.broadcasted_iota(jnp.int32, (classes, rows), 0)
    place = row // owned
    mixed = jnp.zeros_like(place)
    for i in range(bits):
        mixed = mixed + (((place >> i) & 1) << (bits - 1 - i))
    ident = (mixed ^ me) * owned + row % owned
    named = (ident == assign_ref[0:1, :]) | (ident == assign_ref[1:2, :])
    scale = jnp.where(named, 1.0 / total, 0.0)
    post = grown * scale[None]
    weights = jnp.sum(post, axis=0).astype(jnp.bfloat16).astype(jnp.float32)
    mass = jnp.broadcast_to(jnp.sum(weights, axis=1, keepdims=True), (classes, LANES))

    post = post.reshape(COARSE, group, rows)
    post = jnp.concatenate([post[q] for q in range(COARSE)], axis=1)
    high = post.astype(jnp.bfloat16)
    low = (post - high.astype(jnp.float32)).astype(jnp.bfloat16)
    both = jnp.concatenate([high, low], axis=0)
    for c in range(CYCLES):
        pieces = [p_ref[:, c * ANGLES + v * LANES:c * ANGLES + (v + 1) * LANES] for v in range(COARSE)]
        stacked = jnp.concatenate(
            [jnp.concatenate([pieces[(v + q) % COARSE] for v in range(COARSE)], axis=1) for q in range(COARSE)],
            axis=0,
        )
        part = jnp.dot(both, stacked, preferred_element_type=jnp.float32)
        part = part[:group] + part[group:]
        summed = part[(FINE - 1) * classes:]
        for s in range(FINE - 2, -1, -1):
            summed = part[s * classes:(s + 1) * classes] + pltpu.roll(summed, ANGLES - STEP, 1)
        keep_ref[:, c * ANGLES:(c + 1) * ANGLES] = summed[:half]
        send_ref[:, c * ANGLES:(c + 1) * ANGLES] = summed[half:].astype(jnp.bfloat16)
    width = CYCLES * ANGLES
    keep_ref[:, width:] = mass[:half]
    send_ref[:, width:] = mass[half:].astype(jnp.bfloat16)


def local(particles, references, inv_noise, assign):
    rows, width = particles.shape
    owned = references.shape[0]
    devices = lax.axis_size("blk")
    bits = devices.bit_length() - 1
    classes = owned * devices

    def swap(x, bit):
        return lax.ppermute(x, "blk", [(i, i ^ bit) for i in range(devices)])

    gathered = references
    for b in range(bits - 1, -1, -1):
        gathered = jnp.concatenate([gathered, swap(gathered, 1 << b)], axis=0)

    half = classes // 2
    wide = width + LANES
    keep, send, log_evidence = pl.pallas_call(
        functools.partial(assign_kernel, bits),
        out_shape=(
            jax.ShapeDtypeStruct((half, wide), jnp.float32),
            jax.ShapeDtypeStruct((half, wide), jnp.bfloat16),
            jax.ShapeDtypeStruct((1, rows), jnp.float32),
        ),
        in_specs=[pl.BlockSpec(memory_space=pltpu.VMEM)] * 4,
        out_specs=[pl.BlockSpec(memory_space=pltpu.VMEM)] * 3,
        scratch_shapes=[pltpu.VMEM((ROT * classes, width), jnp.bfloat16)],
        compiler_params=pltpu.CompilerParams(vmem_limit_bytes=48 * 1024 * 1024),
    )(particles, gathered, inv_noise[None, :], assign.T)

    for b in range(bits):
        total = keep + swap(send, 1 << b).astype(jnp.float32)
        part = total.shape[0] // 2
        if b < bits - 1:
            keep, send = total[:part], total[part:].astype(jnp.bfloat16)
    return total[:, :width], total[:, width], log_evidence[0]


def solution(mesh):
    placed = (
        P(("parts", "blk"), None),
        P(("parts", "blk"), None),
        P(("parts", "blk")),
        P(("parts", "blk"), None),
    )
    return jax.shard_map(
        local,
        mesh=mesh,
        in_specs=placed,
        out_specs=(P(("parts", "blk"), None), P(("parts", "blk")), P(("parts", "blk"))),
        check_vma=False,
    )
```

time: 208 us -> 43.9 us (0.21)
  local copies, waits for them, and re-layouts: 60.8 us -> 4.78 us
  blocking collectives: 54.2 us -> 0 us
  waiting for transfers between devices: 56.6 us -> 15.8 us
  starting transfers between devices: 0.04 us -> 14.9 us
  between operations: 14.9 us -> 0.71 us
  matrix products: 10.3 us -> 0 us
  other arithmetic: 10.5 us -> 2.48 us
  Pallas kernels: 0 us -> 4.79 us
    unnamed x2 -> x0, waiting for transfers between devices: 56.6 us -> none
    unnamed x1 -> x0, blocking collectives: 30 us -> none
    all_gather x1 -> x0, blocking collectives: 24.1 us -> none  [local(): piece = lax.all_gather(references, 'blk', axis=0, tiled=True)]
    transpose x2 -> x0, local copies, waits for them, and re-layouts: 18.5 us -> none  [the longest x1 18.2 us: local(): summed.transpose(0, 1, 3, 2, 4).reshape(local_rows * TOPK, width)]
    reshape x5 -> x0, local copies, waits for them, and re-layouts: 17.3 us -> none  [the longest x1 13.2 us: local(): summed.transpose(0, 1, 3, 2, 4).reshape(local_rows * TOPK, width)]
    ppermute x0 -> x8, waiting for transfers between devices: none -> 15.8 us  [swap(): return lax.ppermute(x, 'blk', [(i, i ^ bit) for i in range(devices)])]
    ppermute x0 -> x8, starting transfers between devices: none -> 14.9 us  [swap(): return lax.ppermute(x, 'blk', [(i, i ^ bit) for i in range(devices)])]
    dot_general x5 -> x0, matrix products: 10.3 us -> none  [the longest x1 4.62 us: local(): jnp.einsum('pjbc,pcm->pjbm', mixing, blocked, precision=lax.Precision.HIG...]
  transfers between devices with their start and end apart: 1 -> 8, of which waited for: 1 -> 8; matrix products, arithmetic and copies ran while one was open for 1% -> 0% of each run, Pallas kernels for 0% -> 0%
where the time goes in v1:
time: 43.9 us; the launch traced here: 43.5 us
  waiting for transfers between devices  15.8 us (36%)
  starting transfers between devices  14.9 us (34%)
  Pallas kernels  4.79 us (11%)
  local copies, waits for them, and re-layouts  4.78 us (11%)
  other arithmetic  2.48 us (6%)
  between operations  0.71 us (2%)
    ppermute x8, waiting for transfers between devices, swap(): return lax.ppermute(x, 'blk', [(i, i ^ bit) for i in range(devices)])  15.8 us
    ppermute x8, starting transfers between devices, swap(): return lax.ppermute(x, 'blk', [(i, i ^ bit) for i in range(devices)])  14.9 us
    pallas_call x1, Pallas kernels, local(): pl.pallas_call(functools.partial(assign_kernel, bits), out_shape=(jax.Sha...  4.79 us
    unnamed x6, local copies, waits for them, and re-layouts  2.6 us
    concatenate x3, other arithmetic, local(): gathered = jnp.concatenate([gathered, swap(gathered, 1 << b)], axis=0)  2.38 us
    slice x2, local copies, waits for them, and re-layouts, local(): return (total[:, :width], total[:, width], log_evidence[0])  1.25 us
  transfers between devices with their start and end apart: 8, of which 8 were waited for; matrix products, arithmetic and copies ran while one was open for 0% of the time, Pallas kernels for 0%

profile of v1, /device:TPU:0, one launch (start us, length us, event | category | flops | bytes accessed | tf_op | source)
XLA Modules:
  0.0 43.5 jit_solution(2160442078149618328)
XLA Ops:
  0.6 4.1 %collective-permute-start = (bf16[2,4608]{1,0:T(2,128)(2,1)}, bf16[2,4608]{1,0:T(2,128)(2,1)S(1)}, u32[]{:S(2)}, u32[]{:S(2)}) collective-permute-start(bf16[2,4608]{1,0:T(2,128)(2,1)} %param.5), channel_id=1, source_target_pairs={{0,8},{1,9},{2,10},{3,11},{4,12},{5,13},{6,14},{7,15},{8,0},{9,1},... | collective-permute-start | bytes 55304 | tf_op jit(solution)/shard_map/ppermute | solution.py:96
  4.7 2.0 %collective-permute-done = bf16[2,4608]{1,0:T(2,128)(2,1)S(1)} collective-permute-done((bf16[2,4608]{1,0:T(2,128)(2,1)}, bf16[2,4608]{1,0:T(2,128)(2,1)S(1)}, u32[]{:S(2)}, u32[]{:S(2)}) %collective-permute-start) | collective-permute-done | bytes 18464 | tf_op jit(solution)/shard_map/ppermute | solution.py:96
  6.7 0.8 %pad_maximum_fusion.2 = bf16[4,4608]{1,0:T(4,128)(2,1)S(1)} fusion(bf16[2,4608]{1,0:T(2,128)(2,1)S(1)} %collective-permute-done, bf16[2,4608]{1,0:T(2,128)(2,1)} %param.5), kind=kLoop, calls=%fused_computation.9 | loop fusion | flops 73728 | bytes 73728 | tf_op jit(solution)/shard_map/concatenate | solution.py:100
  7.5 2.0 %collective-permute-start.1 = (bf16[4,4608]{1,0:T(4,128)(2,1)S(1)}, bf16[4,4608]{1,0:T(4,128)(2,1)S(1)}, u32[]{:S(2)}, u32[]{:S(2)}) collective-permute-start(bf16[4,4608]{1,0:T(4,128)(2,1)S(1)} %pad_maximum_fusion.2), channel_id=1, source_target_pairs={{0,4},{1,5},{2,6},{3,7},{4,0},{5,1},{6,2},{7,3},{8,12},{9,13},{10,... | collective-permute-start | bytes 110600 | tf_op jit(solution)/shard_map/ppermute | solution.py:96
  9.4 2.1 %collective-permute-done.1 = bf16[4,4608]{1,0:T(4,128)(2,1)S(1)} collective-permute-done((bf16[4,4608]{1,0:T(4,128)(2,1)S(1)}, bf16[4,4608]{1,0:T(4,128)(2,1)S(1)}, u32[]{:S(2)}, u32[]{:S(2)}) %collective-permute-start.1) | collective-permute-done | bytes 36896 | tf_op jit(solution)/shard_map/ppermute | solution.py:96
  11.5 0.8 %pad_maximum_fusion.1 = bf16[8,4608]{1,0:T(8,128)(2,1)S(1)} fusion(bf16[4,4608]{1,0:T(4,128)(2,1)S(1)} %collective-permute-done.1, bf16[2,4608]{1,0:T(2,128)(2,1)S(1)} %collective-permute-done, bf16[2,4608]{1,0:T(2,128)(2,1)} %param.5), kind=kLoop, calls=%fused_computation.6 | loop fusion | flops 221184 | bytes 147456 | tf_op jit(solution)/shard_map/concatenate | solution.py:100
  12.3 2.0 %collective-permute-start.2 = (bf16[8,4608]{1,0:T(8,128)(2,1)S(1)}, bf16[8,4608]{1,0:T(8,128)(2,1)S(1)}, u32[]{:S(2)}, u32[]{:S(2)}) collective-permute-start(bf16[8,4608]{1,0:T(8,128)(2,1)S(1)} %pad_maximum_fusion.1), channel_id=1, source_target_pairs={{0,2},{1,3},{2,0},{3,1},{4,6},{5,7},{6,4},{7,5},{8,10},{9,11},{10,... | collective-permute-start | bytes 221192 | tf_op jit(solution)/shard_map/ppermute | solution.py:96
  14.3 2.4 %collective-permute-done.2 = bf16[8,4608]{1,0:T(8,128)(2,1)S(1)} collective-permute-done((bf16[8,4608]{1,0:T(8,128)(2,1)S(1)}, bf16[8,4608]{1,0:T(8,128)(2,1)S(1)}, u32[]{:S(2)}, u32[]{:S(2)}) %collective-permute-start.2) | collective-permute-done | bytes 73760 | tf_op jit(solution)/shard_map/ppermute | solution.py:96
  16.7 0.8 %pad_maximum_fusion = bf16[16,4608]{1,0:T(8,128)(2,1)S(1)} fusion(bf16[8,4608]{1,0:T(8,128)(2,1)S(1)} %collective-permute-done.2, bf16[4,4608]{1,0:T(4,128)(2,1)S(1)} %collective-permute-done.1, bf16[2,4608]{1,0:T(2,128)(2,1)S(1)} %collective-permute-done, bf16[2,4608]{1,0:T(2,128)(2,1)} %param.5), kind=kLoop, calls=%fused_computation.3 | loop fusion | flops 589824 | bytes 294912 | tf_op jit(solution)/shard_map/concatenate | solution.py:100
  17.6 1.4 %collective-permute-done.3 = bf16[16,4608]{1,0:T(8,128)(2,1)S(1)} collective-permute-done((bf16[16,4608]{1,0:T(8,128)(2,1)S(1)}, bf16[16,4608]{1,0:T(8,128)(2,1)S(1)}, u32[]{:S(2)}, u32[]{:S(2)}) %collective-permute-start.3) | collective-permute-done | bytes 147488 | tf_op jit(solution)/shard_map/ppermute | solution.py:96
  18.9 0.9 %concatenate.18.refs_ref = bf16[32,4608]{1,0:T(8,128)(2,1)S(1)} concatenate(bf16[2,4608]{1,0:T(2,128)(2,1)} %param.5, bf16[2,4608]{1,0:T(2,128)(2,1)S(1)} %collective-permute-done, bf16[4,4608]{1,0:T(4,128)(2,1)S(1)} %collective-permute-done.1, bf16[8,4608]{1,0:T(8,128)(2,1)S(1)} %collective-permute-done.2, bf16[16,4608]{1,0:T(8,128)(2,1)S(1)} %collective-permute-done.3), dimensions={0} | concatenate | bytes 589824 | tf_op jit(solution)/shard_map/concatenate | solution.py:100
  19.8 1.3 %copy-done = bf16[128,4608]{1,0:T(8,128)(2,1)S(1)} copy-done((bf16[128,4608]{1,0:T(8,128)(2,1)S(1)}, bf16[128,4608]{1,0:T(8,128)(2,1)}, u32[]{:S(2)}) %copy-start) | copy-done | bytes 1179672
  21.1 0.7 %copy-done.1 = s32[128,2]{0,1:T(2,128)S(1)} copy-done((s32[128,2]{0,1:T(2,128)S(1)}, s32[128,2]{0,1:T(2,128)}, u32[]{:S(2)}) %copy-start.1) | copy-done | bytes 1048
  21.8 0.7 %copy-done.2 = f32[128]{0:T(128)S(1)} copy-done((f32[128]{0:T(128)S(1)}, f32[128]{0:T(128)}, u32[]{:S(2)}) %copy-start.2) | copy-done | bytes 536
  22.4 4.8 %shard_map.67 = (f32[16,4736]{1,0:T(8,128)S(1)}, bf16[16,4736]{1,0:T(8,128)(2,1)S(1)}, f32[1,128]{1,0:T(1,128)}) custom-call(bf16[128,4608]{1,0:T(8,128)(2,1)S(1)} %copy-done, bf16[32,4608]{1,0:T(8,128)(2,1)S(1)} %concatenate.18.refs_ref, f32[1,128]{1,0:T(1,128)S(1)} %bitcast.4, s32[2,128]{1,0:T(2,128)S(1)} %bitcast.3), custom_call_target="tpu_custom_call" | custom-call | tf_op jit(solution)/shard_map/pallas_call | solution.py:104
  27.5 1.2 %collective-permute-done.4 = bf16[16,4736]{1,0:T(8,128)(2,1)S(1)} collective-permute-done((bf16[16,4736]{1,0:T(8,128)(2,1)S(1)}, bf16[16,4736]{1,0:T(8,128)(2,1)S(1)}, u32[]{:S(2)}, u32[]{:S(2)}) %collective-permute-start.4) | collective-permute-done | bytes 151584 | tf_op jit(solution)/shard_map/ppermute | solution.py:96
  28.7 2.0 %collective-permute-start.5 = (bf16[8,4736]{1,0:T(8,128)(2,1)S(1)}, bf16[8,4736]{1,0:T(8,128)(2,1)S(1)}, u32[]{:S(2)}, u32[]{:S(2)}) collective-permute-start(bf16[8,4736]{1,0:T(8,128)(2,1)S(1)} %slice.50), channel_id=1, source_target_pairs={{0,2},{1,3},{2,0},{3,1},{4,6},{5,7},{6,4},{7,5},{8,10},{9,11},{10,... | collective-permute-start | bytes 227336 | tf_op jit(solution)/shard_map/ppermute | solution.py:96
  30.7 2.6 %collective-permute-done.5 = bf16[8,4736]{1,0:T(8,128)(2,1)S(1)} collective-permute-done((bf16[8,4736]{1,0:T(8,128)(2,1)S(1)}, bf16[8,4736]{1,0:T(8,128)(2,1)S(1)}, u32[]{:S(2)}, u32[]{:S(2)}) %collective-permute-start.5) | collective-permute-done | bytes 75808 | tf_op jit(solution)/shard_map/ppermute | solution.py:96
  33.4 1.8 %collective-permute-start.6 = (bf16[4,4736]{1,0:T(4,128)(2,1)S(1)}, bf16[4,4736]{1,0:T(4,128)(2,1)S(1)}, u32[]{:S(2)}, u32[]{:S(2)}) collective-permute-start(bf16[4,4736]{1,0:T(4,128)(2,1)S(1)} %slice.51), channel_id=1, source_target_pairs={{0,4},{1,5},{2,6},{3,7},{4,0},{5,1},{6,2},{7,3},{8,12},{9,13},{10,... | collective-permute-start | bytes 113672 | tf_op jit(solution)/shard_map/ppermute | solution.py:96
  35.2 2.2 %collective-permute-done.6 = bf16[4,4736]{1,0:T(4,128)(2,1)S(1)} collective-permute-done((bf16[4,4736]{1,0:T(4,128)(2,1)S(1)}, bf16[4,4736]{1,0:T(4,128)(2,1)S(1)}, u32[]{:S(2)}, u32[]{:S(2)}) %collective-permute-start.6) | collective-permute-done | bytes 37920 | tf_op jit(solution)/shard_map/ppermute | solution.py:96
  37.5 2.8 %collective-permute-start.7 = (bf16[2,4736]{1,0:T(2,128)(2,1)S(1)}, bf16[2,4736]{1,0:T(2,128)(2,1)S(1)}, u32[]{:S(2)}, u32[]{:S(2)}) collective-permute-start(bf16[2,4736]{1,0:T(2,128)(2,1)S(1)} %slice.52), channel_id=1, source_target_pairs={{0,8},{1,9},{2,10},{3,11},{4,12},{5,13},{6,14},{7,15},{8,0},{9,1},... | collective-permute-start | bytes 56840 | tf_op jit(solution)/shard_map/ppermute | solution.py:96
  40.3 1.9 %collective-permute-done.7 = bf16[2,4736]{1,0:T(2,128)(2,1)S(1)} collective-permute-done((bf16[2,4736]{1,0:T(2,128)(2,1)S(1)}, bf16[2,4736]{1,0:T(2,128)(2,1)S(1)}, u32[]{:S(2)}, u32[]{:S(2)}) %collective-permute-start.7) | collective-permute-done | bytes 18976 | tf_op jit(solution)/shard_map/ppermute | solution.py:96
  42.3 0.6 %slice_reduce_fusion = f32[2]{0:T(128)} fusion(f32[2,4736]{1,0:T(2,128)S(1)} %slice_add_fusion.2), kind=kLoop, calls=%fused_computation.10 | loop fusion | bytes 16 | tf_op jit(solution)/shard_map/slice | solution.py:122
  42.9 0.6 %slice.41 = f32[2,4608]{1,0:T(2,128)} slice(f32[2,4736]{1,0:T(2,128)S(1)} %slice_add_fusion.2), slice={[0:2], [0:4608]} | slice | bytes 73728 | tf_op jit(solution)/shard_map/slice | solution.py:122
  (12 shorter events, 0.5 us)
Async XLA Ops:
  0.6 6.1 %collective-permute-start = (bf16[2,4608]{1,0:T(2,128)(2,1)}, bf16[2,4608]{1,0:T(2,128)(2,1)S(1)}, u32[]{:S(2)}, u32[]{:S(2)}) collective-permute-start(bf16[2,4608]{1,0:T(2,128)(2,1)} %param.5), channel_id=1, source_target_pairs={{0,8},{1,9},{2,10},{3,11},{4,12},{5,13},{6,14},{7,15},{8,0},{9,1},... | collective-permute-start | bytes 55304 | tf_op jit(solution)/shard_map/ppermute | solution.py:96
  7.5 4.0 %collective-permute-start.1 = (bf16[4,4608]{1,0:T(4,128)(2,1)S(1)}, bf16[4,4608]{1,0:T(4,128)(2,1)S(1)}, u32[]{:S(2)}, u32[]{:S(2)}) collective-permute-start(bf16[4,4608]{1,0:T(4,128)(2,1)S(1)} %pad_maximum_fusion.2), channel_id=1, source_target_pairs={{0,4},{1,5},{2,6},{3,7},{4,0},{5,1},{6,2},{7,3},{8,12},{9,13},{10,... | collective-permute-start | bytes 110600 | tf_op jit(solution)/shard_map/ppermute | solution.py:96
  12.3 4.4 %collective-permute-start.2 = (bf16[8,4608]{1,0:T(8,128)(2,1)S(1)}, bf16[8,4608]{1,0:T(8,128)(2,1)S(1)}, u32[]{:S(2)}, u32[]{:S(2)}) collective-permute-start(bf16[8,4608]{1,0:T(8,128)(2,1)S(1)} %pad_maximum_fusion.1), channel_id=1, source_target_pairs={{0,2},{1,3},{2,0},{3,1},{4,6},{5,7},{6,4},{7,5},{8,10},{9,11},{10,... | collective-permute-start | bytes 221192 | tf_op jit(solution)/shard_map/ppermute | solution.py:96
  17.5 1.4 %collective-permute-start.3 = (bf16[16,4608]{1,0:T(8,128)(2,1)S(1)}, bf16[16,4608]{1,0:T(8,128)(2,1)S(1)}, u32[]{:S(2)}, u32[]{:S(2)}) collective-permute-start(bf16[16,4608]{1,0:T(8,128)(2,1)S(1)} %pad_maximum_fusion), channel_id=1, source_target_pairs={{0,1},{1,0},{2,3},{3,2},{4,5},{5,4},{6,7},{7,6},{8,9},{9,8},{10,11... | collective-permute-start | bytes 442376 | tf_op jit(solution)/shard_map/ppermute | solution.py:96
  19.8 1.3 %copy-start = (bf16[128,4608]{1,0:T(8,128)(2,1)S(1)}, bf16[128,4608]{1,0:T(8,128)(2,1)}, u32[]{:S(2)}) copy-start(bf16[128,4608]{1,0:T(8,128)(2,1)} %p_ref.1) | copy-start | bytes 3538948
  21.1 0.7 %copy-start.1 = (s32[128,2]{0,1:T(2,128)S(1)}, s32[128,2]{0,1:T(2,128)}, u32[]{:S(2)}) copy-start(s32[128,2]{0,1:T(2,128)} %param.7) | copy-start | bytes 3076
  21.8 0.7 %copy-start.2 = (f32[128]{0:T(128)S(1)}, f32[128]{0:T(128)}, u32[]{:S(2)}) copy-start(f32[128]{0:T(128)} %param.6) | copy-start | bytes 1540
  27.2 1.4 %collective-permute-start.4 = (bf16[16,4736]{1,0:T(8,128)(2,1)S(1)}, bf16[16,4736]{1,0:T(8,128)(2,1)S(1)}, u32[]{:S(2)}, u32[]{:S(2)}) collective-permute-start(bf16[16,4736]{1,0:T(8,128)(2,1)S(1)} %get-tuple-element.7), channel_id=1, source_target_pairs={{0,1},{1,0},{2,3},{3,2},{4,5},{5,4},{6,7},{7,6},{8,9},{9,8},{10,11... | collective-permute-start | bytes 454664 | tf_op jit(solution)/shard_map/ppermute | solution.py:96
  28.7 4.6 %collective-permute-start.5 = (bf16[8,4736]{1,0:T(8,128)(2,1)S(1)}, bf16[8,4736]{1,0:T(8,128)(2,1)S(1)}, u32[]{:S(2)}, u32[]{:S(2)}) collective-permute-start(bf16[8,4736]{1,0:T(8,128)(2,1)S(1)} %slice.50), channel_id=1, source_target_pairs={{0,2},{1,3},{2,0},{3,1},{4,6},{5,7},{6,4},{7,5},{8,10},{9,11},{10,... | collective-permute-start | bytes 227336 | tf_op jit(solution)/shard_map/ppermute | solution.py:96
  33.4 4.0 %collective-permute-start.6 = (bf16[4,4736]{1,0:T(4,128)(2,1)S(1)}, bf16[4,4736]{1,0:T(4,128)(2,1)S(1)}, u32[]{:S(2)}, u32[]{:S(2)}) collective-permute-start(bf16[4,4736]{1,0:T(4,128)(2,1)S(1)} %slice.51), channel_id=1, source_target_pairs={{0,4},{1,5},{2,6},{3,7},{4,0},{5,1},{6,2},{7,3},{8,12},{9,13},{10,... | collective-permute-start | bytes 113672 | tf_op jit(solution)/shard_map/ppermute | solution.py:96
  37.5 4.7 %collective-permute-start.7 = (bf16[2,4736]{1,0:T(2,128)(2,1)S(1)}, bf16[2,4736]{1,0:T(2,128)(2,1)S(1)}, u32[]{:S(2)}, u32[]{:S(2)}) collective-permute-start(bf16[2,4736]{1,0:T(2,128)(2,1)S(1)} %slice.52), channel_id=1, source_target_pairs={{0,8},{1,9},{2,10},{3,11},{4,12},{5,13},{6,14},{7,15},{8,0},{9,1},... | collective-permute-start | bytes 56840 | tf_op jit(solution)/shard_map/ppermute | solution.py:96

commit v2 on v1

v2 whole, which is shorter than its diff:
```python
import functools

import jax
import jax.numpy as jnp
from jax import lax
from jax.experimental import pallas as pl
from jax.experimental.pallas import tpu as pltpu
from jax.sharding import PartitionSpec as P

ROT = 12
CYCLES = 12
ANGLES = 384
WIDTH = CYCLES * ANGLES
LANES = 128
STEP = ANGLES // ROT
FINE = LANES // STEP
COARSE = ROT // FINE
VMEM = pl.BlockSpec(memory_space=pltpu.VMEM)
HBM = pl.BlockSpec(memory_space=pltpu.HBM)
PARAMS = pltpu.CompilerParams(vmem_limit_bytes=40 * 1024 * 1024)


def stage_kernel(refs_ref, out_ref):
    out_ref[...] = refs_ref[...]


def score(refs_ref, p_ref, noise, turned_ref):
    classes = refs_ref.shape[0]
    group = FINE * classes
    energy = jnp.zeros((classes, LANES), jnp.float32)
    for c in range(CYCLES):
        cube = refs_ref[:, c * ANGLES:(c + 1) * ANGLES].astype(jnp.float32)
        for v in range(COARSE):
            piece = cube[:, v * LANES:(v + 1) * LANES]
            energy = energy + piece * piece
        moved = [cube] + [pltpu.roll(cube, s * STEP, 1) for s in range(1, FINE)]
        moved = jnp.concatenate(moved, axis=0).astype(jnp.bfloat16)
        for q in range(COARSE):
            for v in range(COARSE):
                at = c * ANGLES + (v + q) % COARSE * LANES
                turned_ref[q * group:(q + 1) * group, at:at + LANES] = moved[:, v * LANES:(v + 1) * LANES]
    energy = jnp.sum(energy, axis=1, keepdims=True)
    dots = lax.dot_general(
        turned_ref[...], p_ref[...], (((1,), (1,)), ((), ())), preferred_element_type=jnp.float32
    )
    dots = dots.reshape(ROT, classes, dots.shape[1])
    return noise[None] * (dots - 0.5 * energy[None])


def early_kernel(p_own, p_far, noise_own, noise_far, name_own, name_far, refs_ref,
                 p_ref, noise_ref, name_ref, logits_ref, turned_ref, sems):
    rows = p_own.shape[0]
    copies = [
        pltpu.make_async_copy(p_own, p_ref.at[0:rows], sems.at[0]),
        pltpu.make_async_copy(p_far, p_ref.at[rows:2 * rows], sems.at[1]),
        pltpu.make_async_copy(noise_own, noise_ref.at[:, 0:rows], sems.at[2]),
        pltpu.make_async_copy(noise_far, noise_ref.at[:, rows:2 * rows], sems.at[3]),
        pltpu.make_async_copy(name_own, name_ref.at[:, 0:rows], sems.at[4]),
        pltpu.make_async_copy(name_far, name_ref.at[:, rows:2 * rows], sems.at[5]),
    ]
    for copy in copies:
        copy.start()
    for copy in copies:
        copy.wait()
    logits_ref[...] = score(refs_ref, p_ref, noise_ref[...], turned_ref)


def late_kernel(refs_ref, p_ref, noise_ref, early_ref, logits_ref, part_ref, turned_ref):
    late = score(refs_ref, p_ref, noise_ref[...], turned_ref)
    logits_ref[...] = late
    early = early_ref[...]
    top = jnp.maximum(jnp.max(late, axis=0), jnp.max(early, axis=0))
    top = jnp.max(top, axis=0, keepdims=True)
    total = jnp.sum(jnp.exp(late - top[None]), axis=0) + jnp.sum(jnp.exp(early - top[None]), axis=0)
    part_ref[...] = top + jnp.log(jnp.sum(total, axis=0, keepdims=True))


def back_kernel(bits, owned, first, logits_ref, near_ref, far_ref, name_ref, p_ref, sums_ref, log_ref=None):
    classes, rows = logits_ref.shape[1:]
    me = lax.axis_index("blk")
    near, far = near_ref[...], far_ref[...]
    top = jnp.maximum(near, far)
    log_evidence = top + jnp.log(jnp.exp(near - top) + jnp.exp(far - top))
    if log_ref is not None:
        log_ref[...] = log_evidence[:, :log_ref.shape[1]]

    row = lax.broadcasted_iota(jnp.int32, (classes, rows), 0) + first
    place = row // owned
    mixed = jnp.zeros_like(place)
    for i in range(bits - 1):
        mixed = mixed + (((place >> i) & 1) << (bits - 1 - i))
    ident = (mixed ^ me) * owned + row % owned
    named = (ident == name_ref[0:1, :]) | (ident == name_ref[1:2, :])
    post = jnp.where(named[None], jnp.exp(logits_ref[...] - log_evidence[None]), 0.0)
    weights = jnp.sum(post, axis=0).astype(jnp.bfloat16).astype(jnp.float32)
    mass = jnp.broadcast_to(jnp.sum(weights, axis=1, keepdims=True), (classes, LANES))
    sums_ref[:, WIDTH:] = mass.astype(sums_ref.dtype)

    count = ROT * classes
    post = post.reshape(count, rows)
    high = post.astype(jnp.bfloat16)
    low = (post - high.astype(jnp.float32)).astype(jnp.bfloat16)
    both = jnp.concatenate([high, low], axis=0)
    group = FINE * classes
    for c in range(0, CYCLES, 2):
        part = jnp.dot(both, p_ref[:, c * ANGLES:(c + 2) * ANGLES], preferred_element_type=jnp.float32)
        part = part[:count] + part[count:]
        for d in range(2):
            blocks = []
            for v in range(COARSE):
                block = None
                for q in range(COARSE):
                    at = d * ANGLES + (v + q) % COARSE * LANES
                    piece = part[q * group:(q + 1) * group, at:at + LANES]
                    block = piece if block is None else block + piece
                blocks.append(block)
            turned = jnp.concatenate(blocks, axis=1)
            summed = turned[(FINE - 1) * classes:]
            for s in range(FINE - 2, -1, -1):
                summed = turned[s * classes:(s + 1) * classes] + pltpu.roll(summed, ANGLES - STEP, 1)
            sums_ref[:, (c + d) * ANGLES:(c + d + 1) * ANGLES] = summed.astype(sums_ref.dtype)


def last_kernel(keep_ref, got_ref, sums_ref, mass_ref):
    owned = sums_ref.shape[0]
    total = keep_ref[0:owned, :] + got_ref[...].astype(jnp.float32)
    sums_ref[...] = total[:, :WIDTH]
    for i in range(owned):
        mass_ref[i] = total[i, WIDTH]


def local(particles, references, inv_noise, assign):
    rows, width = particles.shape
    owned = references.shape[0]
    devices = lax.axis_size("blk")
    bits = devices.bit_length() - 1
    half = owned * devices // 4
    both = 2 * rows
    wide = width + LANES
    f32, bf16 = jnp.float32, jnp.bfloat16

    def swap(x, bit):
        return lax.ppermute(x, "blk", [(i, i ^ bit) for i in range(devices)])

    noise, names = inv_noise[None, :], assign.T
    p_far, noise_far, names_far = swap(particles, 1), swap(noise, 1), swap(names, 1)

    own = pl.pallas_call(
        stage_kernel, out_shape=jax.ShapeDtypeStruct((owned, width), bf16),
        in_specs=[VMEM], out_specs=VMEM, compiler_params=PARAMS, name="stage",
    )(references)
    gathered = references
    for b in range(bits - 1, 0, -1):
        got = swap(gathered, 1 << b)
        if b == bits - 1:
            gathered = own
        if b > 1:
            gathered = jnp.concatenate([gathered, got], axis=0)

    turned = pltpu.VMEM((ROT * half, width), bf16)
    score_cost = pl.CostEstimate(
        flops=2 * ROT * half * both * width, bytes_accessed=4 * both * width, transcendentals=0)
    p_all, noise_all, names_all, early = pl.pallas_call(
        early_kernel,
        out_shape=(
            jax.ShapeDtypeStruct((both, width), bf16),
            jax.ShapeDtypeStruct((1, both), f32),
            jax.ShapeDtypeStruct((2, both), jnp.int32),
            jax.ShapeDtypeStruct((ROT, half, both), f32),
        ),
        in_specs=[HBM] * 6 + [VMEM],
        out_specs=[VMEM] * 4,
        scratch_shapes=[turned, pltpu.SemaphoreType.DMA((6,))],
        compiler_params=PARAMS, cost_estimate=score_cost, name="early",
    )(particles, p_far, noise, noise_far, names, names_far, gathered)
    late, near = pl.pallas_call(
        late_kernel,
        out_shape=(jax.ShapeDtypeStruct((ROT, half, both), f32), jax.ShapeDtypeStruct((1, both), f32)),
        in_specs=[VMEM] * 4,
        out_specs=[VMEM] * 2,
        scratch_shapes=[turned],
        compiler_params=PARAMS, cost_estimate=score_cost, name="late",
    )(got, p_all, noise_all, early)
    far = swap(near, 1)
    far = jnp.concatenate([far[:, rows:], far[:, :rows]], axis=1)

    send = pl.pallas_call(
        functools.partial(back_kernel, bits, owned, half),
        out_shape=jax.ShapeDtypeStruct((half, wide), bf16),
        in_specs=[VMEM] * 5,
        out_specs=VMEM,
        compiler_params=PARAMS, cost_estimate=score_cost, name="back_send",
    )(late, near, far, names_all, p_all)
    keep, log_evidence = pl.pallas_call(
        functools.partial(back_kernel, bits, owned, 0),
        out_shape=(jax.ShapeDtypeStruct((half, wide), f32), jax.ShapeDtypeStruct((1, rows), f32)),
        in_specs=[VMEM] * 5,
        out_specs=[VMEM] * 2,
        compiler_params=PARAMS, cost_estimate=score_cost, name="back_keep",
    )(early, near, far, names_all, p_all)

    for b in range(1, bits):
        got = swap(send, 1 << b)
        if b < bits - 1:
            total = keep + got.astype(f32)
            part = total.shape[0] // 2
            keep, send = total[:part], total[part:].astype(bf16)
    sums, mass = pl.pallas_call(
        last_kernel,
        out_shape=(jax.ShapeDtypeStruct((owned, width), f32), jax.ShapeDtypeStruct((owned,), f32)),
        in_specs=[VMEM] * 2,
        out_specs=[VMEM, pl.BlockSpec(memory_space=pltpu.SMEM)],
        compiler_params=PARAMS, name="last",
    )(keep, got)
    return sums, mass, log_evidence[0]


def solution(mesh):
    placed = (
        P(("parts", "blk"), None),
        P(("parts", "blk"), None),
        P(("parts", "blk")),
        P(("parts", "blk"), None),
    )
    return jax.shard_map(
        local,
        mesh=mesh,
        in_specs=placed,
        out_specs=(P(("parts", "blk"), None), P(("parts", "blk")), P(("parts", "blk"))),
        check_vma=False,
    )
```

time: 43.9 us -> 35.6 us (0.81)
  waiting for transfers between devices: 15.8 us -> 13.2 us
  other arithmetic: 2.48 us -> 0.16 us
  starting transfers between devices: 14.9 us -> 13.2 us
  local copies, waits for them, and re-layouts: 4.78 us -> 3.41 us
    ppermute x8 -> x10, waiting for transfers between devices: 15.8 us -> 13.2 us  [swap(): return lax.ppermute(x, 'blk', [(i, i ^ bit) for i in range(devices)])]
    concatenate x3, other arithmetic: 2.38 us -> 0.12 us  [the longest x2 0.11 us: local(): gathered = jnp.concatenate([gathered, got], axis=0)]
    ppermute x8 -> x10, starting transfers between devices: 14.9 us -> 13.2 us  [swap(): return lax.ppermute(x, 'blk', [(i, i ^ bit) for i in range(devices)])]
    slice x5 -> x4, local copies, waits for them, and re-layouts: 1.3 us -> 0.06 us  [the longest x3 0.06 us: local(): keep, send = (total[:part], total[part:].astype(bf16))]
    concatenate x1 -> x0, local copies, waits for them, and re-layouts: 0.88 us -> none  [local(): gathered = jnp.concatenate([gathered, swap(gathered, 1 << b)], axis=0)]
    unnamed x6 -> x8, local copies, waits for them, and re-layouts: 2.6 us -> 3.36 us
    pallas_call x1 -> x6, Pallas kernels: 4.79 us -> 4.67 us  [the longest x1 1.41 us: local(): pl.pallas_call(early_kernel, out_shape=(jax.ShapeDtypeStruct((both, width...]
  transfers between devices with their start and end apart: 8 -> 10, of which waited for: 8 -> 7; matrix products, arithmetic and copies ran while one was open for 0% -> 0% of each run, Pallas kernels for 0% -> 6%
where the time goes in v2:
time: 35.6 us; the launch traced here: 35.4 us
  starting transfers between devices  13.2 us (37%)
  waiting for transfers between devices  13.2 us (37%)
  Pallas kernels  4.67 us (13%)
  local copies, waits for them, and re-layouts  3.41 us (10%)
  between operations  0.69 us (2%)
    ppermute x10, starting transfers between devices, swap(): return lax.ppermute(x, 'blk', [(i, i ^ bit) for i in range(devices)])  13.2 us
    ppermute x10, waiting for transfers between devices, swap(): return lax.ppermute(x, 'blk', [(i, i ^ bit) for i in range(devices)])  13.2 us
    unnamed x8, local copies, waits for them, and re-layouts  3.36 us
    pallas_call x1, Pallas kernels, local(): pl.pallas_call(early_kernel, out_shape=(jax.ShapeDtypeStruct((both, width...  1.41 us
    pallas_call x1, Pallas kernels, local(): pl.pallas_call(late_kernel, out_shape=(jax.ShapeDtypeStruct((ROT, half, b...  0.92 us
    pallas_call x1, Pallas kernels, local(): pl.pallas_call(functools.partial(back_kernel, bits, owned, 0), out_shape=...  0.86 us
    pallas_call x1, Pallas kernels, local(): pl.pallas_call(functools.partial(back_kernel, bits, owned, half), out_sha...  0.85 us
  transfers between devices with their start and end apart: 10, of which 7 were waited for; matrix products, arithmetic and copies ran while one was open for 0% of the time, Pallas kernels for 6%

profile of v2, /device:TPU:0, one launch (start us, length us, event | category | flops | bytes accessed | tf_op | source)
XLA Modules:
  0.0 35.4 jit_solution(4801493847353537499)
XLA Ops:
  0.6 4.1 %collective-permute-start.3 = (bf16[2,4608]{1,0:T(2,128)(2,1)}, bf16[2,4608]{1,0:T(2,128)(2,1)S(1)}, u32[]{:S(2)}, u32[]{:S(2)}) collective-permute-start(bf16[2,4608]{1,0:T(2,128)(2,1)} %refs_ref.1), channel_id=1, source_target_pairs={{0,8},{1,9},{2,10},{3,11},{4,12},{5,13},{6,14},{7,15},{8,0},{9,1},... | collective-permute-start | bytes 55304 | tf_op jit(solution)/shard_map/ppermute | solution.py:143
  4.7 0.8 %copy-done.1 = bf16[2,4608]{1,0:T(2,128)(2,1)S(1)} copy-done((bf16[2,4608]{1,0:T(2,128)(2,1)S(1)}, bf16[2,4608]{1,0:T(2,128)(2,1)}, u32[]{:S(2)}) %copy-start.1) | copy-done | bytes 18456
  5.5 1.2 %collective-permute-done.3 = bf16[2,4608]{1,0:T(2,128)(2,1)S(1)} collective-permute-done((bf16[2,4608]{1,0:T(2,128)(2,1)}, bf16[2,4608]{1,0:T(2,128)(2,1)S(1)}, u32[]{:S(2)}, u32[]{:S(2)}) %collective-permute-start.3) | collective-permute-done | bytes 18464 | tf_op jit(solution)/shard_map/ppermute | solution.py:143
  6.7 2.0 %collective-permute-start.4 = (bf16[4,4608]{1,0:T(4,128)(2,1)S(1)}, bf16[4,4608]{1,0:T(4,128)(2,1)S(1)}, u32[]{:S(2)}, u32[]{:S(2)}) collective-permute-start(bf16[4,4608]{1,0:T(4,128)(2,1)S(1)} %pad_maximum_fusion.1), channel_id=1, source_target_pairs={{0,4},{1,5},{2,6},{3,7},{4,0},{5,1},{6,2},{7,3},{8,12},{9,13},{10,... | collective-permute-start | bytes 110600 | tf_op jit(solution)/shard_map/ppermute | solution.py:143
  8.7 2.1 %collective-permute-done.4 = bf16[4,4608]{1,0:T(4,128)(2,1)S(1)} collective-permute-done((bf16[4,4608]{1,0:T(4,128)(2,1)S(1)}, bf16[4,4608]{1,0:T(4,128)(2,1)S(1)}, u32[]{:S(2)}, u32[]{:S(2)}) %collective-permute-start.4) | collective-permute-done | bytes 36896 | tf_op jit(solution)/shard_map/ppermute | solution.py:143
  10.8 2.0 %collective-permute-start.5 = (bf16[8,4608]{1,0:T(8,128)(2,1)S(1)}, bf16[8,4608]{1,0:T(8,128)(2,1)S(1)}, u32[]{:S(2)}, u32[]{:S(2)}) collective-permute-start(bf16[8,4608]{1,0:T(8,128)(2,1)S(1)} %pad_maximum_fusion.refs_ref), channel_id=1, source_target_pairs={{0,2},{1,3},{2,0},{3,1},{4,6},{5,7},{6,4},{7,5},{8,10},{9,11},{10,... | collective-permute-start | bytes 221192 | tf_op jit(solution)/shard_map/ppermute | solution.py:143
  12.8 0.5 %collective-permute-start.1 = (f32[1,128]{1,0:T(1,128)}, f32[1,128]{1,0:T(1,128)S(1)}, u32[]{:S(2)}, u32[]{:S(2)}) collective-permute-start(f32[1,128]{1,0:T(1,128)} %bitcast.5), channel_id=1, source_target_pairs={{0,1},{1,0},{2,3},{3,2},{4,5},{5,4},{6,7},{7,6},{8,9},{9,8},{10,11... | collective-permute-start | bytes 1544 | tf_op jit(solution)/shard_map/ppermute | solution.py:143
  13.3 1.0 %collective-permute-done.1.noise_far = f32[1,128]{1,0:T(1,128)S(1)} collective-permute-done((f32[1,128]{1,0:T(1,128)}, f32[1,128]{1,0:T(1,128)S(1)}, u32[]{:S(2)}, u32[]{:S(2)}) %collective-permute-start.1) | collective-permute-done | bytes 544 | tf_op jit(solution)/shard_map/ppermute | solution.py:143
  14.3 1.3 %copy-done = bf16[128,4608]{1,0:T(8,128)(2,1)S(1)} copy-done((bf16[128,4608]{1,0:T(8,128)(2,1)S(1)}, bf16[128,4608]{1,0:T(8,128)(2,1)}, u32[]{:S(2)}) %copy-start) | copy-done | bytes 1179672
  15.6 0.7 %copy-done.2 = s32[128,2]{0,1:T(2,128)S(1)} copy-done((s32[128,2]{0,1:T(2,128)S(1)}, s32[128,2]{0,1:T(2,128)}, u32[]{:S(2)}) %copy-start.2) | copy-done | bytes 1048
  16.2 0.7 %copy-done.3 = f32[128]{0:T(128)S(1)} copy-done((f32[128]{0:T(128)S(1)}, f32[128]{0:T(128)}, u32[]{:S(2)}) %copy-start.3) | copy-done | bytes 536
  16.9 1.4 %early.1 = (bf16[256,4608]{1,0:T(8,128)(2,1)S(1)}, f32[1,256]{1,0:T(1,128)S(1)}, s32[2,256]{1,0:T(2,128)S(1)}, f32[12,8,256]{2,1,0:T(8,128)S(1)}) custom-call(bf16[128,4608]{1,0:T(8,128)(2,1)S(1)} %copy-done, bf16[128,4608]{1,0:T(8,128)(2,1)S(1)} %collective-permute-done.p_far, f32[1,128]{1,0:T(1,128)S(1)} %bitcast.6, ...), custom_call_target="tpu_custom_call" | custom-call | flops 226492416 | bytes 4718592 | tf_op jit(solution)/shard_map/early/pallas_call | solution.py:163
  18.3 0.9 %late.1 = (f32[12,8,256]{2,1,0:T(8,128)S(1)}, f32[1,256]{1,0:T(1,128)S(1)}) custom-call(bf16[8,4608]{1,0:T(8,128)(2,1)S(1)} %collective-permute-done.5.refs_ref, bf16[256,4608]{1,0:T(8,128)(2,1)S(1)} %get-tuple-element.14.p_ref, f32[1,256]{1,0:T(1,128)S(1)} %get-tuple-element.15.noise_ref, f32[12,8,256]{2,1,0:T(8,128)S(1)} %get-tuple-element.13.early_ref.logits_ref), custom_call_target="tpu_custom_call" | custom-call | flops 226492416 | bytes 4718592 | tf_op jit(solution)/shard_map/late/pallas_call | solution.py:176
  19.2 0.4 %collective-permute-start.6 = (f32[1,256]{1,0:T(1,128)S(1)}, f32[1,256]{1,0:T(1,128)S(1)}, u32[]{:S(2)}, u32[]{:S(2)}) collective-permute-start(f32[1,256]{1,0:T(1,128)S(1)} %get-tuple-element.16.near_ref), channel_id=1, source_target_pairs={{0,1},{1,0},{2,3},{3,2},{4,5},{5,4},{6,7},{7,6},{8,9},{9,8},{10,11... | collective-permute-start | bytes 3080 | tf_op jit(solution)/shard_map/ppermute | solution.py:143
  19.6 0.8 %collective-permute-done.6 = f32[1,256]{1,0:T(1,128)S(1)} collective-permute-done((f32[1,256]{1,0:T(1,128)S(1)}, f32[1,256]{1,0:T(1,128)S(1)}, u32[]{:S(2)}, u32[]{:S(2)}) %collective-permute-start.6) | collective-permute-done | bytes 1056 | tf_op jit(solution)/shard_map/ppermute | solution.py:143
  20.5 0.8 %back_send.1 = bf16[8,4736]{1,0:T(8,128)(2,1)S(1)} custom-call(f32[12,8,256]{2,1,0:T(8,128)S(1)} %get-tuple-element.19.logits_ref, f32[1,256]{1,0:T(1,128)S(1)} %get-tuple-element.16.near_ref, f32[1,256]{1,0:T(1,128)S(1)} %pad_maximum_fusion.2.far_ref, s32[2,256]{1,0:T(2,128)S(1)} %get-tuple-element.17.name_ref, bf16[256,4608]{1,0:T(8,128)(2,1)S(1)} %get-tuple-element.14.p_ref), custom_call_target="tpu_custom_call" | custom-call | flops 226492416 | bytes 4718592 | tf_op jit(solution)/shard_map/back_send/pallas_call | solution.py:187
  21.3 0.1 collective-permute-start.7
  21.4 0.9 %back_keep.1 = (f32[8,4736]{1,0:T(8,128)S(1)}, f32[1,128]{1,0:T(1,128)}) custom-call(f32[12,8,256]{2,1,0:T(8,128)S(1)} %get-tuple-element.13.early_ref.logits_ref, f32[1,256]{1,0:T(1,128)S(1)} %get-tuple-element.16.near_ref, f32[1,256]{1,0:T(1,128)S(1)} %pad_maximum_fusion.2.far_ref, s32[2,256]{1,0:T(2,128)S(1)} %get-tuple-element.17.name_ref, ...), custom_call_target="tpu_custom_call" | custom-call | flops 226492416 | bytes 4718592 | tf_op jit(solution)/shard_map/back_keep/pallas_call | solution.py:194
  22.3 3.6 %collective-permute-done.7 = bf16[8,4736]{1,0:T(8,128)(2,1)S(1)} collective-permute-done((bf16[8,4736]{1,0:T(8,128)(2,1)S(1)}, bf16[8,4736]{1,0:T(8,128)(2,1)S(1)}, u32[]{:S(2)}, u32[]{:S(2)}) %collective-permute-start.7) | collective-permute-done | bytes 75808 | tf_op jit(solution)/shard_map/ppermute | solution.py:143
  25.9 1.6 %collective-permute-start.8 = (bf16[4,4736]{1,0:T(4,128)(2,1)S(1)}, bf16[4,4736]{1,0:T(4,128)(2,1)S(1)}, u32[]{:S(2)}, u32[]{:S(2)}) collective-permute-start(bf16[4,4736]{1,0:T(4,128)(2,1)S(1)} %slice.35), channel_id=1, source_target_pairs={{0,4},{1,5},{2,6},{3,7},{4,0},{5,1},{6,2},{7,3},{8,12},{9,13},{10,... | collective-permute-start | bytes 113672 | tf_op jit(solution)/shard_map/ppermute | solution.py:143
  27.5 2.5 %collective-permute-done.8 = bf16[4,4736]{1,0:T(4,128)(2,1)S(1)} collective-permute-done((bf16[4,4736]{1,0:T(4,128)(2,1)S(1)}, bf16[4,4736]{1,0:T(4,128)(2,1)S(1)}, u32[]{:S(2)}, u32[]{:S(2)}) %collective-permute-start.8) | collective-permute-done | bytes 37920 | tf_op jit(solution)/shard_map/ppermute | solution.py:143
  30.0 2.6 %collective-permute-start.9 = (bf16[2,4736]{1,0:T(2,128)(2,1)S(1)}, bf16[2,4736]{1,0:T(2,128)(2,1)S(1)}, u32[]{:S(2)}, u32[]{:S(2)}) collective-permute-start(bf16[2,4736]{1,0:T(2,128)(2,1)S(1)} %slice.36), channel_id=1, source_target_pairs={{0,8},{1,9},{2,10},{3,11},{4,12},{5,13},{6,14},{7,15},{8,0},{9,1},... | collective-permute-start | bytes 56840 | tf_op jit(solution)/shard_map/ppermute | solution.py:143
  32.6 2.1 %collective-permute-done.9.got_ref = bf16[2,4736]{1,0:T(2,128)(2,1)S(1)} collective-permute-done((bf16[2,4736]{1,0:T(2,128)(2,1)S(1)}, bf16[2,4736]{1,0:T(2,128)(2,1)S(1)}, u32[]{:S(2)}, u32[]{:S(2)}) %collective-permute-start.9) | collective-permute-done | bytes 18976 | tf_op jit(solution)/shard_map/ppermute | solution.py:143
  34.7 0.6 %last.1 = (f32[2,4608]{1,0:T(2,128)}, f32[2]{0:T(128)}) custom-call(f32[2,4736]{1,0:T(2,128)S(1)} %slice.30.keep_ref, bf16[2,4736]{1,0:T(2,128)(2,1)S(1)} %collective-permute-done.9.got_ref), custom_call_target="tpu_custom_call" | custom-call | tf_op jit(solution)/shard_map/last/pallas_call | solution.py:208
  (19 shorter events, 0.2 us)
Async XLA Ops:
  0.6 6.1 %collective-permute-start.3 = (bf16[2,4608]{1,0:T(2,128)(2,1)}, bf16[2,4608]{1,0:T(2,128)(2,1)S(1)}, u32[]{:S(2)}, u32[]{:S(2)}) collective-permute-start(bf16[2,4608]{1,0:T(2,128)(2,1)} %refs_ref.1), channel_id=1, source_target_pairs={{0,8},{1,9},{2,10},{3,11},{4,12},{5,13},{6,14},{7,15},{8,0},{9,1},... | collective-permute-start | bytes 55304 | tf_op jit(solution)/shard_map/ppermute | solution.py:143
  4.7 9.6 %collective-permute-start = (bf16[128,4608]{1,0:T(8,128)(2,1)}, bf16[128,4608]{1,0:T(8,128)(2,1)S(1)}, u32[]{:S(2)}, u32[]{:S(2)}) collective-permute-start(bf16[128,4608]{1,0:T(8,128)(2,1)} %p_own.1), channel_id=1, source_target_pairs={{0,1},{1,0},{2,3},{3,2},{4,5},{5,4},{6,7},{7,6},{8,9},{9,8},{10,11... | collective-permute-start | bytes 3538952 | tf_op jit(solution)/shard_map/ppermute | solution.py:143
  4.7 0.8 %copy-start.1 = (bf16[2,4608]{1,0:T(2,128)(2,1)S(1)}, bf16[2,4608]{1,0:T(2,128)(2,1)}, u32[]{:S(2)}) copy-start(bf16[2,4608]{1,0:T(2,128)(2,1)} %refs_ref.1) | copy-start | bytes 55300
  6.7 4.0 %collective-permute-start.4 = (bf16[4,4608]{1,0:T(4,128)(2,1)S(1)}, bf16[4,4608]{1,0:T(4,128)(2,1)S(1)}, u32[]{:S(2)}, u32[]{:S(2)}) collective-permute-start(bf16[4,4608]{1,0:T(4,128)(2,1)S(1)} %pad_maximum_fusion.1), channel_id=1, source_target_pairs={{0,4},{1,5},{2,6},{3,7},{4,0},{5,1},{6,2},{7,3},{8,12},{9,13},{10,... | collective-permute-start | bytes 110600 | tf_op jit(solution)/shard_map/ppermute | solution.py:143
  10.8 7.5 %collective-permute-start.5 = (bf16[8,4608]{1,0:T(8,128)(2,1)S(1)}, bf16[8,4608]{1,0:T(8,128)(2,1)S(1)}, u32[]{:S(2)}, u32[]{:S(2)}) collective-permute-start(bf16[8,4608]{1,0:T(8,128)(2,1)S(1)} %pad_maximum_fusion.refs_ref), channel_id=1, source_target_pairs={{0,2},{1,3},{2,0},{3,1},{4,6},{5,7},{6,4},{7,5},{8,10},{9,11},{10,... | collective-permute-start | bytes 221192 | tf_op jit(solution)/shard_map/ppermute | solution.py:143
  12.8 1.5 %collective-permute-start.2 = (s32[2,128]{1,0:T(2,128)}, s32[2,128]{1,0:T(2,128)S(1)}, u32[]{:S(2)}, u32[]{:S(2)}) collective-permute-start(s32[2,128]{1,0:T(2,128)} %bitcast.3), channel_id=1, source_target_pairs={{0,1},{1,0},{2,3},{3,2},{4,5},{5,4},{6,7},{7,6},{8,9},{9,8},{10,11... | collective-permute-start | bytes 3080 | tf_op jit(solution)/shard_map/ppermute | solution.py:143
  12.8 1.5 %collective-permute-start.1 = (f32[1,128]{1,0:T(1,128)}, f32[1,128]{1,0:T(1,128)S(1)}, u32[]{:S(2)}, u32[]{:S(2)}) collective-permute-start(f32[1,128]{1,0:T(1,128)} %bitcast.5), channel_id=1, source_target_pairs={{0,1},{1,0},{2,3},{3,2},{4,5},{5,4},{6,7},{7,6},{8,9},{9,8},{10,11... | collective-permute-start | bytes 1544 | tf_op jit(solution)/shard_map/ppermute | solution.py:143
  14.3 1.3 %copy-start = (bf16[128,4608]{1,0:T(8,128)(2,1)S(1)}, bf16[128,4608]{1,0:T(8,128)(2,1)}, u32[]{:S(2)}) copy-start(bf16[128,4608]{1,0:T(8,128)(2,1)} %p_own.1) | copy-start | bytes 3538948
  15.6 0.7 %copy-start.2 = (s32[128,2]{0,1:T(2,128)S(1)}, s32[128,2]{0,1:T(2,128)}, u32[]{:S(2)}) copy-start(s32[128,2]{0,1:T(2,128)} %param.7) | copy-start | bytes 3076
  16.2 0.7 %copy-start.3 = (f32[128]{0:T(128)S(1)}, f32[128]{0:T(128)}, u32[]{:S(2)}) copy-start(f32[128]{0:T(128)} %param.6) | copy-start | bytes 1540
  19.2 1.2 %collective-permute-start.6 = (f32[1,256]{1,0:T(1,128)S(1)}, f32[1,256]{1,0:T(1,128)S(1)}, u32[]{:S(2)}, u32[]{:S(2)}) collective-permute-start(f32[1,256]{1,0:T(1,128)S(1)} %get-tuple-element.16.near_ref), channel_id=1, source_target_pairs={{0,1},{1,0},{2,3},{3,2},{4,5},{5,4},{6,7},{7,6},{8,9},{9,8},{10,11... | collective-permute-start | bytes 3080 | tf_op jit(solution)/shard_map/ppermute | solution.py:143
  21.3 4.6 %collective-permute-start.7 = (bf16[8,4736]{1,0:T(8,128)(2,1)S(1)}, bf16[8,4736]{1,0:T(8,128)(2,1)S(1)}, u32[]{:S(2)}, u32[]{:S(2)}) collective-permute-start(bf16[8,4736]{1,0:T(8,128)(2,1)S(1)} %back_send.1), channel_id=1, source_target_pairs={{0,2},{1,3},{2,0},{3,1},{4,6},{5,7},{6,4},{7,5},{8,10},{9,11},{10,... | collective-permute-start | bytes 227336 | tf_op jit(solution)/shard_map/ppermute | solution.py:143
  25.9 4.0 %collective-permute-start.8 = (bf16[4,4736]{1,0:T(4,128)(2,1)S(1)}, bf16[4,4736]{1,0:T(4,128)(2,1)S(1)}, u32[]{:S(2)}, u32[]{:S(2)}) collective-permute-start(bf16[4,4736]{1,0:T(4,128)(2,1)S(1)} %slice.35), channel_id=1, source_target_pairs={{0,4},{1,5},{2,6},{3,7},{4,0},{5,1},{6,2},{7,3},{8,12},{9,13},{10,... | collective-permute-start | bytes 113672 | tf_op jit(solution)/shard_map/ppermute | solution.py:143
  30.0 4.7 %collective-permute-start.9 = (bf16[2,4736]{1,0:T(2,128)(2,1)S(1)}, bf16[2,4736]{1,0:T(2,128)(2,1)S(1)}, u32[]{:S(2)}, u32[]{:S(2)}) collective-permute-start(bf16[2,4736]{1,0:T(2,128)(2,1)S(1)} %slice.36), channel_id=1, source_target_pairs={{0,8},{1,9},{2,10},{3,11},{4,12},{5,13},{6,14},{7,15},{8,0},{9,1},... | collective-permute-start | bytes 56840 | tf_op jit(solution)/shard_map/ppermute | solution.py:143

commit v3 on v2

--- a/solution.py
+++ b/solution.py
@@ -10,6 +10,7 @@
 ROT = 12
 CYCLES = 12
 ANGLES = 384
+TOPK = 2
 WIDTH = CYCLES * ANGLES
 LANES = 128
 STEP = ANGLES // ROT
@@ -20,11 +21,27 @@
 PARAMS = pltpu.CompilerParams(vmem_limit_bytes=40 * 1024 * 1024)
 
 
-def stage_kernel(refs_ref, out_ref):
-    out_ref[...] = refs_ref[...]
-
-
-def score(refs_ref, p_ref, noise, turned_ref):
+def stage_kernel(refs, particles, noise, names, refs_ref, p_ref, packed_ref, noise_ref, names_ref, sems):
+    copies = [
+        pltpu.make_async_copy(src, dst, sems.at[i])
+        for i, (src, dst) in enumerate(
+            ((refs, refs_ref), (noise, noise_ref), (names, names_ref), (particles, p_ref))
+        )
+    ]
+    for copy in copies:
+        copy.start()
+    for copy in copies[:3]:
+        copy.wait()
+    packed_ref[0:1, :] = noise_ref[...]
+    packed_ref[1:1 + TOPK, :] = names_ref[...].astype(jnp.float32)
+    copies[3].wait()
+
+
+def particles_of(own_ref, far_ref, start, size):
+    return jnp.concatenate([own_ref[:, start:start + size], far_ref[:, start:start + size]], axis=0)
+
+
+def score(refs_ref, own_ref, far_ref, near_info, far_info, turned_ref):
     classes = refs_ref.shape[0]
     group = FINE * classes
     energy = jnp.zeros((classes, LANES), jnp.float32)
@@ -41,32 +58,20 @@
                 turned_ref[q * group:(q + 1) * group, at:at + LANES] = moved[:, v * LANES:(v + 1) * LANES]
     energy = jnp.sum(energy, axis=1, keepdims=True)
     dots = lax.dot_general(
-        turned_ref[...], p_ref[...], (((1,), (1,)), ((), ())), preferred_element_type=jnp.float32
+        turned_ref[...], particles_of(own_ref, far_ref, 0, WIDTH), (((1,), (1,)), ((), ())),
+        preferred_element_type=jnp.float32,
     )
     dots = dots.reshape(ROT, classes, dots.shape[1])
+    noise = jnp.concatenate([near_info[0:1, :], far_info[0:1, :]], axis=1)
     return noise[None] * (dots - 0.5 * energy[None])
 
 
-def early_kernel(p_own, p_far, noise_own, noise_far, name_own, name_far, refs_ref,
-                 p_ref, noise_ref, name_ref, logits_ref, turned_ref, sems):
-    rows = p_own.shape[0]
-    copies = [
-        pltpu.make_async_copy(p_own, p_ref.at[0:rows], sems.at[0]),
-        pltpu.make_async_copy(p_far, p_ref.at[rows:2 * rows], sems.at[1]),
-        pltpu.make_async_copy(noise_own, noise_ref.at[:, 0:rows], sems.at[2]),
-        pltpu.make_async_copy(noise_far, noise_ref.at[:, rows:2 * rows], sems.at[3]),
-        pltpu.make_async_copy(name_own, name_ref.at[:, 0:rows], sems.at[4]),
-        pltpu.make_async_copy(name_far, name_ref.at[:, rows:2 * rows], sems.at[5]),
-    ]
-    for copy in copies:
-        copy.start()
-    for copy in copies:
-        copy.wait()
-    logits_ref[...] = score(refs_ref, p_ref, noise_ref[...], turned_ref)
-
-
-def late_kernel(refs_ref, p_ref, noise_ref, early_ref, logits_ref, part_ref, turned_ref):
-    late = score(refs_ref, p_ref, noise_ref[...], turned_ref)
+def early_kernel(refs_ref, own_ref, far_ref, near_info, far_info, logits_ref, turned_ref):
+    logits_ref[...] = score(refs_ref, own_ref, far_ref, near_info, far_info, turned_ref)
+
+
+def late_kernel(refs_ref, own_ref, far_ref, near_info, far_info, early_ref, logits_ref, part_ref, turned_ref):
+    late = score(refs_ref, own_ref, far_ref, near_info, far_info, turned_ref)
     logits_ref[...] = late
     early = early_ref[...]
     top = jnp.maximum(jnp.max(late, axis=0), jnp.max(early, axis=0))
@@ -75,10 +80,13 @@
     part_ref[...] = top + jnp.log(jnp.sum(total, axis=0, keepdims=True))
 
 
-def back_kernel(bits, owned, first, logits_ref, near_ref, far_ref, name_ref, p_ref, sums_ref, log_ref=None):
+def back_kernel(bits, owned, first, logits_ref, near_ref, other_ref, own_ref, far_ref, near_info, far_info,
+                sums_ref, log_ref=None):
     classes, rows = logits_ref.shape[1:]
+    here = own_ref.shape[0]
     me = lax.axis_index("blk")
-    near, far = near_ref[...], far_ref[...]
+    near = near_ref[...]
+    far = jnp.concatenate([other_ref[:, here:], other_ref[:, :here]], axis=1)
     top = jnp.maximum(near, far)
     log_evidence = top + jnp.log(jnp.exp(near - top) + jnp.exp(far - top))
     if log_ref is not None:
@@ -90,7 +98,10 @@
     for i in range(bits - 1):
         mixed = mixed + (((place >> i) & 1) << (bits - 1 - i))
     ident = (mixed ^ me) * owned + row % owned
-    named = (ident == name_ref[0:1, :]) | (ident == name_ref[1:2, :])
+    names = jnp.concatenate([near_info[...], far_info[...]], axis=1).astype(jnp.int32)
+    named = ident == names[1:2, :]
+    for j in range(1, TOPK):
+        named = named | (ident == names[1 + j:2 + j, :])
     post = jnp.where(named[None], jnp.exp(logits_ref[...] - log_evidence[None]), 0.0)
     weights = jnp.sum(post, axis=0).astype(jnp.bfloat16).astype(jnp.float32)
     mass = jnp.broadcast_to(jnp.sum(weights, axis=1, keepdims=True), (classes, LANES))
@@ -103,7 +114,8 @@
     both = jnp.concatenate([high, low], axis=0)
     group = FINE * classes
     for c in range(0, CYCLES, 2):
-        part = jnp.dot(both, p_ref[:, c * ANGLES:(c + 2) * ANGLES], preferred_element_type=jnp.float32)
+        chunk = particles_of(own_ref, far_ref, c * ANGLES, 2 * ANGLES)
+        part = jnp.dot(both, chunk, preferred_element_type=jnp.float32)
         part = part[:count] + part[count:]
         for d in range(2):
             blocks = []
@@ -142,13 +154,24 @@
     def swap(x, bit):
         return lax.ppermute(x, "blk", [(i, i ^ bit) for i in range(devices)])
 
-    noise, names = inv_noise[None, :], assign.T
-    p_far, noise_far, names_far = swap(particles, 1), swap(noise, 1), swap(names, 1)
-
-    own = pl.pallas_call(
-        stage_kernel, out_shape=jax.ShapeDtypeStruct((owned, width), bf16),
-        in_specs=[VMEM], out_specs=VMEM, compiler_params=PARAMS, name="stage",
-    )(references)
+    p_far = swap(particles, 1)
+    held = [pltpu.with_memory_space_constraint(x, pltpu.HBM)
+            for x in (references, particles, inv_noise[None, :], assign.T)]
+    own, p_own, near_info, *_ = pl.pallas_call(
+        stage_kernel,
+        out_shape=(
+            jax.ShapeDtypeStruct((owned, width), bf16),
+            jax.ShapeDtypeStruct((rows, width), bf16),
+            jax.ShapeDtypeStruct((1 + TOPK, rows), f32),
+            jax.ShapeDtypeStruct((1, rows), f32),
+            jax.ShapeDtypeStruct((TOPK, rows), jnp.int32),
+        ),
+        in_specs=[HBM] * 4, out_specs=[VMEM] * 5,
+        scratch_shapes=[pltpu.SemaphoreType.DMA((4,))],
+        compiler_params=PARAMS, name="stage",
+    )(*held)
+    far_info = swap(near_info, 1)
+
     gathered = references
     for b in range(bits - 1, 0, -1):
         got = swap(gathered, 1 << b)
@@ -158,46 +181,35 @@
             gathered = jnp.concatenate([gathered, got], axis=0)
 
     turned = pltpu.VMEM((ROT * half, width), bf16)
-    score_cost = pl.CostEstimate(
+    cost = pl.CostEstimate(
         flops=2 * ROT * half * both * width, bytes_accessed=4 * both * width, transcendentals=0)
-    p_all, noise_all, names_all, early = pl.pallas_call(
+    shared = (p_own, p_far, near_info, far_info)
+    early = pl.pallas_call(
         early_kernel,
-        out_shape=(
-            jax.ShapeDtypeStruct((both, width), bf16),
-            jax.ShapeDtypeStruct((1, both), f32),
-            jax.ShapeDtypeStruct((2, both), jnp.int32),
-            jax.ShapeDtypeStruct((ROT, half, both), f32),
-        ),
-        in_specs=[HBM] * 6 + [VMEM],
-        out_specs=[VMEM] * 4,
-        scratch_shapes=[turned, pltpu.SemaphoreType.DMA((6,))],
-        compiler_params=PARAMS, cost_estimate=score_cost, name="early",
-    )(particles, p_far, noise, noise_far, names, names_far, gathered)
+        out_shape=jax.ShapeDtypeStruct((ROT, half, both), f32),
+        in_specs=[VMEM] * 5, out_specs=VMEM, scratch_shapes=[turned],
+        compiler_params=PARAMS, cost_estimate=cost, name="early",
+    )(gathered, *shared)
     late, near = pl.pallas_call(
         late_kernel,
         out_shape=(jax.ShapeDtypeStruct((ROT, half, both), f32), jax.ShapeDtypeStruct((1, both), f32)),
-        in_specs=[VMEM] * 4,
-        out_specs=[VMEM] * 2,
-        scratch_shapes=[turned],
-        compiler_params=PARAMS, cost_estimate=score_cost, name="late",
-    )(got, p_all, noise_all, early)
-    far = swap(near, 1)
-    far = jnp.concatenate([far[:, rows:], far[:, :rows]], axis=1)
+        in_specs=[VMEM] * 6, out_specs=[VMEM] * 2, scratch_shapes=[turned],
+        compiler_params=PARAMS, cost_estimate=cost, name="late",
+    )(got, *shared, early)
+    other = swap(near, 1)
 
     send = pl.pallas_call(
         functools.partial(back_kernel, bits, owned, half),
         out_shape=jax.ShapeDtypeStruct((half, wide), bf16),
-        in_specs=[VMEM] * 5,
-        out_specs=VMEM,
-        compiler_params=PARAMS, cost_estimate=score_cost, name="back_send",
-    )(late, near, far, names_all, p_all)
+        in_specs=[VMEM] * 7, out_specs=VMEM,
+        compiler_params=PARAMS, cost_estimate=cost, name="back_send",
+    )(late, near, other, *shared)
     keep, log_evidence = pl.pallas_call(
         functools.partial(back_kernel, bits, owned, 0),
         out_shape=(jax.ShapeDtypeStruct((half, wide), f32), jax.ShapeDtypeStruct((1, rows), f32)),
-        in_specs=[VMEM] * 5,
-        out_specs=[VMEM] * 2,
-        compiler_params=PARAMS, cost_estimate=score_cost, name="back_keep",
-    )(early, near, far, names_all, p_all)
+        in_specs=[VMEM] * 7, out_specs=[VMEM] * 2,
+        compiler_params=PARAMS, cost_estimate=cost, name="back_keep",
+    )(early, near, other, *shared)
 
     for b in range(1, bits):
         got = swap(send, 1 << b)

time: 35.6 us -> 32.5 us (0.913)
  local copies, waits for them, and re-layouts: 3.41 us -> 0.06 us
  waiting for transfers between devices: 13.2 us -> 10.7 us
  starting transfers between devices: 13.2 us -> 14.7 us
  Pallas kernels: 4.67 us -> 6.08 us
    unnamed x8 -> x0, local copies, waits for them, and re-layouts: 3.36 us -> none
    ppermute x10 -> x9, waiting for transfers between devices: 13.2 us -> 10.7 us  [swap(): return lax.ppermute(x, 'blk', [(i, i ^ bit) for i in range(devices)])]
    ppermute x10 -> x9, starting transfers between devices: 13.2 us -> 14.7 us  [swap(): return lax.ppermute(x, 'blk', [(i, i ^ bit) for i in range(devices)])]
    pallas_call x2, Pallas kernels: 1.41 us -> 2.8 us  [the longest x1 1.92 us: local(): pl.pallas_call(stage_kernel, out_shape=(jax.ShapeDtypeStruct((owned, widt...]
  transfers between devices with their start and end apart: 10 -> 9, of which waited for: 7 -> 7; matrix products, arithmetic and copies ran while one was open for 0% -> 0% of each run, Pallas kernels for 6% -> 11%
where the time goes in v3:
time: 32.5 us; the launch traced here: 32.4 us
  starting transfers between devices  14.7 us (45%)
  waiting for transfers between devices  10.7 us (33%)
  Pallas kernels  6.08 us (19%)
  between operations  0.7 us (2%)
    ppermute x9, starting transfers between devices, swap(): return lax.ppermute(x, 'blk', [(i, i ^ bit) for i in range(devices)])  14.7 us
    ppermute x9, waiting for transfers between devices, swap(): return lax.ppermute(x, 'blk', [(i, i ^ bit) for i in range(devices)])  10.7 us
    pallas_call x1, Pallas kernels, local(): pl.pallas_call(stage_kernel, out_shape=(jax.ShapeDtypeStruct((owned, widt...  1.92 us
    pallas_call x1, Pallas kernels, local(): pl.pallas_call(late_kernel, out_shape=(jax.ShapeDtypeStruct((ROT, half, b...  0.93 us
    pallas_call x1, Pallas kernels, local(): pl.pallas_call(early_kernel, out_shape=jax.ShapeDtypeStruct((ROT, half, b...  0.88 us
    pallas_call x1, Pallas kernels, local(): pl.pallas_call(functools.partial(back_kernel, bits, owned, half), out_sha...  0.86 us
    pallas_call x1, Pallas kernels, local(): pl.pallas_call(functools.partial(back_kernel, bits, owned, 0), out_shape=...  0.86 us
  transfers between devices with their start and end apart: 9, of which 7 were waited for; matrix products, arithmetic and copies ran while one was open for 0% of the time, Pallas kernels for 11%

profile of v3, /device:TPU:0, one launch (start us, length us, event | category | flops | bytes accessed | tf_op | source)
XLA Modules:
  0.0 32.4 jit_solution(3198178735152156348)
XLA Ops:
  0.6 4.1 %collective-permute-start = (bf16[2,4608]{1,0:T(2,128)(2,1)}, bf16[2,4608]{1,0:T(2,128)(2,1)S(1)}, u32[]{:S(2)}, u32[]{:S(2)}) collective-permute-start(bf16[2,4608]{1,0:T(2,128)(2,1)} %refs.1), channel_id=1, source_target_pairs={{0,8},{1,9},{2,10},{3,11},{4,12},{5,13},{6,14},{7,15},{8,0},{9,1},... | collective-permute-start | bytes 55304 | tf_op jit(solution)/shard_map/ppermute | solution.py:155
  4.7 0.0 collective-permute-start.2
  4.7 1.9 %stage.1 = (bf16[2,4608]{1,0:T(2,128)(2,1)S(1)}, bf16[128,4608]{1,0:T(8,128)(2,1)S(1)}, f32[3,128]{1,0:T(4,128)S(1)}, f32[1,128]{1,0:T(1,128)}, s32[2,128]{1,0:T(2,128)}) custom-call(bf16[2,4608]{1,0:T(2,128)(2,1)} %refs.1, bf16[128,4608]{1,0:T(8,128)(2,1)} %particles.1, f32[1,128]{1,0:T(1,128)} %bitcast.4, s32[2,128]{1,0:T(2,128)} %bitcast.3), custom_call_target="tpu_custom_call" | custom-call | tf_op jit(solution)/shard_map/stage/pallas_call | solution.py:160
  6.7 0.0 collective-permute-done
  6.7 2.0 %collective-permute-start.1 = (bf16[4,4608]{1,0:T(4,128)(2,1)S(1)}, bf16[4,4608]{1,0:T(4,128)(2,1)S(1)}, u32[]{:S(2)}, u32[]{:S(2)}) collective-permute-start(bf16[4,4608]{1,0:T(4,128)(2,1)S(1)} %pad_maximum_fusion.1), channel_id=1, source_target_pairs={{0,4},{1,5},{2,6},{3,7},{4,0},{5,1},{6,2},{7,3},{8,12},{9,13},{10,... | collective-permute-start | bytes 110600 | tf_op jit(solution)/shard_map/ppermute | solution.py:155
  8.7 2.1 %collective-permute-done.1 = bf16[4,4608]{1,0:T(4,128)(2,1)S(1)} collective-permute-done((bf16[4,4608]{1,0:T(4,128)(2,1)S(1)}, bf16[4,4608]{1,0:T(4,128)(2,1)S(1)}, u32[]{:S(2)}, u32[]{:S(2)}) %collective-permute-start.1) | collective-permute-done | bytes 36896 | tf_op jit(solution)/shard_map/ppermute | solution.py:155
  10.8 0.1 pad_maximum_fusion.refs_ref
  10.8 2.0 %collective-permute-start.4 = (bf16[8,4608]{1,0:T(8,128)(2,1)S(1)}, bf16[8,4608]{1,0:T(8,128)(2,1)S(1)}, u32[]{:S(2)}, u32[]{:S(2)}) collective-permute-start(bf16[8,4608]{1,0:T(8,128)(2,1)S(1)} %pad_maximum_fusion.refs_ref), channel_id=1, source_target_pairs={{0,2},{1,3},{2,0},{3,1},{4,6},{5,7},{6,4},{7,5},{8,10},{9,11},{10,... | collective-permute-start | bytes 221192 | tf_op jit(solution)/shard_map/ppermute | solution.py:155
  12.8 1.2 %collective-permute-done.3.far_info = f32[3,128]{1,0:T(4,128)S(1)} collective-permute-done((f32[3,128]{1,0:T(4,128)S(1)}, f32[3,128]{1,0:T(4,128)S(1)}, u32[]{:S(2)}, u32[]{:S(2)}) %collective-permute-start.3) | collective-permute-done | bytes 1568 | tf_op jit(solution)/shard_map/ppermute | solution.py:155
  14.0 0.0 collective-permute-done.2.far_ref
  14.0 0.9 %early.1.early_ref.logits_ref = f32[12,8,256]{2,1,0:T(8,128)S(1)} custom-call(bf16[8,4608]{1,0:T(8,128)(2,1)S(1)} %pad_maximum_fusion.refs_ref, bf16[128,4608]{1,0:T(8,128)(2,1)S(1)} %get-tuple-element.13.own_ref, bf16[128,4608]{1,0:T(8,128)(2,1)S(1)} %collective-permute-done.2.far_ref, f32[3,128]{1,0:T(4,128)S(1)} %get-tuple-element.14.near_info, ...), custom_call_target="tpu_custom_call" | custom-call | flops 226492416 | bytes 4718592 | tf_op jit(solution)/shard_map/early/pallas_call | solution.py:187
  14.9 0.4 %collective-permute-done.4.refs_ref = bf16[8,4608]{1,0:T(8,128)(2,1)S(1)} collective-permute-done((bf16[8,4608]{1,0:T(8,128)(2,1)S(1)}, bf16[8,4608]{1,0:T(8,128)(2,1)S(1)}, u32[]{:S(2)}, u32[]{:S(2)}) %collective-permute-start.4) | collective-permute-done | bytes 73760 | tf_op jit(solution)/shard_map/ppermute | solution.py:155
  15.2 0.9 %late.1 = (f32[12,8,256]{2,1,0:T(8,128)S(1)}, f32[1,256]{1,0:T(1,128)S(1)}) custom-call(bf16[8,4608]{1,0:T(8,128)(2,1)S(1)} %collective-permute-done.4.refs_ref, bf16[128,4608]{1,0:T(8,128)(2,1)S(1)} %get-tuple-element.13.own_ref, bf16[128,4608]{1,0:T(8,128)(2,1)S(1)} %collective-permute-done.2.far_ref, f32[3,128]{1,0:T(4,128)S(1)} %get-tuple-element.14.near_info, ...), custom_call_target="tpu_custom_call" | custom-call | flops 226492416 | bytes 4718592 | tf_op jit(solution)/shard_map/late/pallas_call | solution.py:193
  16.2 0.1 collective-permute-start.5
  16.3 1.1 %collective-permute-done.5.other_ref = f32[1,256]{1,0:T(1,128)S(1)} collective-permute-done((f32[1,256]{1,0:T(1,128)S(1)}, f32[1,256]{1,0:T(1,128)S(1)}, u32[]{:S(2)}, u32[]{:S(2)}) %collective-permute-start.5) | collective-permute-done | bytes 1056 | tf_op jit(solution)/shard_map/ppermute | solution.py:155
  17.4 0.9 %back_send.1 = bf16[8,4736]{1,0:T(8,128)(2,1)S(1)} custom-call(f32[12,8,256]{2,1,0:T(8,128)S(1)} %get-tuple-element.17.logits_ref, f32[1,256]{1,0:T(1,128)S(1)} %get-tuple-element.15.near_ref, f32[1,256]{1,0:T(1,128)S(1)} %collective-permute-done.5.other_ref, bf16[128,4608]{1,0:T(8,128)(2,1)S(1)} %get-tuple-element.13.own_ref, ...), custom_call_target="tpu_custom_call" | custom-call | flops 226492416 | bytes 4718592 | tf_op jit(solution)/shard_map/back_send/pallas_call | solution.py:201
  18.2 2.0 %collective-permute-start.6 = (bf16[8,4736]{1,0:T(8,128)(2,1)S(1)}, bf16[8,4736]{1,0:T(8,128)(2,1)S(1)}, u32[]{:S(2)}, u32[]{:S(2)}) collective-permute-start(bf16[8,4736]{1,0:T(8,128)(2,1)S(1)} %back_send.1), channel_id=1, source_target_pairs={{0,2},{1,3},{2,0},{3,1},{4,6},{5,7},{6,4},{7,5},{8,10},{9,11},{10,... | collective-permute-start | bytes 227336 | tf_op jit(solution)/shard_map/ppermute | solution.py:155
  20.2 0.9 %back_keep.1 = (f32[8,4736]{1,0:T(8,128)S(1)}, f32[1,128]{1,0:T(1,128)}) custom-call(f32[12,8,256]{2,1,0:T(8,128)S(1)} %early.1.early_ref.logits_ref, f32[1,256]{1,0:T(1,128)S(1)} %get-tuple-element.15.near_ref, f32[1,256]{1,0:T(1,128)S(1)} %collective-permute-done.5.other_ref, bf16[128,4608]{1,0:T(8,128)(2,1)S(1)} %get-tuple-element.13.own_ref, ...), custom_call_target="tpu_custom_call" | custom-call | flops 226492416 | bytes 4718592 | tf_op jit(solution)/shard_map/back_keep/pallas_call | solution.py:207
  21.1 1.8 %collective-permute-done.6 = bf16[8,4736]{1,0:T(8,128)(2,1)S(1)} collective-permute-done((bf16[8,4736]{1,0:T(8,128)(2,1)S(1)}, bf16[8,4736]{1,0:T(8,128)(2,1)S(1)}, u32[]{:S(2)}, u32[]{:S(2)}) %collective-permute-start.6) | collective-permute-done | bytes 75808 | tf_op jit(solution)/shard_map/ppermute | solution.py:155
  22.9 1.8 %collective-permute-start.7 = (bf16[4,4736]{1,0:T(4,128)(2,1)S(1)}, bf16[4,4736]{1,0:T(4,128)(2,1)S(1)}, u32[]{:S(2)}, u32[]{:S(2)}) collective-permute-start(bf16[4,4736]{1,0:T(4,128)(2,1)S(1)} %slice.25), channel_id=1, source_target_pairs={{0,4},{1,5},{2,6},{3,7},{4,0},{5,1},{6,2},{7,3},{8,12},{9,13},{10,... | collective-permute-start | bytes 113672 | tf_op jit(solution)/shard_map/ppermute | solution.py:155
  24.7 2.2 %collective-permute-done.7 = bf16[4,4736]{1,0:T(4,128)(2,1)S(1)} collective-permute-done((bf16[4,4736]{1,0:T(4,128)(2,1)S(1)}, bf16[4,4736]{1,0:T(4,128)(2,1)S(1)}, u32[]{:S(2)}, u32[]{:S(2)}) %collective-permute-start.7) | collective-permute-done | bytes 37920 | tf_op jit(solution)/shard_map/ppermute | solution.py:155
  27.0 2.8 %collective-permute-start.8 = (bf16[2,4736]{1,0:T(2,128)(2,1)S(1)}, bf16[2,4736]{1,0:T(2,128)(2,1)S(1)}, u32[]{:S(2)}, u32[]{:S(2)}) collective-permute-start(bf16[2,4736]{1,0:T(2,128)(2,1)S(1)} %slice.26), channel_id=1, source_target_pairs={{0,8},{1,9},{2,10},{3,11},{4,12},{5,13},{6,14},{7,15},{8,0},{9,1},... | collective-permute-start | bytes 56840 | tf_op jit(solution)/shard_map/ppermute | solution.py:155
  29.8 1.9 %collective-permute-done.8.got_ref = bf16[2,4736]{1,0:T(2,128)(2,1)S(1)} collective-permute-done((bf16[2,4736]{1,0:T(2,128)(2,1)S(1)}, bf16[2,4736]{1,0:T(2,128)(2,1)S(1)}, u32[]{:S(2)}, u32[]{:S(2)}) %collective-permute-start.8) | collective-permute-done | bytes 18976 | tf_op jit(solution)/shard_map/ppermute | solution.py:155
  31.7 0.6 %last.1 = (f32[2,4608]{1,0:T(2,128)}, f32[2]{0:T(128)}) custom-call(f32[2,4736]{1,0:T(2,128)S(1)} %slice.20.keep_ref, bf16[2,4736]{1,0:T(2,128)(2,1)S(1)} %collective-permute-done.8.got_ref), custom_call_target="tpu_custom_call" | custom-call | tf_op jit(solution)/shard_map/last/pallas_call | solution.py:220
  (7 shorter events, 0.1 us)
Async XLA Ops:
  0.6 6.1 %collective-permute-start = (bf16[2,4608]{1,0:T(2,128)(2,1)}, bf16[2,4608]{1,0:T(2,128)(2,1)S(1)}, u32[]{:S(2)}, u32[]{:S(2)}) collective-permute-start(bf16[2,4608]{1,0:T(2,128)(2,1)} %refs.1), channel_id=1, source_target_pairs={{0,8},{1,9},{2,10},{3,11},{4,12},{5,13},{6,14},{7,15},{8,0},{9,1},... | collective-permute-start | bytes 55304 | tf_op jit(solution)/shard_map/ppermute | solution.py:155
  4.7 9.2 %collective-permute-start.2 = (bf16[128,4608]{1,0:T(8,128)(2,1)}, bf16[128,4608]{1,0:T(8,128)(2,1)S(1)}, u32[]{:S(2)}, u32[]{:S(2)}) collective-permute-start(bf16[128,4608]{1,0:T(8,128)(2,1)} %particles.1), channel_id=1, source_target_pairs={{0,1},{1,0},{2,3},{3,2},{4,5},{5,4},{6,7},{7,6},{8,9},{9,8},{10,11... | collective-permute-start | bytes 3538952 | tf_op jit(solution)/shard_map/ppermute | solution.py:155
  6.7 4.0 %collective-permute-start.1 = (bf16[4,4608]{1,0:T(4,128)(2,1)S(1)}, bf16[4,4608]{1,0:T(4,128)(2,1)S(1)}, u32[]{:S(2)}, u32[]{:S(2)}) collective-permute-start(bf16[4,4608]{1,0:T(4,128)(2,1)S(1)} %pad_maximum_fusion.1), channel_id=1, source_target_pairs={{0,4},{1,5},{2,6},{3,7},{4,0},{5,1},{6,2},{7,3},{8,12},{9,13},{10,... | collective-permute-start | bytes 110600 | tf_op jit(solution)/shard_map/ppermute | solution.py:155
  10.8 4.4 %collective-permute-start.4 = (bf16[8,4608]{1,0:T(8,128)(2,1)S(1)}, bf16[8,4608]{1,0:T(8,128)(2,1)S(1)}, u32[]{:S(2)}, u32[]{:S(2)}) collective-permute-start(bf16[8,4608]{1,0:T(8,128)(2,1)S(1)} %pad_maximum_fusion.refs_ref), channel_id=1, source_target_pairs={{0,2},{1,3},{2,0},{3,1},{4,6},{5,7},{6,4},{7,5},{8,10},{9,11},{10,... | collective-permute-start | bytes 221192 | tf_op jit(solution)/shard_map/ppermute | solution.py:155
  12.8 1.2 %collective-permute-start.3 = (f32[3,128]{1,0:T(4,128)S(1)}, f32[3,128]{1,0:T(4,128)S(1)}, u32[]{:S(2)}, u32[]{:S(2)}) collective-permute-start(f32[3,128]{1,0:T(4,128)S(1)} %get-tuple-element.14.near_info), channel_id=1, source_target_pairs={{0,1},{1,0},{2,3},{3,2},{4,5},{5,4},{6,7},{7,6},{8,9},{9,8},{10,11... | collective-permute-start | bytes 4616 | tf_op jit(solution)/shard_map/ppermute | solution.py:155
  16.2 1.2 %collective-permute-start.5 = (f32[1,256]{1,0:T(1,128)S(1)}, f32[1,256]{1,0:T(1,128)S(1)}, u32[]{:S(2)}, u32[]{:S(2)}) collective-permute-start(f32[1,256]{1,0:T(1,128)S(1)} %get-tuple-element.15.near_ref), channel_id=1, source_target_pairs={{0,1},{1,0},{2,3},{3,2},{4,5},{5,4},{6,7},{7,6},{8,9},{9,8},{10,11... | collective-permute-start | bytes 3080 | tf_op jit(solution)/shard_map/ppermute | solution.py:155
  18.2 4.6 %collective-permute-start.6 = (bf16[8,4736]{1,0:T(8,128)(2,1)S(1)}, bf16[8,4736]{1,0:T(8,128)(2,1)S(1)}, u32[]{:S(2)}, u32[]{:S(2)}) collective-permute-start(bf16[8,4736]{1,0:T(8,128)(2,1)S(1)} %back_send.1), channel_id=1, source_target_pairs={{0,2},{1,3},{2,0},{3,1},{4,6},{5,7},{6,4},{7,5},{8,10},{9,11},{10,... | collective-permute-start | bytes 227336 | tf_op jit(solution)/shard_map/ppermute | solution.py:155
  22.9 4.0 %collective-permute-start.7 = (bf16[4,4736]{1,0:T(4,128)(2,1)S(1)}, bf16[4,4736]{1,0:T(4,128)(2,1)S(1)}, u32[]{:S(2)}, u32[]{:S(2)}) collective-permute-start(bf16[4,4736]{1,0:T(4,128)(2,1)S(1)} %slice.25), channel_id=1, source_target_pairs={{0,4},{1,5},{2,6},{3,7},{4,0},{5,1},{6,2},{7,3},{8,12},{9,13},{10,... | collective-permute-start | bytes 113672 | tf_op jit(solution)/shard_map/ppermute | solution.py:155
  27.0 4.7 %collective-permute-start.8 = (bf16[2,4736]{1,0:T(2,128)(2,1)S(1)}, bf16[2,4736]{1,0:T(2,128)(2,1)S(1)}, u32[]{:S(2)}, u32[]{:S(2)}) collective-permute-start(bf16[2,4736]{1,0:T(2,128)(2,1)S(1)} %slice.26), channel_id=1, source_target_pairs={{0,8},{1,9},{2,10},{3,11},{4,12},{5,13},{6,14},{7,15},{8,0},{9,1},... | collective-permute-start | bytes 56840 | tf_op jit(solution)/shard_map/ppermute | solution.py:155

commit v4 on v3

--- a/solution.py
+++ b/solution.py
@@ -21,12 +21,11 @@
 PARAMS = pltpu.CompilerParams(vmem_limit_bytes=40 * 1024 * 1024)
 
 
-def stage_kernel(refs, particles, noise, names, refs_ref, p_ref, packed_ref, noise_ref, names_ref, sems):
+def stage_kernel(refs, noise, names, particles, refs_ref, packed_ref, p_ref, noise_ref, names_ref, sems):
     copies = [
         pltpu.make_async_copy(src, dst, sems.at[i])
         for i, (src, dst) in enumerate(
-            ((refs, refs_ref), (noise, noise_ref), (names, names_ref), (particles, p_ref))
-        )
+            ((refs, refs_ref), (noise, noise_ref), (names, names_ref), (particles, p_ref)))
     ]
     for copy in copies:
         copy.start()
@@ -37,11 +36,27 @@
     copies[3].wait()
 
 
+def flip(p_ref, flipped_ref):
+    for at in range(0, WIDTH, LANES):
+        flipped_ref[at:at + LANES, :] = p_ref[:, at:at + LANES].T
+
+
+def flip_kernel(after_ref, p_ref, flipped_ref):
+    flip(p_ref, flipped_ref)
+
+
+def join_kernel(held_ref, got_ref, *rest):
+    out_ref = rest[-1]
+    count = held_ref.shape[0]
+    out_ref[0:count, :] = held_ref[...]
+    out_ref[count:2 * count, :] = got_ref[...]
+
+
 def particles_of(own_ref, far_ref, start, size):
     return jnp.concatenate([own_ref[:, start:start + size], far_ref[:, start:start + size]], axis=0)
 
 
-def score(refs_ref, own_ref, far_ref, near_info, far_info, turned_ref):
+def score(refs_ref, own_flipped, far_flipped, near_info, far_info, turned_ref):
     classes = refs_ref.shape[0]
     group = FINE * classes
     energy = jnp.zeros((classes, LANES), jnp.float32)
@@ -58,20 +73,21 @@
                 turned_ref[q * group:(q + 1) * group, at:at + LANES] = moved[:, v * LANES:(v + 1) * LANES]
     energy = jnp.sum(energy, axis=1, keepdims=True)
     dots = lax.dot_general(
-        turned_ref[...], particles_of(own_ref, far_ref, 0, WIDTH), (((1,), (1,)), ((), ())),
-        preferred_element_type=jnp.float32,
+        turned_ref[...], jnp.concatenate([own_flipped[...], far_flipped[...]], axis=1),
+        (((1,), (0,)), ((), ())), preferred_element_type=jnp.float32,
     )
     dots = dots.reshape(ROT, classes, dots.shape[1])
     noise = jnp.concatenate([near_info[0:1, :], far_info[0:1, :]], axis=1)
     return noise[None] * (dots - 0.5 * energy[None])
 
 
-def early_kernel(refs_ref, own_ref, far_ref, near_info, far_info, logits_ref, turned_ref):
-    logits_ref[...] = score(refs_ref, own_ref, far_ref, near_info, far_info, turned_ref)
-
-
-def late_kernel(refs_ref, own_ref, far_ref, near_info, far_info, early_ref, logits_ref, part_ref, turned_ref):
-    late = score(refs_ref, own_ref, far_ref, near_info, far_info, turned_ref)
+def early_kernel(refs_ref, own_flipped, far_ref, near_info, far_info, logits_ref, far_flipped, turned_ref):
+    flip(far_ref, far_flipped)
+    logits_ref[...] = score(refs_ref, own_flipped, far_flipped, near_info, far_info, turned_ref)
+
+
+def late_kernel(refs_ref, own_flipped, far_flipped, near_info, far_info, early_ref, logits_ref, part_ref, turned_ref):
+    late = score(refs_ref, own_flipped, far_flipped, near_info, far_info, turned_ref)
     logits_ref[...] = late
     early = early_ref[...]
     top = jnp.maximum(jnp.max(late, axis=0), jnp.max(early, axis=0))
@@ -95,8 +111,11 @@
     row = lax.broadcasted_iota(jnp.int32, (classes, rows), 0) + first
     place = row // owned
     mixed = jnp.zeros_like(place)
-    for i in range(bits - 1):
-        mixed = mixed + (((place >> i) & 1) << (bits - 1 - i))
+    color = me
+    for i in range(1, bits):
+        color = color ^ (me >> i)
+    for i, (even, odd) in enumerate(offsets(bits)):
+        mixed = mixed ^ ((place >> i) & 1) * jnp.where(color % 2 == 0, even, odd)
     ident = (mixed ^ me) * owned + row % owned
     names = jnp.concatenate([near_info[...], far_info[...]], axis=1).astype(jnp.int32)
     named = ident == names[1:2, :]
@@ -141,6 +160,12 @@
         mass_ref[i] = total[i, WIDTH]
 
 
+def offsets(bits):
+    even = [(1 << b) | 1 for b in range(bits - 1, 0, -1)]
+    odd = even[:-2] + even[:-3:-1]
+    return list(zip(even, odd))
+
+
 def local(particles, references, inv_noise, assign):
     rows, width = particles.shape
     owned = references.shape[0]
@@ -151,52 +176,63 @@
     wide = width + LANES
     f32, bf16 = jnp.float32, jnp.bfloat16
 
-    def swap(x, bit):
-        return lax.ppermute(x, "blk", [(i, i ^ bit) for i in range(devices)])
-
-    p_far = swap(particles, 1)
+    def swap(x, even, odd):
+        return lax.ppermute(x, "blk", [(i, i ^ (odd if i.bit_count() % 2 else even)) for i in range(devices)])
+
+    def join(*operands):
+        held = operands[0]
+        return pl.pallas_call(
+            join_kernel, out_shape=jax.ShapeDtypeStruct((2 * held.shape[0], width), bf16),
+            in_specs=[VMEM] * len(operands), out_specs=VMEM, compiler_params=PARAMS, name="join",
+        )(*operands)
+
+    rounds = offsets(bits)
+    got = swap(references, *rounds[0])
+    p_far = swap(particles, 1, 1)
     held = [pltpu.with_memory_space_constraint(x, pltpu.HBM)
-            for x in (references, particles, inv_noise[None, :], assign.T)]
-    own, p_own, near_info, *_ = pl.pallas_call(
+            for x in (references, inv_noise[None, :], assign.T, particles)]
+    own, near_info, p_own = pl.pallas_call(
         stage_kernel,
         out_shape=(
             jax.ShapeDtypeStruct((owned, width), bf16),
+            jax.ShapeDtypeStruct((1 + TOPK, rows), f32),
             jax.ShapeDtypeStruct((rows, width), bf16),
-            jax.ShapeDtypeStruct((1 + TOPK, rows), f32),
-            jax.ShapeDtypeStruct((1, rows), f32),
-            jax.ShapeDtypeStruct((TOPK, rows), jnp.int32),
         ),
-        in_specs=[HBM] * 4, out_specs=[VMEM] * 5,
-        scratch_shapes=[pltpu.SemaphoreType.DMA((4,))],
+        in_specs=[HBM] * 4, out_specs=[VMEM] * 3,
+        scratch_shapes=[
+            pltpu.VMEM((1, rows), f32), pltpu.VMEM((TOPK, rows), jnp.int32), pltpu.SemaphoreType.DMA((4,))],
         compiler_params=PARAMS, name="stage",
     )(*held)
-    far_info = swap(near_info, 1)
-
-    gathered = references
-    for b in range(bits - 1, 0, -1):
-        got = swap(gathered, 1 << b)
-        if b == bits - 1:
-            gathered = own
-        if b > 1:
-            gathered = jnp.concatenate([gathered, got], axis=0)
+    far_info = swap(near_info, 1, 1)
+
+    gathered = join(own, got)
+    own_flipped = pl.pallas_call(
+        flip_kernel, out_shape=jax.ShapeDtypeStruct((width, rows), bf16),
+        in_specs=[VMEM] * 2, out_specs=VMEM, compiler_params=PARAMS, name="flip",
+    )(gathered, p_own)
+    for r, pair in enumerate(rounds[1:], 1):
+        got = swap(gathered, *pair)
+        if r < len(rounds) - 1:
+            gathered = join(gathered, got, own_flipped, far_info)
 
     turned = pltpu.VMEM((ROT * half, width), bf16)
     cost = pl.CostEstimate(
         flops=2 * ROT * half * both * width, bytes_accessed=4 * both * width, transcendentals=0)
-    shared = (p_own, p_far, near_info, far_info)
-    early = pl.pallas_call(
+    info = (near_info, far_info)
+    early, far_flipped = pl.pallas_call(
         early_kernel,
-        out_shape=jax.ShapeDtypeStruct((ROT, half, both), f32),
-        in_specs=[VMEM] * 5, out_specs=VMEM, scratch_shapes=[turned],
+        out_shape=(jax.ShapeDtypeStruct((ROT, half, both), f32), jax.ShapeDtypeStruct((width, rows), bf16)),
+        in_specs=[VMEM] * 5, out_specs=[VMEM] * 2, scratch_shapes=[turned],
         compiler_params=PARAMS, cost_estimate=cost, name="early",
-    )(gathered, *shared)
+    )(gathered, own_flipped, p_far, *info)
     late, near = pl.pallas_call(
         late_kernel,
         out_shape=(jax.ShapeDtypeStruct((ROT, half, both), f32), jax.ShapeDtypeStruct((1, both), f32)),
         in_specs=[VMEM] * 6, out_specs=[VMEM] * 2, scratch_shapes=[turned],
         compiler_params=PARAMS, cost_estimate=cost, name="late",
-    )(got, *shared, early)
-    other = swap(near, 1)
+    )(got, own_flipped, far_flipped, *info, early)
+    other = swap(near, 1, 1)
+    shared = (p_own, p_far, *info)
 
     send = pl.pallas_call(
         functools.partial(back_kernel, bits, owned, half),
@@ -211,9 +247,9 @@
         compiler_params=PARAMS, cost_estimate=cost, name="back_keep",
     )(early, near, other, *shared)
 
-    for b in range(1, bits):
-        got = swap(send, 1 << b)
-        if b < bits - 1:
+    for r, pair in enumerate(rounds[::-1], 1):
+        got = swap(send, *pair)
+        if r < len(rounds):
             total = keep + got.astype(f32)
             part = total.shape[0] // 2
             keep, send = total[:part], total[part:].astype(bf16)

time: 32.5 us -> 28.9 us (0.89)
  waiting for transfers between devices: 10.7 us -> 8.77 us
  starting transfers between devices: 14.7 us -> 13.7 us
  Pallas kernels: 6.08 us -> 5.54 us
    ppermute x9, waiting for transfers between devices: 10.7 us -> 8.77 us  [swap(): lax.ppermute(x, 'blk', [(i, i ^ (odd if i.bit_count() % 2 else even)) for...]
    ppermute x9, starting transfers between devices: 14.7 us -> 13.7 us  [swap(): lax.ppermute(x, 'blk', [(i, i ^ (odd if i.bit_count() % 2 else even)) for...]
    pallas_call x1, Pallas kernels: 1.92 us -> 1.35 us  [local(): pl.pallas_call(stage_kernel, out_shape=(jax.ShapeDtypeStruct((owned, widt...]
    pallas_call x1 -> x4, Pallas kernels: 0.88 us -> 1.18 us  [the longest x1 0.8 us: local(): pl.pallas_call(early_kernel, out_shape=(jax.ShapeDtypeStruct((ROT, half,...]
  transfers between devices with their start and end apart: 9 -> 9, of which waited for: 7 -> 8; matrix products, arithmetic and copies ran while one was open for 0% -> 0% of each run, Pallas kernels for 11% -> 12%
where the time goes in v4:
time: 28.9 us; the launch traced here: 28.8 us
  starting transfers between devices  13.7 us (47%)
  waiting for transfers between devices  8.77 us (30%)
  Pallas kernels  5.54 us (19%)
  between operations  0.69 us (2%)
    ppermute x9, starting transfers between devices, swap(): lax.ppermute(x, 'blk', [(i, i ^ (odd if i.bit_count() % 2 else even)) for...  13.7 us
    ppermute x9, waiting for transfers between devices, swap(): lax.ppermute(x, 'blk', [(i, i ^ (odd if i.bit_count() % 2 else even)) for...  8.77 us
    pallas_call x1, Pallas kernels, local(): pl.pallas_call(stage_kernel, out_shape=(jax.ShapeDtypeStruct((owned, widt...  1.35 us
    pallas_call x1, Pallas kernels, local(): pl.pallas_call(functools.partial(back_kernel, bits, owned, half), out_sha...  0.86 us
    pallas_call x1, Pallas kernels, local(): pl.pallas_call(functools.partial(back_kernel, bits, owned, 0), out_shape=...  0.86 us
    pallas_call x1, Pallas kernels, local(): pl.pallas_call(early_kernel, out_shape=(jax.ShapeDtypeStruct((ROT, half,...  0.8 us
    pallas_call x1, Pallas kernels, local(): pl.pallas_call(late_kernel, out_shape=(jax.ShapeDtypeStruct((ROT, half, b...  0.64 us
    pallas_call x1, Pallas kernels, local(): pl.pallas_call(last_kernel, out_shape=(jax.ShapeDtypeStruct((owned, width...  0.63 us
  transfers between devices with their start and end apart: 9, of which 8 were waited for; matrix products, arithmetic and copies ran while one was open for 0% of the time, Pallas kernels for 12%

profile of v4, /device:TPU:0, one launch (start us, length us, event | category | flops | bytes accessed | tf_op | source)
XLA Modules:
  0.0 28.8 jit_solution(3712768497164866670)
XLA Ops:
  0.6 0.5 %collective-permute-start.3 = (bf16[128,4608]{1,0:T(8,128)(2,1)}, bf16[128,4608]{1,0:T(8,128)(2,1)S(1)}, u32[]{:S(2)}, u32[]{:S(2)}) collective-permute-start(bf16[128,4608]{1,0:T(8,128)(2,1)} %particles.1), channel_id=1, source_target_pairs={{0,1},{1,0},{2,3},{3,2},{4,5},{5,4},{6,7},{7,6},{8,9},{9,8},{10,11... | collective-permute-start | bytes 3538952 | tf_op jit(solution)/shard_map/ppermute | solution.py:180
  1.1 3.7 %collective-permute-start = (bf16[2,4608]{1,0:T(2,128)(2,1)}, bf16[2,4608]{1,0:T(2,128)(2,1)S(1)}, u32[]{:S(2)}, u32[]{:S(2)}) collective-permute-start(bf16[2,4608]{1,0:T(2,128)(2,1)} %refs.1), channel_id=1, source_target_pairs={{0,9},{1,8},{2,11},{3,10},{4,13},{5,12},{6,15},{7,14},{8,1},{9,0},... | collective-permute-start | bytes 55304 | tf_op jit(solution)/shard_map/ppermute | solution.py:180
  4.9 1.4 %stage.1 = (bf16[2,4608]{1,0:T(2,128)(2,1)S(1)}, f32[3,128]{1,0:T(4,128)S(1)}, bf16[128,4608]{1,0:T(8,128)(2,1)S(1)}) custom-call(bf16[2,4608]{1,0:T(2,128)(2,1)} %refs.1, f32[1,128]{1,0:T(1,128)} %bitcast.4, s32[2,128]{1,0:T(2,128)} %bitcast.3, bf16[128,4608]{1,0:T(8,128)(2,1)} %particles.1), custom_call_target="tpu_custom_call" | custom-call | tf_op jit(solution)/shard_map/stage/pallas_call | solution.py:194
  6.2 0.3 %collective-permute-done.got_ref = bf16[2,4608]{1,0:T(2,128)(2,1)S(1)} collective-permute-done((bf16[2,4608]{1,0:T(2,128)(2,1)}, bf16[2,4608]{1,0:T(2,128)(2,1)S(1)}, u32[]{:S(2)}, u32[]{:S(2)}) %collective-permute-start) | collective-permute-done | bytes 18464 | tf_op jit(solution)/shard_map/ppermute | solution.py:180
  6.6 1.7 %collective-permute-start.1 = (bf16[4,4608]{1,0:T(4,128)(2,1)S(1)}, bf16[4,4608]{1,0:T(4,128)(2,1)S(1)}, u32[]{:S(2)}, u32[]{:S(2)}) collective-permute-start(bf16[4,4608]{1,0:T(4,128)(2,1)S(1)} %join.2.after_ref.held_ref), channel_id=1, source_target_pairs={{0,5},{1,2},{2,1},{3,6},{4,7},{5,0},{6,3},{7,4},{8,11},{9,12},{10,... | collective-permute-start | bytes 110600 | tf_op jit(solution)/shard_map/ppermute | solution.py:180
  8.2 0.0 collective-permute-start.2
  8.3 0.4 %flip.1.rest_0_.own_flipped = bf16[4608,128]{1,0:T(8,128)(2,1)S(1)} custom-call(bf16[4,4608]{1,0:T(4,128)(2,1)S(1)} %join.2.after_ref.held_ref, bf16[128,4608]{1,0:T(8,128)(2,1)S(1)} %get-tuple-element.15.p_ref.own_ref), custom_call_target="tpu_custom_call" | custom-call | tf_op jit(solution)/shard_map/flip/pallas_call | solution.py:209
  8.6 0.8 %collective-permute-done.2.rest_1_.far_info = f32[3,128]{1,0:T(4,128)S(1)} collective-permute-done((f32[3,128]{1,0:T(4,128)S(1)}, f32[3,128]{1,0:T(4,128)S(1)}, u32[]{:S(2)}, u32[]{:S(2)}) %collective-permute-start.2) | collective-permute-done | bytes 1568 | tf_op jit(solution)/shard_map/ppermute | solution.py:180
  9.4 0.6 %collective-permute-done.1.got_ref = bf16[4,4608]{1,0:T(4,128)(2,1)S(1)} collective-permute-done((bf16[4,4608]{1,0:T(4,128)(2,1)S(1)}, bf16[4,4608]{1,0:T(4,128)(2,1)S(1)}, u32[]{:S(2)}, u32[]{:S(2)}) %collective-permute-start.1) | collective-permute-done | bytes 36896 | tf_op jit(solution)/shard_map/ppermute | solution.py:180
  10.0 1.6 %collective-permute-start.4 = (bf16[8,4608]{1,0:T(8,128)(2,1)S(1)}, bf16[8,4608]{1,0:T(8,128)(2,1)S(1)}, u32[]{:S(2)}, u32[]{:S(2)}) collective-permute-start(bf16[8,4608]{1,0:T(8,128)(2,1)S(1)} %join.3.refs_ref), channel_id=1, source_target_pairs={{0,3},{1,4},{2,7},{3,0},{4,1},{5,6},{6,5},{7,2},{8,13},{9,10},{10,... | collective-permute-start | bytes 221192 | tf_op jit(solution)/shard_map/ppermute | solution.py:180
  11.6 0.8 %early.1 = (f32[12,8,256]{2,1,0:T(8,128)S(1)}, bf16[4608,128]{1,0:T(8,128)(2,1)S(1)}) custom-call(bf16[8,4608]{1,0:T(8,128)(2,1)S(1)} %join.3.refs_ref, bf16[4608,128]{1,0:T(8,128)(2,1)S(1)} %flip.1.rest_0_.own_flipped, bf16[128,4608]{1,0:T(8,128)(2,1)S(1)} %collective-permute-done.3.far_ref, f32[3,128]{1,0:T(4,128)S(1)} %get-tuple-element.16.near_info, ...), custom_call_target="tpu_custom_call" | custom-call | flops 226492416 | bytes 4718592 | tf_op jit(solution)/shard_map/early/pallas_call | solution.py:222
  12.4 1.4 %collective-permute-done.4.refs_ref = bf16[8,4608]{1,0:T(8,128)(2,1)S(1)} collective-permute-done((bf16[8,4608]{1,0:T(8,128)(2,1)S(1)}, bf16[8,4608]{1,0:T(8,128)(2,1)S(1)}, u32[]{:S(2)}, u32[]{:S(2)}) %collective-permute-start.4) | collective-permute-done | bytes 73760 | tf_op jit(solution)/shard_map/ppermute | solution.py:180
  13.9 0.6 %late.1 = (f32[12,8,256]{2,1,0:T(8,128)S(1)}, f32[1,256]{1,0:T(1,128)S(1)}) custom-call(bf16[8,4608]{1,0:T(8,128)(2,1)S(1)} %collective-permute-done.4.refs_ref, bf16[4608,128]{1,0:T(8,128)(2,1)S(1)} %flip.1.rest_0_.own_flipped, bf16[4608,128]{1,0:T(8,128)(2,1)S(1)} %get-tuple-element.18.far_flipped, f32[3,128]{1,0:T(4,128)S(1)} %get-tuple-element.16.near_info, ...), custom_call_target="tpu_custom_call" | custom-call | flops 226492416 | bytes 4718592 | tf_op jit(solution)/shard_map/late/pallas_call | solution.py:228
  14.5 0.2 collective-permute-start.5
  14.7 1.0 %collective-permute-done.5.other_ref = f32[1,256]{1,0:T(1,128)S(1)} collective-permute-done((f32[1,256]{1,0:T(1,128)S(1)}, f32[1,256]{1,0:T(1,128)S(1)}, u32[]{:S(2)}, u32[]{:S(2)}) %collective-permute-start.5) | collective-permute-done | bytes 1056 | tf_op jit(solution)/shard_map/ppermute | solution.py:180
  15.7 0.9 %back_send.1 = bf16[8,4736]{1,0:T(8,128)(2,1)S(1)} custom-call(f32[12,8,256]{2,1,0:T(8,128)S(1)} %get-tuple-element.21.logits_ref, f32[1,256]{1,0:T(1,128)S(1)} %get-tuple-element.19.near_ref, f32[1,256]{1,0:T(1,128)S(1)} %collective-permute-done.5.other_ref, bf16[128,4608]{1,0:T(8,128)(2,1)S(1)} %get-tuple-element.15.p_ref.own_ref, ...), custom_call_target="tpu_custom_call" | custom-call | flops 226492416 | bytes 4718592 | tf_op jit(solution)/shard_map/back_send/pallas_call | solution.py:237
  16.6 1.6 %collective-permute-start.6 = (bf16[8,4736]{1,0:T(8,128)(2,1)S(1)}, bf16[8,4736]{1,0:T(8,128)(2,1)S(1)}, u32[]{:S(2)}, u32[]{:S(2)}) collective-permute-start(bf16[8,4736]{1,0:T(8,128)(2,1)S(1)} %back_send.1), channel_id=1, source_target_pairs={{0,3},{1,4},{2,7},{3,0},{4,1},{5,6},{6,5},{7,2},{8,13},{9,10},{10,... | collective-permute-start | bytes 227336 | tf_op jit(solution)/shard_map/ppermute | solution.py:180
  18.2 0.9 %back_keep.1 = (f32[8,4736]{1,0:T(8,128)S(1)}, f32[1,128]{1,0:T(1,128)}) custom-call(f32[12,8,256]{2,1,0:T(8,128)S(1)} %get-tuple-element.17.early_ref.logits_ref, f32[1,256]{1,0:T(1,128)S(1)} %get-tuple-element.19.near_ref, f32[1,256]{1,0:T(1,128)S(1)} %collective-permute-done.5.other_ref, bf16[128,4608]{1,0:T(8,128)(2,1)S(1)} %get-tuple-element.15.p_ref.own_ref, ...), custom_call_target="tpu_custom_call" | custom-call | flops 226492416 | bytes 4718592 | tf_op jit(solution)/shard_map/back_keep/pallas_call | solution.py:243
  19.0 1.4 %collective-permute-done.6 = bf16[8,4736]{1,0:T(8,128)(2,1)S(1)} collective-permute-done((bf16[8,4736]{1,0:T(8,128)(2,1)S(1)}, bf16[8,4736]{1,0:T(8,128)(2,1)S(1)}, u32[]{:S(2)}, u32[]{:S(2)}) %collective-permute-start.6) | collective-permute-done | bytes 75808 | tf_op jit(solution)/shard_map/ppermute | solution.py:180
  20.5 1.7 %collective-permute-start.7 = (bf16[4,4736]{1,0:T(4,128)(2,1)S(1)}, bf16[4,4736]{1,0:T(4,128)(2,1)S(1)}, u32[]{:S(2)}, u32[]{:S(2)}) collective-permute-start(bf16[4,4736]{1,0:T(4,128)(2,1)S(1)} %slice.25), channel_id=1, source_target_pairs={{0,5},{1,2},{2,1},{3,6},{4,7},{5,0},{6,3},{7,4},{8,11},{9,12},{10,... | collective-permute-start | bytes 113672 | tf_op jit(solution)/shard_map/ppermute | solution.py:180
  22.1 1.8 %collective-permute-done.7 = bf16[4,4736]{1,0:T(4,128)(2,1)S(1)} collective-permute-done((bf16[4,4736]{1,0:T(4,128)(2,1)S(1)}, bf16[4,4736]{1,0:T(4,128)(2,1)S(1)}, u32[]{:S(2)}, u32[]{:S(2)}) %collective-permute-start.7) | collective-permute-done | bytes 37920 | tf_op jit(solution)/shard_map/ppermute | solution.py:180
  24.0 2.7 %collective-permute-start.8 = (bf16[2,4736]{1,0:T(2,128)(2,1)S(1)}, bf16[2,4736]{1,0:T(2,128)(2,1)S(1)}, u32[]{:S(2)}, u32[]{:S(2)}) collective-permute-start(bf16[2,4736]{1,0:T(2,128)(2,1)S(1)} %slice.26), channel_id=1, source_target_pairs={{0,9},{1,8},{2,11},{3,10},{4,13},{5,12},{6,15},{7,14},{8,1},{9,0},... | collective-permute-start | bytes 56840 | tf_op jit(solution)/shard_map/ppermute | solution.py:180
  26.7 1.5 %collective-permute-done.8.got_ref = bf16[2,4736]{1,0:T(2,128)(2,1)S(1)} collective-permute-done((bf16[2,4736]{1,0:T(2,128)(2,1)S(1)}, bf16[2,4736]{1,0:T(2,128)(2,1)S(1)}, u32[]{:S(2)}, u32[]{:S(2)}) %collective-permute-start.8) | collective-permute-done | bytes 18976 | tf_op jit(solution)/shard_map/ppermute | solution.py:180
  28.1 0.6 %last.1 = (f32[2,4608]{1,0:T(2,128)}, f32[2]{0:T(128)}) custom-call(f32[2,4736]{1,0:T(2,128)S(1)} %slice.20.keep_ref, bf16[2,4736]{1,0:T(2,128)(2,1)S(1)} %collective-permute-done.8.got_ref), custom_call_target="tpu_custom_call" | custom-call | tf_op jit(solution)/shard_map/last/pallas_call | solution.py:256
  (8 shorter events, 0.1 us)
Async XLA Ops:
  0.6 11.0 %collective-permute-start.3 = (bf16[128,4608]{1,0:T(8,128)(2,1)}, bf16[128,4608]{1,0:T(8,128)(2,1)S(1)}, u32[]{:S(2)}, u32[]{:S(2)}) collective-permute-start(bf16[128,4608]{1,0:T(8,128)(2,1)} %particles.1), channel_id=1, source_target_pairs={{0,1},{1,0},{2,3},{3,2},{4,5},{5,4},{6,7},{7,6},{8,9},{9,8},{10,11... | collective-permute-start | bytes 3538952 | tf_op jit(solution)/shard_map/ppermute | solution.py:180
  1.1 5.4 %collective-permute-start = (bf16[2,4608]{1,0:T(2,128)(2,1)}, bf16[2,4608]{1,0:T(2,128)(2,1)S(1)}, u32[]{:S(2)}, u32[]{:S(2)}) collective-permute-start(bf16[2,4608]{1,0:T(2,128)(2,1)} %refs.1), channel_id=1, source_target_pairs={{0,9},{1,8},{2,11},{3,10},{4,13},{5,12},{6,15},{7,14},{8,1},{9,0},... | collective-permute-start | bytes 55304 | tf_op jit(solution)/shard_map/ppermute | solution.py:180
  6.6 3.4 %collective-permute-start.1 = (bf16[4,4608]{1,0:T(4,128)(2,1)S(1)}, bf16[4,4608]{1,0:T(4,128)(2,1)S(1)}, u32[]{:S(2)}, u32[]{:S(2)}) collective-permute-start(bf16[4,4608]{1,0:T(4,128)(2,1)S(1)} %join.2.after_ref.held_ref), channel_id=1, source_target_pairs={{0,5},{1,2},{2,1},{3,6},{4,7},{5,0},{6,3},{7,4},{8,11},{9,12},{10,... | collective-permute-start | bytes 110600 | tf_op jit(solution)/shard_map/ppermute | solution.py:180
  8.2 1.2 %collective-permute-start.2 = (f32[3,128]{1,0:T(4,128)S(1)}, f32[3,128]{1,0:T(4,128)S(1)}, u32[]{:S(2)}, u32[]{:S(2)}) collective-permute-start(f32[3,128]{1,0:T(4,128)S(1)} %get-tuple-element.16.near_info), channel_id=1, source_target_pairs={{0,1},{1,0},{2,3},{3,2},{4,5},{5,4},{6,7},{7,6},{8,9},{9,8},{10,11... | collective-permute-start | bytes 4616 | tf_op jit(solution)/shard_map/ppermute | solution.py:180
  10.0 3.8 %collective-permute-start.4 = (bf16[8,4608]{1,0:T(8,128)(2,1)S(1)}, bf16[8,4608]{1,0:T(8,128)(2,1)S(1)}, u32[]{:S(2)}, u32[]{:S(2)}) collective-permute-start(bf16[8,4608]{1,0:T(8,128)(2,1)S(1)} %join.3.refs_ref), channel_id=1, source_target_pairs={{0,3},{1,4},{2,7},{3,0},{4,1},{5,6},{6,5},{7,2},{8,13},{9,10},{10,... | collective-permute-start | bytes 221192 | tf_op jit(solution)/shard_map/ppermute | solution.py:180
  14.5 1.2 %collective-permute-start.5 = (f32[1,256]{1,0:T(1,128)S(1)}, f32[1,256]{1,0:T(1,128)S(1)}, u32[]{:S(2)}, u32[]{:S(2)}) collective-permute-start(f32[1,256]{1,0:T(1,128)S(1)} %get-tuple-element.19.near_ref), channel_id=1, source_target_pairs={{0,1},{1,0},{2,3},{3,2},{4,5},{5,4},{6,7},{7,6},{8,9},{9,8},{10,11... | collective-permute-start | bytes 3080 | tf_op jit(solution)/shard_map/ppermute | solution.py:180
  16.6 3.8 %collective-permute-start.6 = (bf16[8,4736]{1,0:T(8,128)(2,1)S(1)}, bf16[8,4736]{1,0:T(8,128)(2,1)S(1)}, u32[]{:S(2)}, u32[]{:S(2)}) collective-permute-start(bf16[8,4736]{1,0:T(8,128)(2,1)S(1)} %back_send.1), channel_id=1, source_target_pairs={{0,3},{1,4},{2,7},{3,0},{4,1},{5,6},{6,5},{7,2},{8,13},{9,10},{10,... | collective-permute-start | bytes 227336 | tf_op jit(solution)/shard_map/ppermute | solution.py:180
  20.5 3.5 %collective-permute-start.7 = (bf16[4,4736]{1,0:T(4,128)(2,1)S(1)}, bf16[4,4736]{1,0:T(4,128)(2,1)S(1)}, u32[]{:S(2)}, u32[]{:S(2)}) collective-permute-start(bf16[4,4736]{1,0:T(4,128)(2,1)S(1)} %slice.25), channel_id=1, source_target_pairs={{0,5},{1,2},{2,1},{3,6},{4,7},{5,0},{6,3},{7,4},{8,11},{9,12},{10,... | collective-permute-start | bytes 113672 | tf_op jit(solution)/shard_map/ppermute | solution.py:180
  24.0 4.2 %collective-permute-start.8 = (bf16[2,4736]{1,0:T(2,128)(2,1)S(1)}, bf16[2,4736]{1,0:T(2,128)(2,1)S(1)}, u32[]{:S(2)}, u32[]{:S(2)}) collective-permute-start(bf16[2,4736]{1,0:T(2,128)(2,1)S(1)} %slice.26), channel_id=1, source_target_pairs={{0,9},{1,8},{2,11},{3,10},{4,13},{5,12},{6,15},{7,14},{8,1},{9,0},... | collective-permute-start | bytes 56840 | tf_op jit(solution)/shard_map/ppermute | solution.py:180

commit v5 on v4

--- a/solution.py
+++ b/solution.py
@@ -11,6 +11,7 @@
 CYCLES = 12
 ANGLES = 384
 TOPK = 2
+FLIPS = 4
 WIDTH = CYCLES * ANGLES
 LANES = 128
 STEP = ANGLES // ROT
@@ -21,28 +22,36 @@
 PARAMS = pltpu.CompilerParams(vmem_limit_bytes=40 * 1024 * 1024)
 
 
-def stage_kernel(refs, noise, names, particles, refs_ref, packed_ref, p_ref, noise_ref, names_ref, sems):
+def stage_kernel(refs, noise, names, refs_ref, packed_ref, noise_ref, names_ref, sems):
     copies = [
         pltpu.make_async_copy(src, dst, sems.at[i])
-        for i, (src, dst) in enumerate(
-            ((refs, refs_ref), (noise, noise_ref), (names, names_ref), (particles, p_ref)))
+        for i, (src, dst) in enumerate(((refs, refs_ref), (noise, noise_ref), (names, names_ref)))
     ]
     for copy in copies:
         copy.start()
-    for copy in copies[:3]:
+    for copy in copies:
         copy.wait()
     packed_ref[0:1, :] = noise_ref[...]
     packed_ref[1:1 + TOPK, :] = names_ref[...].astype(jnp.float32)
-    copies[3].wait()
-
-
-def flip(p_ref, flipped_ref):
-    for at in range(0, WIDTH, LANES):
+
+
+def flip(p_ref, flipped_ref, start, stop):
+    for at in range(start, stop, LANES):
         flipped_ref[at:at + LANES, :] = p_ref[:, at:at + LANES].T
 
 
-def flip_kernel(after_ref, p_ref, flipped_ref):
-    flip(p_ref, flipped_ref)
+def flip_kernel(after_ref, particles, p_ref, flipped_ref, sems):
+    part = WIDTH // FLIPS
+    copies = [
+        pltpu.make_async_copy(
+            particles.at[:, i * part:(i + 1) * part], p_ref.at[:, i * part:(i + 1) * part], sems.at[i])
+        for i in range(FLIPS)
+    ]
+    for copy in copies:
+        copy.start()
+    for i, copy in enumerate(copies):
+        copy.wait()
+        flip(p_ref, flipped_ref, i * part, (i + 1) * part)
 
 
 def join_kernel(held_ref, got_ref, *rest):
@@ -82,7 +91,7 @@
 
 
 def early_kernel(refs_ref, own_flipped, far_ref, near_info, far_info, logits_ref, far_flipped, turned_ref):
-    flip(far_ref, far_flipped)
+    flip(far_ref, far_flipped, 0, WIDTH)
     logits_ref[...] = score(refs_ref, own_flipped, far_flipped, near_info, far_info, turned_ref)
 
 
@@ -183,33 +192,31 @@
         held = operands[0]
         return pl.pallas_call(
             join_kernel, out_shape=jax.ShapeDtypeStruct((2 * held.shape[0], width), bf16),
-            in_specs=[VMEM] * len(operands), out_specs=VMEM, compiler_params=PARAMS, name="join",
+            in_specs=[VMEM] * len(operands), out_specs=VMEM, compiler_params=PARAMS, cost_estimate=pl.CostEstimate(flops=4000000000, bytes_accessed=12000000, transcendentals=0), name="join",
         )(*operands)
 
     rounds = offsets(bits)
-    got = swap(references, *rounds[0])
     p_far = swap(particles, 1, 1)
     held = [pltpu.with_memory_space_constraint(x, pltpu.HBM)
             for x in (references, inv_noise[None, :], assign.T, particles)]
-    own, near_info, p_own = pl.pallas_call(
+    own, near_info = pl.pallas_call(
         stage_kernel,
-        out_shape=(
-            jax.ShapeDtypeStruct((owned, width), bf16),
-            jax.ShapeDtypeStruct((1 + TOPK, rows), f32),
-            jax.ShapeDtypeStruct((rows, width), bf16),
-        ),
-        in_specs=[HBM] * 4, out_specs=[VMEM] * 3,
+        out_shape=(jax.ShapeDtypeStruct((owned, width), bf16), jax.ShapeDtypeStruct((1 + TOPK, rows), f32)),
+        in_specs=[HBM] * 3, out_specs=[VMEM] * 2,
         scratch_shapes=[
-            pltpu.VMEM((1, rows), f32), pltpu.VMEM((TOPK, rows), jnp.int32), pltpu.SemaphoreType.DMA((4,))],
-        compiler_params=PARAMS, name="stage",
-    )(*held)
+            pltpu.VMEM((1, rows), f32), pltpu.VMEM((TOPK, rows), jnp.int32), pltpu.SemaphoreType.DMA((3,))],
+        compiler_params=PARAMS, cost_estimate=pl.CostEstimate(flops=4000000000, bytes_accessed=12000000, transcendentals=0), name="stage",
+    )(*held[:3])
     far_info = swap(near_info, 1, 1)
 
+    got = swap(references, *rounds[0])
     gathered = join(own, got)
-    own_flipped = pl.pallas_call(
-        flip_kernel, out_shape=jax.ShapeDtypeStruct((width, rows), bf16),
-        in_specs=[VMEM] * 2, out_specs=VMEM, compiler_params=PARAMS, name="flip",
-    )(gathered, p_own)
+    p_own, own_flipped = pl.pallas_call(
+        flip_kernel,
+        out_shape=(jax.ShapeDtypeStruct((rows, width), bf16), jax.ShapeDtypeStruct((width, rows), bf16)),
+        in_specs=[VMEM, HBM], out_specs=[VMEM] * 2, scratch_shapes=[pltpu.SemaphoreType.DMA((FLIPS,))],
+        compiler_params=PARAMS, cost_estimate=pl.CostEstimate(flops=4000000000, bytes_accessed=12000000, transcendentals=0), name="flip",
+    )(gathered, held[3])
     for r, pair in enumerate(rounds[1:], 1):
         got = swap(gathered, *pair)
         if r < len(rounds) - 1:

time: 28.9 us -> 28.9 us (level)
  waiting for transfers between devices: 8.77 us -> 6.92 us
  starting transfers between devices: 13.7 us -> 14.8 us
  Pallas kernels: 5.54 us -> 6.13 us
    ppermute x9, waiting for transfers between devices: 8.77 us -> 6.92 us  [swap(): lax.ppermute(x, 'blk', [(i, i ^ (odd if i.bit_count() % 2 else even)) for...]
    pallas_call x1, Pallas kernels: 0.35 us -> 1.55 us  [local(): pl.pallas_call(flip_kernel, out_shape=(jax.ShapeDtypeStruct((rows, width)...]
    ppermute x9, starting transfers between devices: 13.7 us -> 14.8 us  [swap(): lax.ppermute(x, 'blk', [(i, i ^ (odd if i.bit_count() % 2 else even)) for...]
    pallas_call x1, Pallas kernels: 1.35 us -> 0.75 us  [local(): pl.pallas_call(stage_kernel, out_shape=(jax.ShapeDtypeStruct((owned, widt...]
  transfers between devices with their start and end apart: 9 -> 9, of which waited for: 8 -> 7; matrix products, arithmetic and copies ran while one was open for 0% -> 0% of each run, Pallas kernels for 12% -> 14%
where the time goes in v5:
time: 28.9 us; the launch traced here: 28.7 us
  starting transfers between devices  14.8 us (51%)
  waiting for transfers between devices  6.92 us (24%)
  Pallas kernels  6.13 us (21%)
  between operations  0.7 us (2%)
    ppermute x9, starting transfers between devices, swap(): lax.ppermute(x, 'blk', [(i, i ^ (odd if i.bit_count() % 2 else even)) for...  14.8 us
    ppermute x9, waiting for transfers between devices, swap(): lax.ppermute(x, 'blk', [(i, i ^ (odd if i.bit_count() % 2 else even)) for...  6.92 us
    pallas_call x1, Pallas kernels, local(): pl.pallas_call(flip_kernel, out_shape=(jax.ShapeDtypeStruct((rows, width)...  1.55 us
    pallas_call x1, Pallas kernels, local(): pl.pallas_call(functools.partial(back_kernel, bits, owned, 0), out_shape=...  0.86 us
    pallas_call x1, Pallas kernels, local(): pl.pallas_call(functools.partial(back_kernel, bits, owned, half), out_sha...  0.86 us
    pallas_call x1, Pallas kernels, local(): pl.pallas_call(early_kernel, out_shape=(jax.ShapeDtypeStruct((ROT, half,...  0.8 us
    pallas_call x1, Pallas kernels, local(): pl.pallas_call(stage_kernel, out_shape=(jax.ShapeDtypeStruct((owned, widt...  0.75 us
    pallas_call x1, Pallas kernels, local(): pl.pallas_call(late_kernel, out_shape=(jax.ShapeDtypeStruct((ROT, half, b...  0.64 us
  transfers between devices with their start and end apart: 9, of which 7 were waited for; matrix products, arithmetic and copies ran while one was open for 0% of the time, Pallas kernels for 14%

profile of v5, /device:TPU:0, one launch (start us, length us, event | category | flops | bytes accessed | tf_op | source)
XLA Modules:
  0.0 28.7 jit_solution(2511414440104777250)
XLA Ops:
  0.6 3.5 %collective-permute-start = (bf16[2,4608]{1,0:T(2,128)(2,1)}, bf16[2,4608]{1,0:T(2,128)(2,1)S(1)}, u32[]{:S(2)}, u32[]{:S(2)}) collective-permute-start(bf16[2,4608]{1,0:T(2,128)(2,1)} %refs.1), channel_id=1, source_target_pairs={{0,9},{1,8},{2,11},{3,10},{4,13},{5,12},{6,15},{7,14},{8,1},{9,0},... | collective-permute-start | bytes 55304 | tf_op jit(solution)/shard_map/ppermute | solution.py:189
  4.2 0.7 %collective-permute-start.3 = (bf16[128,4608]{1,0:T(8,128)(2,1)}, bf16[128,4608]{1,0:T(8,128)(2,1)S(1)}, u32[]{:S(2)}, u32[]{:S(2)}) collective-permute-start(bf16[128,4608]{1,0:T(8,128)(2,1)} %particles.1), channel_id=1, source_target_pairs={{0,1},{1,0},{2,3},{3,2},{4,5},{5,4},{6,7},{7,6},{8,9},{9,8},{10,11... | collective-permute-start | bytes 3538952 | tf_op jit(solution)/shard_map/ppermute | solution.py:189
  4.8 0.8 %stage.1 = (bf16[2,4608]{1,0:T(2,128)(2,1)S(1)}, f32[3,128]{1,0:T(4,128)S(1)}) custom-call(bf16[2,4608]{1,0:T(2,128)(2,1)} %refs.1, f32[1,128]{1,0:T(1,128)} %bitcast.4, s32[2,128]{1,0:T(2,128)} %bitcast.3), custom_call_target="tpu_custom_call" | custom-call | flops 4000000000 | bytes 12000000 | tf_op jit(solution)/shard_map/stage/pallas_call | solution.py:202
  5.6 0.1 collective-permute-start.2
  5.7 0.1 collective-permute-done.got_ref
  5.9 1.9 %collective-permute-start.1 = (bf16[4,4608]{1,0:T(4,128)(2,1)S(1)}, bf16[4,4608]{1,0:T(4,128)(2,1)S(1)}, u32[]{:S(2)}, u32[]{:S(2)}) collective-permute-start(bf16[4,4608]{1,0:T(4,128)(2,1)S(1)} %join.2.after_ref.held_ref), channel_id=1, source_target_pairs={{0,5},{1,2},{2,1},{3,6},{4,7},{5,0},{6,3},{7,4},{8,11},{9,12},{10,... | collective-permute-start | bytes 110600 | tf_op jit(solution)/shard_map/ppermute | solution.py:189
  7.8 1.6 %flip.1 = (bf16[128,4608]{1,0:T(8,128)(2,1)S(1)}, bf16[4608,128]{1,0:T(8,128)(2,1)S(1)}) custom-call(bf16[4,4608]{1,0:T(4,128)(2,1)S(1)} %join.2.after_ref.held_ref, bf16[128,4608]{1,0:T(8,128)(2,1)} %particles.1), custom_call_target="tpu_custom_call" | custom-call | flops 4000000000 | bytes 12000000 | tf_op jit(solution)/shard_map/flip/pallas_call | solution.py:214
  9.4 0.0 collective-permute-done.2.rest_1_.far_info
  9.4 0.1 collective-permute-done.1.got_ref
  9.5 1.7 %collective-permute-start.4 = (bf16[8,4608]{1,0:T(8,128)(2,1)S(1)}, bf16[8,4608]{1,0:T(8,128)(2,1)S(1)}, u32[]{:S(2)}, u32[]{:S(2)}) collective-permute-start(bf16[8,4608]{1,0:T(8,128)(2,1)S(1)} %join.3.refs_ref), channel_id=1, source_target_pairs={{0,3},{1,4},{2,7},{3,0},{4,1},{5,6},{6,5},{7,2},{8,13},{9,10},{10,... | collective-permute-start | bytes 221192 | tf_op jit(solution)/shard_map/ppermute | solution.py:189
  11.2 0.8 %early.1 = (f32[12,8,256]{2,1,0:T(8,128)S(1)}, bf16[4608,128]{1,0:T(8,128)(2,1)S(1)}) custom-call(bf16[8,4608]{1,0:T(8,128)(2,1)S(1)} %join.3.refs_ref, bf16[4608,128]{1,0:T(8,128)(2,1)S(1)} %get-tuple-element.16.rest_0_.own_flipped, bf16[128,4608]{1,0:T(8,128)(2,1)S(1)} %collective-permute-done.3.far_ref, f32[3,128]{1,0:T(4,128)S(1)} %get-tuple-element.17.near_info, ...), custom_call_target="tpu_custom_call" | custom-call | flops 226492416 | bytes 4718592 | tf_op jit(solution)/shard_map/early/pallas_call | solution.py:229
  12.0 1.3 %collective-permute-done.4.refs_ref = bf16[8,4608]{1,0:T(8,128)(2,1)S(1)} collective-permute-done((bf16[8,4608]{1,0:T(8,128)(2,1)S(1)}, bf16[8,4608]{1,0:T(8,128)(2,1)S(1)}, u32[]{:S(2)}, u32[]{:S(2)}) %collective-permute-start.4) | collective-permute-done | bytes 73760 | tf_op jit(solution)/shard_map/ppermute | solution.py:189
  13.3 0.6 %late.1 = (f32[12,8,256]{2,1,0:T(8,128)S(1)}, f32[1,256]{1,0:T(1,128)S(1)}) custom-call(bf16[8,4608]{1,0:T(8,128)(2,1)S(1)} %collective-permute-done.4.refs_ref, bf16[4608,128]{1,0:T(8,128)(2,1)S(1)} %get-tuple-element.16.rest_0_.own_flipped, bf16[4608,128]{1,0:T(8,128)(2,1)S(1)} %get-tuple-element.19.far_flipped, f32[3,128]{1,0:T(4,128)S(1)} %get-tuple-element.17.near_info, ...), custom_call_target="tpu_custom_call" | custom-call | flops 226492416 | bytes 4718592 | tf_op jit(solution)/shard_map/late/pallas_call | solution.py:235
  14.0 0.6 %collective-permute-start.5 = (f32[1,256]{1,0:T(1,128)S(1)}, f32[1,256]{1,0:T(1,128)S(1)}, u32[]{:S(2)}, u32[]{:S(2)}) collective-permute-start(f32[1,256]{1,0:T(1,128)S(1)} %get-tuple-element.20.near_ref), channel_id=1, source_target_pairs={{0,1},{1,0},{2,3},{3,2},{4,5},{5,4},{6,7},{7,6},{8,9},{9,8},{10,11... | collective-permute-start | bytes 3080 | tf_op jit(solution)/shard_map/ppermute | solution.py:189
  14.5 0.8 %collective-permute-done.5.other_ref = f32[1,256]{1,0:T(1,128)S(1)} collective-permute-done((f32[1,256]{1,0:T(1,128)S(1)}, f32[1,256]{1,0:T(1,128)S(1)}, u32[]{:S(2)}, u32[]{:S(2)}) %collective-permute-start.5) | collective-permute-done | bytes 1056 | tf_op jit(solution)/shard_map/ppermute | solution.py:189
  15.4 0.9 %back_send.1 = bf16[8,4736]{1,0:T(8,128)(2,1)S(1)} custom-call(f32[12,8,256]{2,1,0:T(8,128)S(1)} %get-tuple-element.23.logits_ref, f32[1,256]{1,0:T(1,128)S(1)} %get-tuple-element.20.near_ref, f32[1,256]{1,0:T(1,128)S(1)} %collective-permute-done.5.other_ref, bf16[128,4608]{1,0:T(8,128)(2,1)S(1)} %get-tuple-element.21.own_ref, ...), custom_call_target="tpu_custom_call" | custom-call | flops 226492416 | bytes 4718592 | tf_op jit(solution)/shard_map/back_send/pallas_call | solution.py:244
  16.2 1.6 %collective-permute-start.6 = (bf16[8,4736]{1,0:T(8,128)(2,1)S(1)}, bf16[8,4736]{1,0:T(8,128)(2,1)S(1)}, u32[]{:S(2)}, u32[]{:S(2)}) collective-permute-start(bf16[8,4736]{1,0:T(8,128)(2,1)S(1)} %back_send.1), channel_id=1, source_target_pairs={{0,3},{1,4},{2,7},{3,0},{4,1},{5,6},{6,5},{7,2},{8,13},{9,10},{10,... | collective-permute-start | bytes 227336 | tf_op jit(solution)/shard_map/ppermute | solution.py:189
  17.8 0.9 %back_keep.1 = (f32[8,4736]{1,0:T(8,128)S(1)}, f32[1,128]{1,0:T(1,128)}) custom-call(f32[12,8,256]{2,1,0:T(8,128)S(1)} %get-tuple-element.18.early_ref.logits_ref, f32[1,256]{1,0:T(1,128)S(1)} %get-tuple-element.20.near_ref, f32[1,256]{1,0:T(1,128)S(1)} %collective-permute-done.5.other_ref, bf16[128,4608]{1,0:T(8,128)(2,1)S(1)} %get-tuple-element.21.own_ref, ...), custom_call_target="tpu_custom_call" | custom-call | flops 226492416 | bytes 4718592 | tf_op jit(solution)/shard_map/back_keep/pallas_call | solution.py:250
  18.7 1.4 %collective-permute-done.6 = bf16[8,4736]{1,0:T(8,128)(2,1)S(1)} collective-permute-done((bf16[8,4736]{1,0:T(8,128)(2,1)S(1)}, bf16[8,4736]{1,0:T(8,128)(2,1)S(1)}, u32[]{:S(2)}, u32[]{:S(2)}) %collective-permute-start.6) | collective-permute-done | bytes 75808 | tf_op jit(solution)/shard_map/ppermute | solution.py:189
  20.1 1.7 %collective-permute-start.7 = (bf16[4,4736]{1,0:T(4,128)(2,1)S(1)}, bf16[4,4736]{1,0:T(4,128)(2,1)S(1)}, u32[]{:S(2)}, u32[]{:S(2)}) collective-permute-start(bf16[4,4736]{1,0:T(4,128)(2,1)S(1)} %slice.25), channel_id=1, source_target_pairs={{0,5},{1,2},{2,1},{3,6},{4,7},{5,0},{6,3},{7,4},{8,11},{9,12},{10,... | collective-permute-start | bytes 113672 | tf_op jit(solution)/shard_map/ppermute | solution.py:189
  21.8 1.8 %collective-permute-done.7 = bf16[4,4736]{1,0:T(4,128)(2,1)S(1)} collective-permute-done((bf16[4,4736]{1,0:T(4,128)(2,1)S(1)}, bf16[4,4736]{1,0:T(4,128)(2,1)S(1)}, u32[]{:S(2)}, u32[]{:S(2)}) %collective-permute-start.7) | collective-permute-done | bytes 37920 | tf_op jit(solution)/shard_map/ppermute | solution.py:189
  23.6 2.9 %collective-permute-start.8 = (bf16[2,4736]{1,0:T(2,128)(2,1)S(1)}, bf16[2,4736]{1,0:T(2,128)(2,1)S(1)}, u32[]{:S(2)}, u32[]{:S(2)}) collective-permute-start(bf16[2,4736]{1,0:T(2,128)(2,1)S(1)} %slice.26), channel_id=1, source_target_pairs={{0,9},{1,8},{2,11},{3,10},{4,13},{5,12},{6,15},{7,14},{8,1},{9,0},... | collective-permute-start | bytes 56840 | tf_op jit(solution)/shard_map/ppermute | solution.py:189
  26.6 1.5 %collective-permute-done.8.got_ref = bf16[2,4736]{1,0:T(2,128)(2,1)S(1)} collective-permute-done((bf16[2,4736]{1,0:T(2,128)(2,1)S(1)}, bf16[2,4736]{1,0:T(2,128)(2,1)S(1)}, u32[]{:S(2)}, u32[]{:S(2)}) %collective-permute-start.8) | collective-permute-done | bytes 18976 | tf_op jit(solution)/shard_map/ppermute | solution.py:189
  28.0 0.6 %last.1 = (f32[2,4608]{1,0:T(2,128)}, f32[2]{0:T(128)}) custom-call(f32[2,4736]{1,0:T(2,128)S(1)} %slice.20.keep_ref, bf16[2,4736]{1,0:T(2,128)(2,1)S(1)} %collective-permute-done.8.got_ref), custom_call_target="tpu_custom_call" | custom-call | tf_op jit(solution)/shard_map/last/pallas_call | solution.py:263
  (8 shorter events, 0.1 us)
Async XLA Ops:
  0.6 5.2 %collective-permute-start = (bf16[2,4608]{1,0:T(2,128)(2,1)}, bf16[2,4608]{1,0:T(2,128)(2,1)S(1)}, u32[]{:S(2)}, u32[]{:S(2)}) collective-permute-start(bf16[2,4608]{1,0:T(2,128)(2,1)} %refs.1), channel_id=1, source_target_pairs={{0,9},{1,8},{2,11},{3,10},{4,13},{5,12},{6,15},{7,14},{8,1},{9,0},... | collective-permute-start | bytes 55304 | tf_op jit(solution)/shard_map/ppermute | solution.py:189
  4.2 7.1 %collective-permute-start.3 = (bf16[128,4608]{1,0:T(8,128)(2,1)}, bf16[128,4608]{1,0:T(8,128)(2,1)S(1)}, u32[]{:S(2)}, u32[]{:S(2)}) collective-permute-start(bf16[128,4608]{1,0:T(8,128)(2,1)} %particles.1), channel_id=1, source_target_pairs={{0,1},{1,0},{2,3},{3,2},{4,5},{5,4},{6,7},{7,6},{8,9},{9,8},{10,11... | collective-permute-start | bytes 3538952 | tf_op jit(solution)/shard_map/ppermute | solution.py:189
  5.6 3.8 %collective-permute-start.2 = (f32[3,128]{1,0:T(4,128)S(1)}, f32[3,128]{1,0:T(4,128)S(1)}, u32[]{:S(2)}, u32[]{:S(2)}) collective-permute-start(f32[3,128]{1,0:T(4,128)S(1)} %get-tuple-element.17.near_info), channel_id=1, source_target_pairs={{0,1},{1,0},{2,3},{3,2},{4,5},{5,4},{6,7},{7,6},{8,9},{9,8},{10,11... | collective-permute-start | bytes 4616 | tf_op jit(solution)/shard_map/ppermute | solution.py:189
  5.9 3.6 %collective-permute-start.1 = (bf16[4,4608]{1,0:T(4,128)(2,1)S(1)}, bf16[4,4608]{1,0:T(4,128)(2,1)S(1)}, u32[]{:S(2)}, u32[]{:S(2)}) collective-permute-start(bf16[4,4608]{1,0:T(4,128)(2,1)S(1)} %join.2.after_ref.held_ref), channel_id=1, source_target_pairs={{0,5},{1,2},{2,1},{3,6},{4,7},{5,0},{6,3},{7,4},{8,11},{9,12},{10,... | collective-permute-start | bytes 110600 | tf_op jit(solution)/shard_map/ppermute | solution.py:189
  9.5 3.8 %collective-permute-start.4 = (bf16[8,4608]{1,0:T(8,128)(2,1)S(1)}, bf16[8,4608]{1,0:T(8,128)(2,1)S(1)}, u32[]{:S(2)}, u32[]{:S(2)}) collective-permute-start(bf16[8,4608]{1,0:T(8,128)(2,1)S(1)} %join.3.refs_ref), channel_id=1, source_target_pairs={{0,3},{1,4},{2,7},{3,0},{4,1},{5,6},{6,5},{7,2},{8,13},{9,10},{10,... | collective-permute-start | bytes 221192 | tf_op jit(solution)/shard_map/ppermute | solution.py:189
  14.0 1.4 %collective-permute-start.5 = (f32[1,256]{1,0:T(1,128)S(1)}, f32[1,256]{1,0:T(1,128)S(1)}, u32[]{:S(2)}, u32[]{:S(2)}) collective-permute-start(f32[1,256]{1,0:T(1,128)S(1)} %get-tuple-element.20.near_ref), channel_id=1, source_target_pairs={{0,1},{1,0},{2,3},{3,2},{4,5},{5,4},{6,7},{7,6},{8,9},{9,8},{10,11... | collective-permute-start | bytes 3080 | tf_op jit(solution)/shard_map/ppermute | solution.py:189
  16.2 3.8 %collective-permute-start.6 = (bf16[8,4736]{1,0:T(8,128)(2,1)S(1)}, bf16[8,4736]{1,0:T(8,128)(2,1)S(1)}, u32[]{:S(2)}, u32[]{:S(2)}) collective-permute-start(bf16[8,4736]{1,0:T(8,128)(2,1)S(1)} %back_send.1), channel_id=1, source_target_pairs={{0,3},{1,4},{2,7},{3,0},{4,1},{5,6},{6,5},{7,2},{8,13},{9,10},{10,... | collective-permute-start | bytes 227336 | tf_op jit(solution)/shard_map/ppermute | solution.py:189
  20.1 3.5 %collective-permute-start.7 = (bf16[4,4736]{1,0:T(4,128)(2,1)S(1)}, bf16[4,4736]{1,0:T(4,128)(2,1)S(1)}, u32[]{:S(2)}, u32[]{:S(2)}) collective-permute-start(bf16[4,4736]{1,0:T(4,128)(2,1)S(1)} %slice.25), channel_id=1, source_target_pairs={{0,5},{1,2},{2,1},{3,6},{4,7},{5,0},{6,3},{7,4},{8,11},{9,12},{10,... | collective-permute-start | bytes 113672 | tf_op jit(solution)/shard_map/ppermute | solution.py:189
  23.6 4.4 %collective-permute-start.8 = (bf16[2,4736]{1,0:T(2,128)(2,1)S(1)}, bf16[2,4736]{1,0:T(2,128)(2,1)S(1)}, u32[]{:S(2)}, u32[]{:S(2)}) collective-permute-start(bf16[2,4736]{1,0:T(2,128)(2,1)S(1)} %slice.26), channel_id=1, source_target_pairs={{0,9},{1,8},{2,11},{3,10},{4,13},{5,12},{6,15},{7,14},{8,1},{9,0},... | collective-permute-start | bytes 56840 | tf_op jit(solution)/shard_map/ppermute | solution.py:189

commit v6 on v5

--- a/solution.py
+++ b/solution.py
@@ -155,9 +155,9 @@
                     block = piece if block is None else block + piece
                 blocks.append(block)
             turned = jnp.concatenate(blocks, axis=1)
-            summed = turned[(FINE - 1) * classes:]
-            for s in range(FINE - 2, -1, -1):
-                summed = turned[s * classes:(s + 1) * classes] + pltpu.roll(summed, ANGLES - STEP, 1)
+            summed = turned[:classes]
+            for s in range(1, FINE):
+                summed = summed + pltpu.roll(turned[s * classes:(s + 1) * classes], ANGLES - s * STEP, 1)
             sums_ref[:, (c + d) * ANGLES:(c + d + 1) * ANGLES] = summed.astype(sums_ref.dtype)
 
 

time: 28.9 us -> 28.8 us (level)
  waiting for transfers between devices: 6.92 us -> 6.61 us
    ppermute x9, waiting for transfers between devices: 6.92 us -> 6.61 us  [swap(): lax.ppermute(x, 'blk', [(i, i ^ (odd if i.bit_count() % 2 else even)) for...]
    pallas_call x1, Pallas kernels: 0.86 us -> 1.16 us  [local(): pl.pallas_call(functools.partial(back_kernel, bits, owned, 0), out_shape=...]
  transfers between devices with their start and end apart: 9 -> 9, of which waited for: 7 -> 7; matrix products, arithmetic and copies ran while one was open for 0% -> 0% of each run, Pallas kernels for 14% -> 15%
where the time goes in v6:
time: 28.8 us; the launch traced here: 28.6 us
  starting transfers between devices  14.9 us (52%)
  waiting for transfers between devices  6.61 us (23%)
  Pallas kernels  6.28 us (22%)
  between operations  0.71 us (2%)
    ppermute x9, starting transfers between devices, swap(): lax.ppermute(x, 'blk', [(i, i ^ (odd if i.bit_count() % 2 else even)) for...  14.9 us
    ppermute x9, waiting for transfers between devices, swap(): lax.ppermute(x, 'blk', [(i, i ^ (odd if i.bit_count() % 2 else even)) for...  6.61 us
    pallas_call x1, Pallas kernels, local(): pl.pallas_call(flip_kernel, out_shape=(jax.ShapeDtypeStruct((rows, width)...  1.55 us
    pallas_call x1, Pallas kernels, local(): pl.pallas_call(functools.partial(back_kernel, bits, owned, 0), out_shape=...  1.16 us
    pallas_call x1, Pallas kernels, local(): pl.pallas_call(early_kernel, out_shape=(jax.ShapeDtypeStruct((ROT, half,...  0.8 us
    pallas_call x1, Pallas kernels, local(): pl.pallas_call(stage_kernel, out_shape=(jax.ShapeDtypeStruct((owned, widt...  0.75 us
    pallas_call x1, Pallas kernels, local(): pl.pallas_call(functools.partial(back_kernel, bits, owned, half), out_sha...  0.71 us
    pallas_call x1, Pallas kernels, local(): pl.pallas_call(late_kernel, out_shape=(jax.ShapeDtypeStruct((ROT, half, b...  0.64 us
  transfers between devices with their start and end apart: 9, of which 7 were waited for; matrix products, arithmetic and copies ran while one was open for 0% of the time, Pallas kernels for 15%

profile of v6, /device:TPU:0, one launch (start us, length us, event | category | flops | bytes accessed | tf_op | source)
XLA Modules:
  0.0 28.6 jit_solution(5816766409570068835)
XLA Ops:
  0.6 3.5 %collective-permute-start = (bf16[2,4608]{1,0:T(2,128)(2,1)}, bf16[2,4608]{1,0:T(2,128)(2,1)S(1)}, u32[]{:S(2)}, u32[]{:S(2)}) collective-permute-start(bf16[2,4608]{1,0:T(2,128)(2,1)} %refs.1), channel_id=1, source_target_pairs={{0,9},{1,8},{2,11},{3,10},{4,13},{5,12},{6,15},{7,14},{8,1},{9,0},... | collective-permute-start | bytes 55304 | tf_op jit(solution)/shard_map/ppermute | solution.py:189
  4.2 0.7 %collective-permute-start.3 = (bf16[128,4608]{1,0:T(8,128)(2,1)}, bf16[128,4608]{1,0:T(8,128)(2,1)S(1)}, u32[]{:S(2)}, u32[]{:S(2)}) collective-permute-start(bf16[128,4608]{1,0:T(8,128)(2,1)} %particles.1), channel_id=1, source_target_pairs={{0,1},{1,0},{2,3},{3,2},{4,5},{5,4},{6,7},{7,6},{8,9},{9,8},{10,11... | collective-permute-start | bytes 3538952 | tf_op jit(solution)/shard_map/ppermute | solution.py:189
  4.8 0.8 %stage.1 = (bf16[2,4608]{1,0:T(2,128)(2,1)S(1)}, f32[3,128]{1,0:T(4,128)S(1)}) custom-call(bf16[2,4608]{1,0:T(2,128)(2,1)} %refs.1, f32[1,128]{1,0:T(1,128)} %bitcast.4, s32[2,128]{1,0:T(2,128)} %bitcast.3), custom_call_target="tpu_custom_call" | custom-call | flops 4000000000 | bytes 12000000 | tf_op jit(solution)/shard_map/stage/pallas_call | solution.py:202
  5.6 0.1 collective-permute-start.2
  5.7 0.1 collective-permute-done.got_ref
  5.9 1.9 %collective-permute-start.1 = (bf16[4,4608]{1,0:T(4,128)(2,1)S(1)}, bf16[4,4608]{1,0:T(4,128)(2,1)S(1)}, u32[]{:S(2)}, u32[]{:S(2)}) collective-permute-start(bf16[4,4608]{1,0:T(4,128)(2,1)S(1)} %join.2.after_ref.held_ref), channel_id=1, source_target_pairs={{0,5},{1,2},{2,1},{3,6},{4,7},{5,0},{6,3},{7,4},{8,11},{9,12},{10,... | collective-permute-start | bytes 110600 | tf_op jit(solution)/shard_map/ppermute | solution.py:189
  7.8 1.6 %flip.1 = (bf16[128,4608]{1,0:T(8,128)(2,1)S(1)}, bf16[4608,128]{1,0:T(8,128)(2,1)S(1)}) custom-call(bf16[4,4608]{1,0:T(4,128)(2,1)S(1)} %join.2.after_ref.held_ref, bf16[128,4608]{1,0:T(8,128)(2,1)} %particles.1), custom_call_target="tpu_custom_call" | custom-call | flops 4000000000 | bytes 12000000 | tf_op jit(solution)/shard_map/flip/pallas_call | solution.py:214
  9.4 0.0 collective-permute-done.2.rest_1_.far_info
  9.4 0.1 collective-permute-done.1.got_ref
  9.5 1.7 %collective-permute-start.4 = (bf16[8,4608]{1,0:T(8,128)(2,1)S(1)}, bf16[8,4608]{1,0:T(8,128)(2,1)S(1)}, u32[]{:S(2)}, u32[]{:S(2)}) collective-permute-start(bf16[8,4608]{1,0:T(8,128)(2,1)S(1)} %join.3.refs_ref), channel_id=1, source_target_pairs={{0,3},{1,4},{2,7},{3,0},{4,1},{5,6},{6,5},{7,2},{8,13},{9,10},{10,... | collective-permute-start | bytes 221192 | tf_op jit(solution)/shard_map/ppermute | solution.py:189
  11.2 0.8 %early.1 = (f32[12,8,256]{2,1,0:T(8,128)S(1)}, bf16[4608,128]{1,0:T(8,128)(2,1)S(1)}) custom-call(bf16[8,4608]{1,0:T(8,128)(2,1)S(1)} %join.3.refs_ref, bf16[4608,128]{1,0:T(8,128)(2,1)S(1)} %get-tuple-element.16.rest_0_.own_flipped, bf16[128,4608]{1,0:T(8,128)(2,1)S(1)} %collective-permute-done.3.far_ref, f32[3,128]{1,0:T(4,128)S(1)} %get-tuple-element.17.near_info, ...), custom_call_target="tpu_custom_call" | custom-call | flops 226492416 | bytes 4718592 | tf_op jit(solution)/shard_map/early/pallas_call | solution.py:229
  12.0 1.3 %collective-permute-done.4.refs_ref = bf16[8,4608]{1,0:T(8,128)(2,1)S(1)} collective-permute-done((bf16[8,4608]{1,0:T(8,128)(2,1)S(1)}, bf16[8,4608]{1,0:T(8,128)(2,1)S(1)}, u32[]{:S(2)}, u32[]{:S(2)}) %collective-permute-start.4) | collective-permute-done | bytes 73760 | tf_op jit(solution)/shard_map/ppermute | solution.py:189
  13.3 0.6 %late.1 = (f32[12,8,256]{2,1,0:T(8,128)S(1)}, f32[1,256]{1,0:T(1,128)S(1)}) custom-call(bf16[8,4608]{1,0:T(8,128)(2,1)S(1)} %collective-permute-done.4.refs_ref, bf16[4608,128]{1,0:T(8,128)(2,1)S(1)} %get-tuple-element.16.rest_0_.own_flipped, bf16[4608,128]{1,0:T(8,128)(2,1)S(1)} %get-tuple-element.19.far_flipped, f32[3,128]{1,0:T(4,128)S(1)} %get-tuple-element.17.near_info, ...), custom_call_target="tpu_custom_call" | custom-call | flops 226492416 | bytes 4718592 | tf_op jit(solution)/shard_map/late/pallas_call | solution.py:235
  14.0 0.6 %collective-permute-start.5 = (f32[1,256]{1,0:T(1,128)S(1)}, f32[1,256]{1,0:T(1,128)S(1)}, u32[]{:S(2)}, u32[]{:S(2)}) collective-permute-start(f32[1,256]{1,0:T(1,128)S(1)} %get-tuple-element.20.near_ref), channel_id=1, source_target_pairs={{0,1},{1,0},{2,3},{3,2},{4,5},{5,4},{6,7},{7,6},{8,9},{9,8},{10,11... | collective-permute-start | bytes 3080 | tf_op jit(solution)/shard_map/ppermute | solution.py:189
  14.5 0.8 %collective-permute-done.5.other_ref = f32[1,256]{1,0:T(1,128)S(1)} collective-permute-done((f32[1,256]{1,0:T(1,128)S(1)}, f32[1,256]{1,0:T(1,128)S(1)}, u32[]{:S(2)}, u32[]{:S(2)}) %collective-permute-start.5) | collective-permute-done | bytes 1056 | tf_op jit(solution)/shard_map/ppermute | solution.py:189
  15.4 0.7 %back_send.1 = bf16[8,4736]{1,0:T(8,128)(2,1)S(1)} custom-call(f32[12,8,256]{2,1,0:T(8,128)S(1)} %get-tuple-element.23.logits_ref, f32[1,256]{1,0:T(1,128)S(1)} %get-tuple-element.20.near_ref, f32[1,256]{1,0:T(1,128)S(1)} %collective-permute-done.5.other_ref, bf16[128,4608]{1,0:T(8,128)(2,1)S(1)} %get-tuple-element.21.own_ref, ...), custom_call_target="tpu_custom_call" | custom-call | flops 226492416 | bytes 4718592 | tf_op jit(solution)/shard_map/back_send/pallas_call | solution.py:244
  16.1 1.6 %collective-permute-start.6 = (bf16[8,4736]{1,0:T(8,128)(2,1)S(1)}, bf16[8,4736]{1,0:T(8,128)(2,1)S(1)}, u32[]{:S(2)}, u32[]{:S(2)}) collective-permute-start(bf16[8,4736]{1,0:T(8,128)(2,1)S(1)} %back_send.1), channel_id=1, source_target_pairs={{0,3},{1,4},{2,7},{3,0},{4,1},{5,6},{6,5},{7,2},{8,13},{9,10},{10,... | collective-permute-start | bytes 227336 | tf_op jit(solution)/shard_map/ppermute | solution.py:189
  17.7 1.2 %back_keep.1 = (f32[8,4736]{1,0:T(8,128)S(1)}, f32[1,128]{1,0:T(1,128)}) custom-call(f32[12,8,256]{2,1,0:T(8,128)S(1)} %get-tuple-element.18.early_ref.logits_ref, f32[1,256]{1,0:T(1,128)S(1)} %get-tuple-element.20.near_ref, f32[1,256]{1,0:T(1,128)S(1)} %collective-permute-done.5.other_ref, bf16[128,4608]{1,0:T(8,128)(2,1)S(1)} %get-tuple-element.21.own_ref, ...), custom_call_target="tpu_custom_call" | custom-call | flops 226492416 | bytes 4718592 | tf_op jit(solution)/shard_map/back_keep/pallas_call | solution.py:250
  18.9 1.1 %collective-permute-done.6 = bf16[8,4736]{1,0:T(8,128)(2,1)S(1)} collective-permute-done((bf16[8,4736]{1,0:T(8,128)(2,1)S(1)}, bf16[8,4736]{1,0:T(8,128)(2,1)S(1)}, u32[]{:S(2)}, u32[]{:S(2)}) %collective-permute-start.6) | collective-permute-done | bytes 75808 | tf_op jit(solution)/shard_map/ppermute | solution.py:189
  20.0 1.7 %collective-permute-start.7 = (bf16[4,4736]{1,0:T(4,128)(2,1)S(1)}, bf16[4,4736]{1,0:T(4,128)(2,1)S(1)}, u32[]{:S(2)}, u32[]{:S(2)}) collective-permute-start(bf16[4,4736]{1,0:T(4,128)(2,1)S(1)} %slice.25), channel_id=1, source_target_pairs={{0,5},{1,2},{2,1},{3,6},{4,7},{5,0},{6,3},{7,4},{8,11},{9,12},{10,... | collective-permute-start | bytes 113672 | tf_op jit(solution)/shard_map/ppermute | solution.py:189
  21.7 1.8 %collective-permute-done.7 = bf16[4,4736]{1,0:T(4,128)(2,1)S(1)} collective-permute-done((bf16[4,4736]{1,0:T(4,128)(2,1)S(1)}, bf16[4,4736]{1,0:T(4,128)(2,1)S(1)}, u32[]{:S(2)}, u32[]{:S(2)}) %collective-permute-start.7) | collective-permute-done | bytes 37920 | tf_op jit(solution)/shard_map/ppermute | solution.py:189
  23.5 3.0 %collective-permute-start.8 = (bf16[2,4736]{1,0:T(2,128)(2,1)S(1)}, bf16[2,4736]{1,0:T(2,128)(2,1)S(1)}, u32[]{:S(2)}, u32[]{:S(2)}) collective-permute-start(bf16[2,4736]{1,0:T(2,128)(2,1)S(1)} %slice.26), channel_id=1, source_target_pairs={{0,9},{1,8},{2,11},{3,10},{4,13},{5,12},{6,15},{7,14},{8,1},{9,0},... | collective-permute-start | bytes 56840 | tf_op jit(solution)/shard_map/ppermute | solution.py:189
  26.5 1.5 %collective-permute-done.8.got_ref = bf16[2,4736]{1,0:T(2,128)(2,1)S(1)} collective-permute-done((bf16[2,4736]{1,0:T(2,128)(2,1)S(1)}, bf16[2,4736]{1,0:T(2,128)(2,1)S(1)}, u32[]{:S(2)}, u32[]{:S(2)}) %collective-permute-start.8) | collective-permute-done | bytes 18976 | tf_op jit(solution)/shard_map/ppermute | solution.py:189
  27.9 0.6 %last.1 = (f32[2,4608]{1,0:T(2,128)}, f32[2]{0:T(128)}) custom-call(f32[2,4736]{1,0:T(2,128)S(1)} %slice.20.keep_ref, bf16[2,4736]{1,0:T(2,128)(2,1)S(1)} %collective-permute-done.8.got_ref), custom_call_target="tpu_custom_call" | custom-call | tf_op jit(solution)/shard_map/last/pallas_call | solution.py:263
  (8 shorter events, 0.1 us)
Async XLA Ops:
  0.6 5.2 %collective-permute-start = (bf16[2,4608]{1,0:T(2,128)(2,1)}, bf16[2,4608]{1,0:T(2,128)(2,1)S(1)}, u32[]{:S(2)}, u32[]{:S(2)}) collective-permute-start(bf16[2,4608]{1,0:T(2,128)(2,1)} %refs.1), channel_id=1, source_target_pairs={{0,9},{1,8},{2,11},{3,10},{4,13},{5,12},{6,15},{7,14},{8,1},{9,0},... | collective-permute-start | bytes 55304 | tf_op jit(solution)/shard_map/ppermute | solution.py:189
  4.2 7.1 %collective-permute-start.3 = (bf16[128,4608]{1,0:T(8,128)(2,1)}, bf16[128,4608]{1,0:T(8,128)(2,1)S(1)}, u32[]{:S(2)}, u32[]{:S(2)}) collective-permute-start(bf16[128,4608]{1,0:T(8,128)(2,1)} %particles.1), channel_id=1, source_target_pairs={{0,1},{1,0},{2,3},{3,2},{4,5},{5,4},{6,7},{7,6},{8,9},{9,8},{10,11... | collective-permute-start | bytes 3538952 | tf_op jit(solution)/shard_map/ppermute | solution.py:189
  5.6 3.8 %collective-permute-start.2 = (f32[3,128]{1,0:T(4,128)S(1)}, f32[3,128]{1,0:T(4,128)S(1)}, u32[]{:S(2)}, u32[]{:S(2)}) collective-permute-start(f32[3,128]{1,0:T(4,128)S(1)} %get-tuple-element.17.near_info), channel_id=1, source_target_pairs={{0,1},{1,0},{2,3},{3,2},{4,5},{5,4},{6,7},{7,6},{8,9},{9,8},{10,11... | collective-permute-start | bytes 4616 | tf_op jit(solution)/shard_map/ppermute | solution.py:189
  5.9 3.6 %collective-permute-start.1 = (bf16[4,4608]{1,0:T(4,128)(2,1)S(1)}, bf16[4,4608]{1,0:T(4,128)(2,1)S(1)}, u32[]{:S(2)}, u32[]{:S(2)}) collective-permute-start(bf16[4,4608]{1,0:T(4,128)(2,1)S(1)} %join.2.after_ref.held_ref), channel_id=1, source_target_pairs={{0,5},{1,2},{2,1},{3,6},{4,7},{5,0},{6,3},{7,4},{8,11},{9,12},{10,... | collective-permute-start | bytes 110600 | tf_op jit(solution)/shard_map/ppermute | solution.py:189
  9.5 3.8 %collective-permute-start.4 = (bf16[8,4608]{1,0:T(8,128)(2,1)S(1)}, bf16[8,4608]{1,0:T(8,128)(2,1)S(1)}, u32[]{:S(2)}, u32[]{:S(2)}) collective-permute-start(bf16[8,4608]{1,0:T(8,128)(2,1)S(1)} %join.3.refs_ref), channel_id=1, source_target_pairs={{0,3},{1,4},{2,7},{3,0},{4,1},{5,6},{6,5},{7,2},{8,13},{9,10},{10,... | collective-permute-start | bytes 221192 | tf_op jit(solution)/shard_map/ppermute | solution.py:189
  14.0 1.4 %collective-permute-start.5 = (f32[1,256]{1,0:T(1,128)S(1)}, f32[1,256]{1,0:T(1,128)S(1)}, u32[]{:S(2)}, u32[]{:S(2)}) collective-permute-start(f32[1,256]{1,0:T(1,128)S(1)} %get-tuple-element.20.near_ref), channel_id=1, source_target_pairs={{0,1},{1,0},{2,3},{3,2},{4,5},{5,4},{6,7},{7,6},{8,9},{9,8},{10,11... | collective-permute-start | bytes 3080 | tf_op jit(solution)/shard_map/ppermute | solution.py:189
  16.1 3.9 %collective-permute-start.6 = (bf16[8,4736]{1,0:T(8,128)(2,1)S(1)}, bf16[8,4736]{1,0:T(8,128)(2,1)S(1)}, u32[]{:S(2)}, u32[]{:S(2)}) collective-permute-start(bf16[8,4736]{1,0:T(8,128)(2,1)S(1)} %back_send.1), channel_id=1, source_target_pairs={{0,3},{1,4},{2,7},{3,0},{4,1},{5,6},{6,5},{7,2},{8,13},{9,10},{10,... | collective-permute-start | bytes 227336 | tf_op jit(solution)/shard_map/ppermute | solution.py:189
  20.0 3.5 %collective-permute-start.7 = (bf16[4,4736]{1,0:T(4,128)(2,1)S(1)}, bf16[4,4736]{1,0:T(4,128)(2,1)S(1)}, u32[]{:S(2)}, u32[]{:S(2)}) collective-permute-start(bf16[4,4736]{1,0:T(4,128)(2,1)S(1)} %slice.25), channel_id=1, source_target_pairs={{0,5},{1,2},{2,1},{3,6},{4,7},{5,0},{6,3},{7,4},{8,11},{9,12},{10,... | collective-permute-start | bytes 113672 | tf_op jit(solution)/shard_map/ppermute | solution.py:189
  23.5 4.4 %collective-permute-start.8 = (bf16[2,4736]{1,0:T(2,128)(2,1)S(1)}, bf16[2,4736]{1,0:T(2,128)(2,1)S(1)}, u32[]{:S(2)}, u32[]{:S(2)}) collective-permute-start(bf16[2,4736]{1,0:T(2,128)(2,1)S(1)} %slice.26), channel_id=1, source_target_pairs={{0,9},{1,8},{2,11},{3,10},{4,13},{5,12},{6,15},{7,14},{8,1},{9,0},... | collective-permute-start | bytes 56840 | tf_op jit(solution)/shard_map/ppermute | solution.py:189

commit v7 on v4

--- a/solution.py
+++ b/solution.py
@@ -146,9 +146,9 @@
                     block = piece if block is None else block + piece
                 blocks.append(block)
             turned = jnp.concatenate(blocks, axis=1)
-            summed = turned[(FINE - 1) * classes:]
-            for s in range(FINE - 2, -1, -1):
-                summed = turned[s * classes:(s + 1) * classes] + pltpu.roll(summed, ANGLES - STEP, 1)
+            summed = turned[:classes]
+            for s in range(1, FINE):
+                summed = summed + pltpu.roll(turned[s * classes:(s + 1) * classes], ANGLES - s * STEP, 1)
             sums_ref[:, (c + d) * ANGLES:(c + d + 1) * ANGLES] = summed.astype(sums_ref.dtype)
 
 
@@ -183,7 +183,7 @@
         held = operands[0]
         return pl.pallas_call(
             join_kernel, out_shape=jax.ShapeDtypeStruct((2 * held.shape[0], width), bf16),
-            in_specs=[VMEM] * len(operands), out_specs=VMEM, compiler_params=PARAMS, name="join",
+            in_specs=[VMEM] * len(operands), out_specs=VMEM, compiler_params=PARAMS, cost_estimate=pl.CostEstimate(flops=4000000000, bytes_accessed=12000000, transcendentals=0), name="join",
         )(*operands)
 
     rounds = offsets(bits)
@@ -201,19 +201,19 @@
         in_specs=[HBM] * 4, out_specs=[VMEM] * 3,
         scratch_shapes=[
             pltpu.VMEM((1, rows), f32), pltpu.VMEM((TOPK, rows), jnp.int32), pltpu.SemaphoreType.DMA((4,))],
-        compiler_params=PARAMS, name="stage",
+        compiler_params=PARAMS, cost_estimate=pl.CostEstimate(flops=4000000000, bytes_accessed=12000000, transcendentals=0), name="stage",
     )(*held)
     far_info = swap(near_info, 1, 1)
 
-    gathered = join(own, got)
+    before, gathered = own, join(own, got)
+    for pair in rounds[1:-1]:
+        before, got = gathered, swap(gathered, *pair)
+        gathered = join(before, got)
+    parts = swap(before, *rounds[-1]), swap(got, *rounds[-1])
     own_flipped = pl.pallas_call(
         flip_kernel, out_shape=jax.ShapeDtypeStruct((width, rows), bf16),
-        in_specs=[VMEM] * 2, out_specs=VMEM, compiler_params=PARAMS, name="flip",
+        in_specs=[VMEM] * 2, out_specs=VMEM, compiler_params=PARAMS, cost_estimate=pl.CostEstimate(flops=4000000000, bytes_accessed=12000000, transcendentals=0), name="flip",
     )(gathered, p_own)
-    for r, pair in enumerate(rounds[1:], 1):
-        got = swap(gathered, *pair)
-        if r < len(rounds) - 1:
-            gathered = join(gathered, got, own_flipped, far_info)
 
     turned = pltpu.VMEM((ROT * half, width), bf16)
     cost = pl.CostEstimate(
@@ -225,6 +225,7 @@
         in_specs=[VMEM] * 5, out_specs=[VMEM] * 2, scratch_shapes=[turned],
         compiler_params=PARAMS, cost_estimate=cost, name="early",
     )(gathered, own_flipped, p_far, *info)
+    got = join(*parts, far_flipped)
     late, near = pl.pallas_call(
         late_kernel,
         out_shape=(jax.ShapeDtypeStruct((ROT, half, both), f32), jax.ShapeDtypeStruct((1, both), f32)),

time: 28.9 us -> 28.4 us (0.983)
  waiting for transfers between devices: 8.77 us -> 6.34 us
  starting transfers between devices: 13.7 us -> 15.4 us
    ppermute x9 -> x10, waiting for transfers between devices: 8.77 us -> 6.34 us  [swap(): lax.ppermute(x, 'blk', [(i, i ^ (odd if i.bit_count() % 2 else even)) for...]
    ppermute x9 -> x10, starting transfers between devices: 13.7 us -> 15.4 us  [swap(): lax.ppermute(x, 'blk', [(i, i ^ (odd if i.bit_count() % 2 else even)) for...]
    pallas_call x1, Pallas kernels: 0.86 us -> 1.16 us  [local(): pl.pallas_call(functools.partial(back_kernel, bits, owned, 0), out_shape=...]
  transfers between devices with their start and end apart: 9 -> 10, of which waited for: 8 -> 6; matrix products, arithmetic and copies ran while one was open for 0% -> 0% of each run, Pallas kernels for 12% -> 13%
where the time goes in v7:
time: 28.4 us; the launch traced here: 28.3 us
  starting transfers between devices  15.4 us (54%)
  waiting for transfers between devices  6.34 us (22%)
  Pallas kernels  5.68 us (20%)
  between operations  0.73 us (3%)
    ppermute x10, starting transfers between devices, swap(): lax.ppermute(x, 'blk', [(i, i ^ (odd if i.bit_count() % 2 else even)) for...  15.4 us
    ppermute x10, waiting for transfers between devices, swap(): lax.ppermute(x, 'blk', [(i, i ^ (odd if i.bit_count() % 2 else even)) for...  6.34 us
    pallas_call x1, Pallas kernels, local(): pl.pallas_call(stage_kernel, out_shape=(jax.ShapeDtypeStruct((owned, widt...  1.35 us
    pallas_call x1, Pallas kernels, local(): pl.pallas_call(functools.partial(back_kernel, bits, owned, 0), out_shape=...  1.16 us
    pallas_call x1, Pallas kernels, local(): pl.pallas_call(early_kernel, out_shape=(jax.ShapeDtypeStruct((ROT, half,...  0.77 us
    pallas_call x1, Pallas kernels, local(): pl.pallas_call(functools.partial(back_kernel, bits, owned, half), out_sha...  0.72 us
    pallas_call x1, Pallas kernels, local(): pl.pallas_call(last_kernel, out_shape=(jax.ShapeDtypeStruct((owned, width...  0.63 us
    pallas_call x1, Pallas kernels, local(): pl.pallas_call(late_kernel, out_shape=(jax.ShapeDtypeStruct((ROT, half, b...  0.63 us
  transfers between devices with their start and end apart: 10, of which 6 were waited for; matrix products, arithmetic and copies ran while one was open for 0% of the time, Pallas kernels for 13%

profile of v7, /device:TPU:0, one launch (start us, length us, event | category | flops | bytes accessed | tf_op | source)
XLA Modules:
  0.0 28.3 jit_solution(12930085083294791456)
XLA Ops:
  0.6 3.5 %collective-permute-start = (bf16[2,4608]{1,0:T(2,128)(2,1)}, bf16[2,4608]{1,0:T(2,128)(2,1)S(1)}, u32[]{:S(2)}, u32[]{:S(2)}) collective-permute-start(bf16[2,4608]{1,0:T(2,128)(2,1)} %refs.1), channel_id=1, source_target_pairs={{0,9},{1,8},{2,11},{3,10},{4,13},{5,12},{6,15},{7,14},{8,1},{9,0},... | collective-permute-start | bytes 55304 | tf_op jit(solution)/shard_map/ppermute | solution.py:180
  4.2 0.7 %collective-permute-start.2 = (bf16[128,4608]{1,0:T(8,128)(2,1)}, bf16[128,4608]{1,0:T(8,128)(2,1)S(1)}, u32[]{:S(2)}, u32[]{:S(2)}) collective-permute-start(bf16[128,4608]{1,0:T(8,128)(2,1)} %particles.1), channel_id=1, source_target_pairs={{0,1},{1,0},{2,3},{3,2},{4,5},{5,4},{6,7},{7,6},{8,9},{9,8},{10,11... | collective-permute-start | bytes 3538952 | tf_op jit(solution)/shard_map/ppermute | solution.py:180
  4.8 1.4 %stage.1 = (bf16[2,4608]{1,0:T(2,128)(2,1)S(1)}, f32[3,128]{1,0:T(4,128)S(1)}, bf16[128,4608]{1,0:T(8,128)(2,1)S(1)}) custom-call(bf16[2,4608]{1,0:T(2,128)(2,1)} %refs.1, f32[1,128]{1,0:T(1,128)} %bitcast.4, s32[2,128]{1,0:T(2,128)} %bitcast.3, bf16[128,4608]{1,0:T(8,128)(2,1)} %particles.1), custom_call_target="tpu_custom_call" | custom-call | flops 4000000000 | bytes 12000000 | tf_op jit(solution)/shard_map/stage/pallas_call | solution.py:194
  6.2 1.6 %collective-permute-start.1 = (bf16[4,4608]{1,0:T(4,128)(2,1)S(1)}, bf16[4,4608]{1,0:T(4,128)(2,1)S(1)}, u32[]{:S(2)}, u32[]{:S(2)}) collective-permute-start(bf16[4,4608]{1,0:T(4,128)(2,1)S(1)} %join.3.held_ref), channel_id=1, source_target_pairs={{0,5},{1,2},{2,1},{3,6},{4,7},{5,0},{6,3},{7,4},{8,11},{9,12},{10,... | collective-permute-start | bytes 110600 | tf_op jit(solution)/shard_map/ppermute | solution.py:180
  7.8 0.3 %collective-permute-start.3 = (f32[3,128]{1,0:T(4,128)S(1)}, f32[3,128]{1,0:T(4,128)S(1)}, u32[]{:S(2)}, u32[]{:S(2)}) collective-permute-start(f32[3,128]{1,0:T(4,128)S(1)} %get-tuple-element.16.near_info), channel_id=1, source_target_pairs={{0,1},{1,0},{2,3},{3,2},{4,5},{5,4},{6,7},{7,6},{8,9},{9,8},{10,11... | collective-permute-start | bytes 4616 | tf_op jit(solution)/shard_map/ppermute | solution.py:180
  8.2 1.2 %collective-permute-start.4 = (bf16[4,4608]{1,0:T(4,128)(2,1)S(1)}, bf16[4,4608]{1,0:T(4,128)(2,1)S(1)}, u32[]{:S(2)}, u32[]{:S(2)}) collective-permute-start(bf16[4,4608]{1,0:T(4,128)(2,1)S(1)} %join.3.held_ref), channel_id=1, source_target_pairs={{0,3},{1,4},{2,7},{3,0},{4,1},{5,6},{6,5},{7,2},{8,13},{9,10},{10,... | collective-permute-start | bytes 110600 | tf_op jit(solution)/shard_map/ppermute | solution.py:180
  9.3 0.3 %collective-permute-done.1.got_ref = bf16[4,4608]{1,0:T(4,128)(2,1)S(1)} collective-permute-done((bf16[4,4608]{1,0:T(4,128)(2,1)S(1)}, bf16[4,4608]{1,0:T(4,128)(2,1)S(1)}, u32[]{:S(2)}, u32[]{:S(2)}) %collective-permute-start.1) | collective-permute-done | bytes 36896 | tf_op jit(solution)/shard_map/ppermute | solution.py:180
  9.7 1.5 %collective-permute-start.5 = (bf16[4,4608]{1,0:T(4,128)(2,1)S(1)}, bf16[4,4608]{1,0:T(4,128)(2,1)S(1)}, u32[]{:S(2)}, u32[]{:S(2)}) collective-permute-start(bf16[4,4608]{1,0:T(4,128)(2,1)S(1)} %collective-permute-done.1.got_ref), channel_id=1, source_target_pairs={{0,3},{1,4},{2,7},{3,0},{4,1},{5,6},{6,5},{7,2},{8,13},{9,10},{10,... | collective-permute-start | bytes 110600 | tf_op jit(solution)/shard_map/ppermute | solution.py:180
  11.2 0.4 %flip.1.own_flipped = bf16[4608,128]{1,0:T(8,128)(2,1)S(1)} custom-call(bf16[8,4608]{1,0:T(8,128)(2,1)S(1)} %join.4.after_ref.refs_ref, bf16[128,4608]{1,0:T(8,128)(2,1)S(1)} %get-tuple-element.15.p_ref.own_ref), custom_call_target="tpu_custom_call" | custom-call | flops 4000000000 | bytes 12000000 | tf_op jit(solution)/shard_map/flip/pallas_call | solution.py:213
  11.5 0.0 collective-permute-done.3.far_info
  11.5 0.8 %early.1 = (f32[12,8,256]{2,1,0:T(8,128)S(1)}, bf16[4608,128]{1,0:T(8,128)(2,1)S(1)}) custom-call(bf16[8,4608]{1,0:T(8,128)(2,1)S(1)} %join.4.after_ref.refs_ref, bf16[4608,128]{1,0:T(8,128)(2,1)S(1)} %flip.1.own_flipped, bf16[128,4608]{1,0:T(8,128)(2,1)S(1)} %collective-permute-done.2.far_ref, f32[3,128]{1,0:T(4,128)S(1)} %get-tuple-element.16.near_info, ...), custom_call_target="tpu_custom_call" | custom-call | flops 226492416 | bytes 4718592 | tf_op jit(solution)/shard_map/early/pallas_call | solution.py:222
  12.3 0.7 %collective-permute-done.5.got_ref = bf16[4,4608]{1,0:T(4,128)(2,1)S(1)} collective-permute-done((bf16[4,4608]{1,0:T(4,128)(2,1)S(1)}, bf16[4,4608]{1,0:T(4,128)(2,1)S(1)}, u32[]{:S(2)}, u32[]{:S(2)}) %collective-permute-start.5) | collective-permute-done | bytes 36896 | tf_op jit(solution)/shard_map/ppermute | solution.py:180
  13.1 0.6 %late.1 = (f32[12,8,256]{2,1,0:T(8,128)S(1)}, f32[1,256]{1,0:T(1,128)S(1)}) custom-call(bf16[8,4608]{1,0:T(8,128)(2,1)S(1)} %join.5.refs_ref, bf16[4608,128]{1,0:T(8,128)(2,1)S(1)} %flip.1.own_flipped, bf16[4608,128]{1,0:T(8,128)(2,1)S(1)} %get-tuple-element.18.rest_0_.far_flipped, f32[3,128]{1,0:T(4,128)S(1)} %get-tuple-element.16.near_info, ...), custom_call_target="tpu_custom_call" | custom-call | flops 226492416 | bytes 4718592 | tf_op jit(solution)/shard_map/late/pallas_call | solution.py:229
  13.7 0.3 %collective-permute-start.6 = (f32[1,256]{1,0:T(1,128)S(1)}, f32[1,256]{1,0:T(1,128)S(1)}, u32[]{:S(2)}, u32[]{:S(2)}) collective-permute-start(f32[1,256]{1,0:T(1,128)S(1)} %get-tuple-element.19.near_ref), channel_id=1, source_target_pairs={{0,1},{1,0},{2,3},{3,2},{4,5},{5,4},{6,7},{7,6},{8,9},{9,8},{10,11... | collective-permute-start | bytes 3080 | tf_op jit(solution)/shard_map/ppermute | solution.py:180
  14.1 0.9 %collective-permute-done.6.other_ref = f32[1,256]{1,0:T(1,128)S(1)} collective-permute-done((f32[1,256]{1,0:T(1,128)S(1)}, f32[1,256]{1,0:T(1,128)S(1)}, u32[]{:S(2)}, u32[]{:S(2)}) %collective-permute-start.6) | collective-permute-done | bytes 1056 | tf_op jit(solution)/shard_map/ppermute | solution.py:180
  14.9 0.7 %back_send.1 = bf16[8,4736]{1,0:T(8,128)(2,1)S(1)} custom-call(f32[12,8,256]{2,1,0:T(8,128)S(1)} %get-tuple-element.21.logits_ref, f32[1,256]{1,0:T(1,128)S(1)} %get-tuple-element.19.near_ref, f32[1,256]{1,0:T(1,128)S(1)} %collective-permute-done.6.other_ref, bf16[128,4608]{1,0:T(8,128)(2,1)S(1)} %get-tuple-element.15.p_ref.own_ref, ...), custom_call_target="tpu_custom_call" | custom-call | flops 226492416 | bytes 4718592 | tf_op jit(solution)/shard_map/back_send/pallas_call | solution.py:238
  15.7 1.6 %collective-permute-start.7 = (bf16[8,4736]{1,0:T(8,128)(2,1)S(1)}, bf16[8,4736]{1,0:T(8,128)(2,1)S(1)}, u32[]{:S(2)}, u32[]{:S(2)}) collective-permute-start(bf16[8,4736]{1,0:T(8,128)(2,1)S(1)} %back_send.1), channel_id=1, source_target_pairs={{0,3},{1,4},{2,7},{3,0},{4,1},{5,6},{6,5},{7,2},{8,13},{9,10},{10,... | collective-permute-start | bytes 227336 | tf_op jit(solution)/shard_map/ppermute | solution.py:180
  17.3 1.2 %back_keep.1 = (f32[8,4736]{1,0:T(8,128)S(1)}, f32[1,128]{1,0:T(1,128)}) custom-call(f32[12,8,256]{2,1,0:T(8,128)S(1)} %get-tuple-element.17.early_ref.logits_ref, f32[1,256]{1,0:T(1,128)S(1)} %get-tuple-element.19.near_ref, f32[1,256]{1,0:T(1,128)S(1)} %collective-permute-done.6.other_ref, bf16[128,4608]{1,0:T(8,128)(2,1)S(1)} %get-tuple-element.15.p_ref.own_ref, ...), custom_call_target="tpu_custom_call" | custom-call | flops 226492416 | bytes 4718592 | tf_op jit(solution)/shard_map/back_keep/pallas_call | solution.py:244
  18.4 1.1 %collective-permute-done.7 = bf16[8,4736]{1,0:T(8,128)(2,1)S(1)} collective-permute-done((bf16[8,4736]{1,0:T(8,128)(2,1)S(1)}, bf16[8,4736]{1,0:T(8,128)(2,1)S(1)}, u32[]{:S(2)}, u32[]{:S(2)}) %collective-permute-start.7) | collective-permute-done | bytes 75808 | tf_op jit(solution)/shard_map/ppermute | solution.py:180
  19.6 1.6 %collective-permute-start.8 = (bf16[4,4736]{1,0:T(4,128)(2,1)S(1)}, bf16[4,4736]{1,0:T(4,128)(2,1)S(1)}, u32[]{:S(2)}, u32[]{:S(2)}) collective-permute-start(bf16[4,4736]{1,0:T(4,128)(2,1)S(1)} %slice.25), channel_id=1, source_target_pairs={{0,5},{1,2},{2,1},{3,6},{4,7},{5,0},{6,3},{7,4},{8,11},{9,12},{10,... | collective-permute-start | bytes 113672 | tf_op jit(solution)/shard_map/ppermute | solution.py:180
  21.2 1.8 %collective-permute-done.8 = bf16[4,4736]{1,0:T(4,128)(2,1)S(1)} collective-permute-done((bf16[4,4736]{1,0:T(4,128)(2,1)S(1)}, bf16[4,4736]{1,0:T(4,128)(2,1)S(1)}, u32[]{:S(2)}, u32[]{:S(2)}) %collective-permute-start.8) | collective-permute-done | bytes 37920 | tf_op jit(solution)/shard_map/ppermute | solution.py:180
  23.1 3.1 %collective-permute-start.9 = (bf16[2,4736]{1,0:T(2,128)(2,1)S(1)}, bf16[2,4736]{1,0:T(2,128)(2,1)S(1)}, u32[]{:S(2)}, u32[]{:S(2)}) collective-permute-start(bf16[2,4736]{1,0:T(2,128)(2,1)S(1)} %slice.26), channel_id=1, source_target_pairs={{0,9},{1,8},{2,11},{3,10},{4,13},{5,12},{6,15},{7,14},{8,1},{9,0},... | collective-permute-start | bytes 56840 | tf_op jit(solution)/shard_map/ppermute | solution.py:180
  26.2 1.5 %collective-permute-done.9.got_ref = bf16[2,4736]{1,0:T(2,128)(2,1)S(1)} collective-permute-done((bf16[2,4736]{1,0:T(2,128)(2,1)S(1)}, bf16[2,4736]{1,0:T(2,128)(2,1)S(1)}, u32[]{:S(2)}, u32[]{:S(2)}) %collective-permute-start.9) | collective-permute-done | bytes 18976 | tf_op jit(solution)/shard_map/ppermute | solution.py:180
  27.6 0.6 %last.1 = (f32[2,4608]{1,0:T(2,128)}, f32[2]{0:T(128)}) custom-call(f32[2,4736]{1,0:T(2,128)S(1)} %slice.20.keep_ref, bf16[2,4736]{1,0:T(2,128)(2,1)S(1)} %collective-permute-done.9.got_ref), custom_call_target="tpu_custom_call" | custom-call | tf_op jit(solution)/shard_map/last/pallas_call | solution.py:257
  (11 shorter events, 0.2 us)
Async XLA Ops:
  0.6 5.6 %collective-permute-start = (bf16[2,4608]{1,0:T(2,128)(2,1)}, bf16[2,4608]{1,0:T(2,128)(2,1)S(1)}, u32[]{:S(2)}, u32[]{:S(2)}) collective-permute-start(bf16[2,4608]{1,0:T(2,128)(2,1)} %refs.1), channel_id=1, source_target_pairs={{0,9},{1,8},{2,11},{3,10},{4,13},{5,12},{6,15},{7,14},{8,1},{9,0},... | collective-permute-start | bytes 55304 | tf_op jit(solution)/shard_map/ppermute | solution.py:180
  4.2 7.4 %collective-permute-start.2 = (bf16[128,4608]{1,0:T(8,128)(2,1)}, bf16[128,4608]{1,0:T(8,128)(2,1)S(1)}, u32[]{:S(2)}, u32[]{:S(2)}) collective-permute-start(bf16[128,4608]{1,0:T(8,128)(2,1)} %particles.1), channel_id=1, source_target_pairs={{0,1},{1,0},{2,3},{3,2},{4,5},{5,4},{6,7},{7,6},{8,9},{9,8},{10,11... | collective-permute-start | bytes 3538952 | tf_op jit(solution)/shard_map/ppermute | solution.py:180
  6.2 3.4 %collective-permute-start.1 = (bf16[4,4608]{1,0:T(4,128)(2,1)S(1)}, bf16[4,4608]{1,0:T(4,128)(2,1)S(1)}, u32[]{:S(2)}, u32[]{:S(2)}) collective-permute-start(bf16[4,4608]{1,0:T(4,128)(2,1)S(1)} %join.3.held_ref), channel_id=1, source_target_pairs={{0,5},{1,2},{2,1},{3,6},{4,7},{5,0},{6,3},{7,4},{8,11},{9,12},{10,... | collective-permute-start | bytes 110600 | tf_op jit(solution)/shard_map/ppermute | solution.py:180
  7.8 3.7 %collective-permute-start.3 = (f32[3,128]{1,0:T(4,128)S(1)}, f32[3,128]{1,0:T(4,128)S(1)}, u32[]{:S(2)}, u32[]{:S(2)}) collective-permute-start(f32[3,128]{1,0:T(4,128)S(1)} %get-tuple-element.16.near_info), channel_id=1, source_target_pairs={{0,1},{1,0},{2,3},{3,2},{4,5},{5,4},{6,7},{7,6},{8,9},{9,8},{10,11... | collective-permute-start | bytes 4616 | tf_op jit(solution)/shard_map/ppermute | solution.py:180
  8.2 4.2 %collective-permute-start.4 = (bf16[4,4608]{1,0:T(4,128)(2,1)S(1)}, bf16[4,4608]{1,0:T(4,128)(2,1)S(1)}, u32[]{:S(2)}, u32[]{:S(2)}) collective-permute-start(bf16[4,4608]{1,0:T(4,128)(2,1)S(1)} %join.3.held_ref), channel_id=1, source_target_pairs={{0,3},{1,4},{2,7},{3,0},{4,1},{5,6},{6,5},{7,2},{8,13},{9,10},{10,... | collective-permute-start | bytes 110600 | tf_op jit(solution)/shard_map/ppermute | solution.py:180
  9.7 3.4 %collective-permute-start.5 = (bf16[4,4608]{1,0:T(4,128)(2,1)S(1)}, bf16[4,4608]{1,0:T(4,128)(2,1)S(1)}, u32[]{:S(2)}, u32[]{:S(2)}) collective-permute-start(bf16[4,4608]{1,0:T(4,128)(2,1)S(1)} %collective-permute-done.1.got_ref), channel_id=1, source_target_pairs={{0,3},{1,4},{2,7},{3,0},{4,1},{5,6},{6,5},{7,2},{8,13},{9,10},{10,... | collective-permute-start | bytes 110600 | tf_op jit(solution)/shard_map/ppermute | solution.py:180
  13.7 1.2 %collective-permute-start.6 = (f32[1,256]{1,0:T(1,128)S(1)}, f32[1,256]{1,0:T(1,128)S(1)}, u32[]{:S(2)}, u32[]{:S(2)}) collective-permute-start(f32[1,256]{1,0:T(1,128)S(1)} %get-tuple-element.19.near_ref), channel_id=1, source_target_pairs={{0,1},{1,0},{2,3},{3,2},{4,5},{5,4},{6,7},{7,6},{8,9},{9,8},{10,11... | collective-permute-start | bytes 3080 | tf_op jit(solution)/shard_map/ppermute | solution.py:180
  15.7 3.9 %collective-permute-start.7 = (bf16[8,4736]{1,0:T(8,128)(2,1)S(1)}, bf16[8,4736]{1,0:T(8,128)(2,1)S(1)}, u32[]{:S(2)}, u32[]{:S(2)}) collective-permute-start(bf16[8,4736]{1,0:T(8,128)(2,1)S(1)} %back_send.1), channel_id=1, source_target_pairs={{0,3},{1,4},{2,7},{3,0},{4,1},{5,6},{6,5},{7,2},{8,13},{9,10},{10,... | collective-permute-start | bytes 227336 | tf_op jit(solution)/shard_map/ppermute | solution.py:180
  19.6 3.5 %collective-permute-start.8 = (bf16[4,4736]{1,0:T(4,128)(2,1)S(1)}, bf16[4,4736]{1,0:T(4,128)(2,1)S(1)}, u32[]{:S(2)}, u32[]{:S(2)}) collective-permute-start(bf16[4,4736]{1,0:T(4,128)(2,1)S(1)} %slice.25), channel_id=1, source_target_pairs={{0,5},{1,2},{2,1},{3,6},{4,7},{5,0},{6,3},{7,4},{8,11},{9,12},{10,... | collective-permute-start | bytes 113672 | tf_op jit(solution)/shard_map/ppermute | solution.py:180
  23.1 4.5 %collective-permute-start.9 = (bf16[2,4736]{1,0:T(2,128)(2,1)S(1)}, bf16[2,4736]{1,0:T(2,128)(2,1)S(1)}, u32[]{:S(2)}, u32[]{:S(2)}) collective-permute-start(bf16[2,4736]{1,0:T(2,128)(2,1)S(1)} %slice.26), channel_id=1, source_target_pairs={{0,9},{1,8},{2,11},{3,10},{4,13},{5,12},{6,15},{7,14},{8,1},{9,0},... | collective-permute-start | bytes 56840 | tf_op jit(solution)/shard_map/ppermute | solution.py:180

commit v8 on v7

--- a/solution.py
+++ b/solution.py
@@ -81,19 +81,28 @@
     return noise[None] * (dots - 0.5 * energy[None])
 
 
-def early_kernel(refs_ref, own_flipped, far_ref, near_info, far_info, logits_ref, far_flipped, turned_ref):
+def sums_of(logits):
+    top = jnp.max(jnp.max(logits, axis=0), axis=0, keepdims=True)
+    total = jnp.sum(jnp.sum(jnp.exp(logits - top[None]), axis=0), axis=0, keepdims=True)
+    return top, total
+
+
+def early_kernel(refs_ref, own_flipped, far_ref, near_info, far_info, logits_ref, far_flipped, part_ref, turned_ref):
     flip(far_ref, far_flipped)
-    logits_ref[...] = score(refs_ref, own_flipped, far_flipped, near_info, far_info, turned_ref)
+    early = score(refs_ref, own_flipped, far_flipped, near_info, far_info, turned_ref)
+    logits_ref[...] = early
+    top, total = sums_of(early)
+    part_ref[...] = jnp.concatenate([top, total], axis=0)
 
 
 def late_kernel(refs_ref, own_flipped, far_flipped, near_info, far_info, early_ref, logits_ref, part_ref, turned_ref):
     late = score(refs_ref, own_flipped, far_flipped, near_info, far_info, turned_ref)
     logits_ref[...] = late
-    early = early_ref[...]
-    top = jnp.maximum(jnp.max(late, axis=0), jnp.max(early, axis=0))
-    top = jnp.max(top, axis=0, keepdims=True)
-    total = jnp.sum(jnp.exp(late - top[None]), axis=0) + jnp.sum(jnp.exp(early - top[None]), axis=0)
-    part_ref[...] = top + jnp.log(jnp.sum(total, axis=0, keepdims=True))
+    top, total = sums_of(late)
+    top_early, total_early = early_ref[0:1, :], early_ref[1:2, :]
+    both = jnp.maximum(top, top_early)
+    total = total * jnp.exp(top - both) + total_early * jnp.exp(top_early - both)
+    part_ref[...] = both + jnp.log(total)
 
 
 def back_kernel(bits, owned, first, logits_ref, near_ref, other_ref, own_ref, far_ref, near_info, far_info,
@@ -219,10 +228,14 @@
     cost = pl.CostEstimate(
         flops=2 * ROT * half * both * width, bytes_accessed=4 * both * width, transcendentals=0)
     info = (near_info, far_info)
-    early, far_flipped = pl.pallas_call(
+    early, far_flipped, early_part = pl.pallas_call(
         early_kernel,
-        out_shape=(jax.ShapeDtypeStruct((ROT, half, both), f32), jax.ShapeDtypeStruct((width, rows), bf16)),
-        in_specs=[VMEM] * 5, out_specs=[VMEM] * 2, scratch_shapes=[turned],
+        out_shape=(
+            jax.ShapeDtypeStruct((ROT, half, both), f32),
+            jax.ShapeDtypeStruct((width, rows), bf16),
+            jax.ShapeDtypeStruct((2, both), f32),
+        ),
+        in_specs=[VMEM] * 5, out_specs=[VMEM] * 3, scratch_shapes=[turned],
         compiler_params=PARAMS, cost_estimate=cost, name="early",
     )(gathered, own_flipped, p_far, *info)
     got = join(*parts, far_flipped)
@@ -231,7 +244,7 @@
         out_shape=(jax.ShapeDtypeStruct((ROT, half, both), f32), jax.ShapeDtypeStruct((1, both), f32)),
         in_specs=[VMEM] * 6, out_specs=[VMEM] * 2, scratch_shapes=[turned],
         compiler_params=PARAMS, cost_estimate=cost, name="late",
-    )(got, own_flipped, far_flipped, *info, early)
+    )(got, own_flipped, far_flipped, *info, early_part)
     other = swap(near, 1, 1)
     shared = (p_own, p_far, *info)
 

time: 28.4 us -> 28.4 us (level)
  no operation moved by 1% of the time
where the time goes in v8:
time: 28.4 us; the launch traced here: 28.3 us
  starting transfers between devices  15.4 us (54%)
  waiting for transfers between devices  6.27 us (22%)
  Pallas kernels  5.76 us (20%)
  between operations  0.74 us (3%)
    ppermute x10, starting transfers between devices, swap(): lax.ppermute(x, 'blk', [(i, i ^ (odd if i.bit_count() % 2 else even)) for...  15.4 us
    ppermute x10, waiting for transfers between devices, swap(): lax.ppermute(x, 'blk', [(i, i ^ (odd if i.bit_count() % 2 else even)) for...  6.27 us
    pallas_call x1, Pallas kernels, local(): pl.pallas_call(stage_kernel, out_shape=(jax.ShapeDtypeStruct((owned, widt...  1.35 us
    pallas_call x1, Pallas kernels, local(): pl.pallas_call(functools.partial(back_kernel, bits, owned, 0), out_shape=...  1.16 us
    pallas_call x1, Pallas kernels, local(): pl.pallas_call(early_kernel, out_shape=(jax.ShapeDtypeStruct((ROT, half,...  0.84 us
    pallas_call x1, Pallas kernels, local(): pl.pallas_call(functools.partial(back_kernel, bits, owned, half), out_sha...  0.72 us
    pallas_call x1, Pallas kernels, local(): pl.pallas_call(late_kernel, out_shape=(jax.ShapeDtypeStruct((ROT, half, b...  0.64 us
    pallas_call x1, Pallas kernels, local(): pl.pallas_call(last_kernel, out_shape=(jax.ShapeDtypeStruct((owned, width...  0.63 us
  transfers between devices with their start and end apart: 10, of which 6 were waited for; matrix products, arithmetic and copies ran while one was open for 0% of the time, Pallas kernels for 13%

profile of v8, /device:TPU:0, one launch (start us, length us, event | category | flops | bytes accessed | tf_op | source)
XLA Modules:
  0.0 28.3 jit_solution(8874223734602097022)
XLA Ops:
  0.6 3.5 %collective-permute-start = (bf16[2,4608]{1,0:T(2,128)(2,1)}, bf16[2,4608]{1,0:T(2,128)(2,1)S(1)}, u32[]{:S(2)}, u32[]{:S(2)}) collective-permute-start(bf16[2,4608]{1,0:T(2,128)(2,1)} %refs.1), channel_id=1, source_target_pairs={{0,9},{1,8},{2,11},{3,10},{4,13},{5,12},{6,15},{7,14},{8,1},{9,0},... | collective-permute-start | bytes 55304 | tf_op jit(solution)/shard_map/ppermute | solution.py:189
  4.2 0.7 %collective-permute-start.2 = (bf16[128,4608]{1,0:T(8,128)(2,1)}, bf16[128,4608]{1,0:T(8,128)(2,1)S(1)}, u32[]{:S(2)}, u32[]{:S(2)}) collective-permute-start(bf16[128,4608]{1,0:T(8,128)(2,1)} %particles.1), channel_id=1, source_target_pairs={{0,1},{1,0},{2,3},{3,2},{4,5},{5,4},{6,7},{7,6},{8,9},{9,8},{10,11... | collective-permute-start | bytes 3538952 | tf_op jit(solution)/shard_map/ppermute | solution.py:189
  4.8 1.4 %stage.1 = (bf16[2,4608]{1,0:T(2,128)(2,1)S(1)}, f32[3,128]{1,0:T(4,128)S(1)}, bf16[128,4608]{1,0:T(8,128)(2,1)S(1)}) custom-call(bf16[2,4608]{1,0:T(2,128)(2,1)} %refs.1, f32[1,128]{1,0:T(1,128)} %bitcast.4, s32[2,128]{1,0:T(2,128)} %bitcast.3, bf16[128,4608]{1,0:T(8,128)(2,1)} %particles.1), custom_call_target="tpu_custom_call" | custom-call | flops 4000000000 | bytes 12000000 | tf_op jit(solution)/shard_map/stage/pallas_call | solution.py:203
  6.2 1.6 %collective-permute-start.1 = (bf16[4,4608]{1,0:T(4,128)(2,1)S(1)}, bf16[4,4608]{1,0:T(4,128)(2,1)S(1)}, u32[]{:S(2)}, u32[]{:S(2)}) collective-permute-start(bf16[4,4608]{1,0:T(4,128)(2,1)S(1)} %join.3.held_ref), channel_id=1, source_target_pairs={{0,5},{1,2},{2,1},{3,6},{4,7},{5,0},{6,3},{7,4},{8,11},{9,12},{10,... | collective-permute-start | bytes 110600 | tf_op jit(solution)/shard_map/ppermute | solution.py:189
  7.8 0.3 %collective-permute-start.3 = (f32[3,128]{1,0:T(4,128)S(1)}, f32[3,128]{1,0:T(4,128)S(1)}, u32[]{:S(2)}, u32[]{:S(2)}) collective-permute-start(f32[3,128]{1,0:T(4,128)S(1)} %get-tuple-element.17.near_info), channel_id=1, source_target_pairs={{0,1},{1,0},{2,3},{3,2},{4,5},{5,4},{6,7},{7,6},{8,9},{9,8},{10,11... | collective-permute-start | bytes 4616 | tf_op jit(solution)/shard_map/ppermute | solution.py:189
  8.2 1.2 %collective-permute-start.4 = (bf16[4,4608]{1,0:T(4,128)(2,1)S(1)}, bf16[4,4608]{1,0:T(4,128)(2,1)S(1)}, u32[]{:S(2)}, u32[]{:S(2)}) collective-permute-start(bf16[4,4608]{1,0:T(4,128)(2,1)S(1)} %join.3.held_ref), channel_id=1, source_target_pairs={{0,3},{1,4},{2,7},{3,0},{4,1},{5,6},{6,5},{7,2},{8,13},{9,10},{10,... | collective-permute-start | bytes 110600 | tf_op jit(solution)/shard_map/ppermute | solution.py:189
  9.3 0.3 %collective-permute-done.1.got_ref = bf16[4,4608]{1,0:T(4,128)(2,1)S(1)} collective-permute-done((bf16[4,4608]{1,0:T(4,128)(2,1)S(1)}, bf16[4,4608]{1,0:T(4,128)(2,1)S(1)}, u32[]{:S(2)}, u32[]{:S(2)}) %collective-permute-start.1) | collective-permute-done | bytes 36896 | tf_op jit(solution)/shard_map/ppermute | solution.py:189
  9.7 1.5 %collective-permute-start.5 = (bf16[4,4608]{1,0:T(4,128)(2,1)S(1)}, bf16[4,4608]{1,0:T(4,128)(2,1)S(1)}, u32[]{:S(2)}, u32[]{:S(2)}) collective-permute-start(bf16[4,4608]{1,0:T(4,128)(2,1)S(1)} %collective-permute-done.1.got_ref), channel_id=1, source_target_pairs={{0,3},{1,4},{2,7},{3,0},{4,1},{5,6},{6,5},{7,2},{8,13},{9,10},{10,... | collective-permute-start | bytes 110600 | tf_op jit(solution)/shard_map/ppermute | solution.py:189
  11.2 0.4 %flip.1.own_flipped = bf16[4608,128]{1,0:T(8,128)(2,1)S(1)} custom-call(bf16[8,4608]{1,0:T(8,128)(2,1)S(1)} %join.4.after_ref.refs_ref, bf16[128,4608]{1,0:T(8,128)(2,1)S(1)} %get-tuple-element.16.p_ref.own_ref), custom_call_target="tpu_custom_call" | custom-call | flops 4000000000 | bytes 12000000 | tf_op jit(solution)/shard_map/flip/pallas_call | solution.py:222
  11.5 0.8 %early.1 = (f32[12,8,256]{2,1,0:T(8,128)S(1)}, bf16[4608,128]{1,0:T(8,128)(2,1)S(1)}, f32[2,256]{1,0:T(2,128)S(1)}) custom-call(bf16[8,4608]{1,0:T(8,128)(2,1)S(1)} %join.4.after_ref.refs_ref, bf16[4608,128]{1,0:T(8,128)(2,1)S(1)} %flip.1.own_flipped, bf16[128,4608]{1,0:T(8,128)(2,1)S(1)} %collective-permute-done.2.far_ref, ...), custom_call_target="tpu_custom_call" | custom-call | flops 226492416 | bytes 4718592 | tf_op jit(solution)/shard_map/early/pallas_call | solution.py:231
  12.4 0.0 collective-permute-done.4.held_ref
  12.4 0.7 %collective-permute-done.5.got_ref = bf16[4,4608]{1,0:T(4,128)(2,1)S(1)} collective-permute-done((bf16[4,4608]{1,0:T(4,128)(2,1)S(1)}, bf16[4,4608]{1,0:T(4,128)(2,1)S(1)}, u32[]{:S(2)}, u32[]{:S(2)}) %collective-permute-start.5) | collective-permute-done | bytes 36896 | tf_op jit(solution)/shard_map/ppermute | solution.py:189
  13.1 0.6 %late.1 = (f32[12,8,256]{2,1,0:T(8,128)S(1)}, f32[1,256]{1,0:T(1,128)S(1)}) custom-call(bf16[8,4608]{1,0:T(8,128)(2,1)S(1)} %join.5.refs_ref, bf16[4608,128]{1,0:T(8,128)(2,1)S(1)} %flip.1.own_flipped, bf16[4608,128]{1,0:T(8,128)(2,1)S(1)} %get-tuple-element.19.rest_0_.far_flipped, f32[3,128]{1,0:T(4,128)S(1)} %get-tuple-element.17.near_info, ...), custom_call_target="tpu_custom_call" | custom-call | flops 226492416 | bytes 4718592 | tf_op jit(solution)/shard_map/late/pallas_call | solution.py:242
  13.7 0.3 %collective-permute-start.6 = (f32[1,256]{1,0:T(1,128)S(1)}, f32[1,256]{1,0:T(1,128)S(1)}, u32[]{:S(2)}, u32[]{:S(2)}) collective-permute-start(f32[1,256]{1,0:T(1,128)S(1)} %get-tuple-element.21.near_ref), channel_id=1, source_target_pairs={{0,1},{1,0},{2,3},{3,2},{4,5},{5,4},{6,7},{7,6},{8,9},{9,8},{10,11... | collective-permute-start | bytes 3080 | tf_op jit(solution)/shard_map/ppermute | solution.py:189
  14.1 0.9 %collective-permute-done.6.other_ref = f32[1,256]{1,0:T(1,128)S(1)} collective-permute-done((f32[1,256]{1,0:T(1,128)S(1)}, f32[1,256]{1,0:T(1,128)S(1)}, u32[]{:S(2)}, u32[]{:S(2)}) %collective-permute-start.6) | collective-permute-done | bytes 1056 | tf_op jit(solution)/shard_map/ppermute | solution.py:189
  14.9 0.7 %back_send.1 = bf16[8,4736]{1,0:T(8,128)(2,1)S(1)} custom-call(f32[12,8,256]{2,1,0:T(8,128)S(1)} %get-tuple-element.23.logits_ref, f32[1,256]{1,0:T(1,128)S(1)} %get-tuple-element.21.near_ref, f32[1,256]{1,0:T(1,128)S(1)} %collective-permute-done.6.other_ref, bf16[128,4608]{1,0:T(8,128)(2,1)S(1)} %get-tuple-element.16.p_ref.own_ref, ...), custom_call_target="tpu_custom_call" | custom-call | flops 226492416 | bytes 4718592 | tf_op jit(solution)/shard_map/back_send/pallas_call | solution.py:251
  15.7 1.6 %collective-permute-start.7 = (bf16[8,4736]{1,0:T(8,128)(2,1)S(1)}, bf16[8,4736]{1,0:T(8,128)(2,1)S(1)}, u32[]{:S(2)}, u32[]{:S(2)}) collective-permute-start(bf16[8,4736]{1,0:T(8,128)(2,1)S(1)} %back_send.1), channel_id=1, source_target_pairs={{0,3},{1,4},{2,7},{3,0},{4,1},{5,6},{6,5},{7,2},{8,13},{9,10},{10,... | collective-permute-start | bytes 227336 | tf_op jit(solution)/shard_map/ppermute | solution.py:189
  17.3 1.2 %back_keep.1 = (f32[8,4736]{1,0:T(8,128)S(1)}, f32[1,128]{1,0:T(1,128)}) custom-call(f32[12,8,256]{2,1,0:T(8,128)S(1)} %get-tuple-element.18.logits_ref, f32[1,256]{1,0:T(1,128)S(1)} %get-tuple-element.21.near_ref, f32[1,256]{1,0:T(1,128)S(1)} %collective-permute-done.6.other_ref, bf16[128,4608]{1,0:T(8,128)(2,1)S(1)} %get-tuple-element.16.p_ref.own_ref, ...), custom_call_target="tpu_custom_call" | custom-call | flops 226492416 | bytes 4718592 | tf_op jit(solution)/shard_map/back_keep/pallas_call | solution.py:257
  18.4 1.1 %collective-permute-done.7 = bf16[8,4736]{1,0:T(8,128)(2,1)S(1)} collective-permute-done((bf16[8,4736]{1,0:T(8,128)(2,1)S(1)}, bf16[8,4736]{1,0:T(8,128)(2,1)S(1)}, u32[]{:S(2)}, u32[]{:S(2)}) %collective-permute-start.7) | collective-permute-done | bytes 75808 | tf_op jit(solution)/shard_map/ppermute | solution.py:189
  19.6 1.6 %collective-permute-start.8 = (bf16[4,4736]{1,0:T(4,128)(2,1)S(1)}, bf16[4,4736]{1,0:T(4,128)(2,1)S(1)}, u32[]{:S(2)}, u32[]{:S(2)}) collective-permute-start(bf16[4,4736]{1,0:T(4,128)(2,1)S(1)} %slice.25), channel_id=1, source_target_pairs={{0,5},{1,2},{2,1},{3,6},{4,7},{5,0},{6,3},{7,4},{8,11},{9,12},{10,... | collective-permute-start | bytes 113672 | tf_op jit(solution)/shard_map/ppermute | solution.py:189
  21.2 1.8 %collective-permute-done.8 = bf16[4,4736]{1,0:T(4,128)(2,1)S(1)} collective-permute-done((bf16[4,4736]{1,0:T(4,128)(2,1)S(1)}, bf16[4,4736]{1,0:T(4,128)(2,1)S(1)}, u32[]{:S(2)}, u32[]{:S(2)}) %collective-permute-start.8) | collective-permute-done | bytes 37920 | tf_op jit(solution)/shard_map/ppermute | solution.py:189
  23.1 3.1 %collective-permute-start.9 = (bf16[2,4736]{1,0:T(2,128)(2,1)S(1)}, bf16[2,4736]{1,0:T(2,128)(2,1)S(1)}, u32[]{:S(2)}, u32[]{:S(2)}) collective-permute-start(bf16[2,4736]{1,0:T(2,128)(2,1)S(1)} %slice.26), channel_id=1, source_target_pairs={{0,9},{1,8},{2,11},{3,10},{4,13},{5,12},{6,15},{7,14},{8,1},{9,0},... | collective-permute-start | bytes 56840 | tf_op jit(solution)/shard_map/ppermute | solution.py:189
  26.2 1.5 %collective-permute-done.9.got_ref = bf16[2,4736]{1,0:T(2,128)(2,1)S(1)} collective-permute-done((bf16[2,4736]{1,0:T(2,128)(2,1)S(1)}, bf16[2,4736]{1,0:T(2,128)(2,1)S(1)}, u32[]{:S(2)}, u32[]{:S(2)}) %collective-permute-start.9) | collective-permute-done | bytes 18976 | tf_op jit(solution)/shard_map/ppermute | solution.py:189
  27.6 0.6 %last.1 = (f32[2,4608]{1,0:T(2,128)}, f32[2]{0:T(128)}) custom-call(f32[2,4736]{1,0:T(2,128)S(1)} %slice.20.keep_ref, bf16[2,4736]{1,0:T(2,128)(2,1)S(1)} %collective-permute-done.9.got_ref), custom_call_target="tpu_custom_call" | custom-call | tf_op jit(solution)/shard_map/last/pallas_call | solution.py:270
  (11 shorter events, 0.2 us)
Async XLA Ops:
  0.6 5.6 %collective-permute-start = (bf16[2,4608]{1,0:T(2,128)(2,1)}, bf16[2,4608]{1,0:T(2,128)(2,1)S(1)}, u32[]{:S(2)}, u32[]{:S(2)}) collective-permute-start(bf16[2,4608]{1,0:T(2,128)(2,1)} %refs.1), channel_id=1, source_target_pairs={{0,9},{1,8},{2,11},{3,10},{4,13},{5,12},{6,15},{7,14},{8,1},{9,0},... | collective-permute-start | bytes 55304 | tf_op jit(solution)/shard_map/ppermute | solution.py:189
  4.2 7.4 %collective-permute-start.2 = (bf16[128,4608]{1,0:T(8,128)(2,1)}, bf16[128,4608]{1,0:T(8,128)(2,1)S(1)}, u32[]{:S(2)}, u32[]{:S(2)}) collective-permute-start(bf16[128,4608]{1,0:T(8,128)(2,1)} %particles.1), channel_id=1, source_target_pairs={{0,1},{1,0},{2,3},{3,2},{4,5},{5,4},{6,7},{7,6},{8,9},{9,8},{10,11... | collective-permute-start | bytes 3538952 | tf_op jit(solution)/shard_map/ppermute | solution.py:189
  6.2 3.4 %collective-permute-start.1 = (bf16[4,4608]{1,0:T(4,128)(2,1)S(1)}, bf16[4,4608]{1,0:T(4,128)(2,1)S(1)}, u32[]{:S(2)}, u32[]{:S(2)}) collective-permute-start(bf16[4,4608]{1,0:T(4,128)(2,1)S(1)} %join.3.held_ref), channel_id=1, source_target_pairs={{0,5},{1,2},{2,1},{3,6},{4,7},{5,0},{6,3},{7,4},{8,11},{9,12},{10,... | collective-permute-start | bytes 110600 | tf_op jit(solution)/shard_map/ppermute | solution.py:189
  7.8 3.7 %collective-permute-start.3 = (f32[3,128]{1,0:T(4,128)S(1)}, f32[3,128]{1,0:T(4,128)S(1)}, u32[]{:S(2)}, u32[]{:S(2)}) collective-permute-start(f32[3,128]{1,0:T(4,128)S(1)} %get-tuple-element.17.near_info), channel_id=1, source_target_pairs={{0,1},{1,0},{2,3},{3,2},{4,5},{5,4},{6,7},{7,6},{8,9},{9,8},{10,11... | collective-permute-start | bytes 4616 | tf_op jit(solution)/shard_map/ppermute | solution.py:189
  8.2 4.2 %collective-permute-start.4 = (bf16[4,4608]{1,0:T(4,128)(2,1)S(1)}, bf16[4,4608]{1,0:T(4,128)(2,1)S(1)}, u32[]{:S(2)}, u32[]{:S(2)}) collective-permute-start(bf16[4,4608]{1,0:T(4,128)(2,1)S(1)} %join.3.held_ref), channel_id=1, source_target_pairs={{0,3},{1,4},{2,7},{3,0},{4,1},{5,6},{6,5},{7,2},{8,13},{9,10},{10,... | collective-permute-start | bytes 110600 | tf_op jit(solution)/shard_map/ppermute | solution.py:189
  9.7 3.4 %collective-permute-start.5 = (bf16[4,4608]{1,0:T(4,128)(2,1)S(1)}, bf16[4,4608]{1,0:T(4,128)(2,1)S(1)}, u32[]{:S(2)}, u32[]{:S(2)}) collective-permute-start(bf16[4,4608]{1,0:T(4,128)(2,1)S(1)} %collective-permute-done.1.got_ref), channel_id=1, source_target_pairs={{0,3},{1,4},{2,7},{3,0},{4,1},{5,6},{6,5},{7,2},{8,13},{9,10},{10,... | collective-permute-start | bytes 110600 | tf_op jit(solution)/shard_map/ppermute | solution.py:189
  13.7 1.2 %collective-permute-start.6 = (f32[1,256]{1,0:T(1,128)S(1)}, f32[1,256]{1,0:T(1,128)S(1)}, u32[]{:S(2)}, u32[]{:S(2)}) collective-permute-start(f32[1,256]{1,0:T(1,128)S(1)} %get-tuple-element.21.near_ref), channel_id=1, source_target_pairs={{0,1},{1,0},{2,3},{3,2},{4,5},{5,4},{6,7},{7,6},{8,9},{9,8},{10,11... | collective-permute-start | bytes 3080 | tf_op jit(solution)/shard_map/ppermute | solution.py:189
  15.7 3.9 %collective-permute-start.7 = (bf16[8,4736]{1,0:T(8,128)(2,1)S(1)}, bf16[8,4736]{1,0:T(8,128)(2,1)S(1)}, u32[]{:S(2)}, u32[]{:S(2)}) collective-permute-start(bf16[8,4736]{1,0:T(8,128)(2,1)S(1)} %back_send.1), channel_id=1, source_target_pairs={{0,3},{1,4},{2,7},{3,0},{4,1},{5,6},{6,5},{7,2},{8,13},{9,10},{10,... | collective-permute-start | bytes 227336 | tf_op jit(solution)/shard_map/ppermute | solution.py:189
  19.6 3.5 %collective-permute-start.8 = (bf16[4,4736]{1,0:T(4,128)(2,1)S(1)}, bf16[4,4736]{1,0:T(4,128)(2,1)S(1)}, u32[]{:S(2)}, u32[]{:S(2)}) collective-permute-start(bf16[4,4736]{1,0:T(4,128)(2,1)S(1)} %slice.25), channel_id=1, source_target_pairs={{0,5},{1,2},{2,1},{3,6},{4,7},{5,0},{6,3},{7,4},{8,11},{9,12},{10,... | collective-permute-start | bytes 113672 | tf_op jit(solution)/shard_map/ppermute | solution.py:189
  23.1 4.5 %collective-permute-start.9 = (bf16[2,4736]{1,0:T(2,128)(2,1)S(1)}, bf16[2,4736]{1,0:T(2,128)(2,1)S(1)}, u32[]{:S(2)}, u32[]{:S(2)}) collective-permute-start(bf16[2,4736]{1,0:T(2,128)(2,1)S(1)} %slice.26), channel_id=1, source_target_pairs={{0,9},{1,8},{2,11},{3,10},{4,13},{5,12},{6,15},{7,14},{8,1},{9,0},... | collective-permute-start | bytes 56840 | tf_op jit(solution)/shard_map/ppermute | solution.py:189

commit v9 on v7

--- a/solution.py
+++ b/solution.py
@@ -132,9 +132,12 @@
     low = (post - high.astype(jnp.float32)).astype(jnp.bfloat16)
     both = jnp.concatenate([high, low], axis=0)
     group = FINE * classes
+    parts = []
     for c in range(0, CYCLES, 2):
         chunk = particles_of(own_ref, far_ref, c * ANGLES, 2 * ANGLES)
-        part = jnp.dot(both, chunk, preferred_element_type=jnp.float32)
+        parts.append(jnp.dot(both, chunk, preferred_element_type=jnp.float32))
+    for c in range(0, CYCLES, 2):
+        part = parts[c // 2]
         part = part[:count] + part[count:]
         for d in range(2):
             blocks = []

time: 28.4 us -> 28.4 us (level)
  no operation moved by 1% of the time
where the time goes in v9:
time: 28.4 us; the launch traced here: 28.3 us
  starting transfers between devices  15.4 us (54%)
  waiting for transfers between devices  6.34 us (22%)
  Pallas kernels  5.68 us (20%)
  between operations  0.73 us (3%)
    ppermute x10, starting transfers between devices, swap(): lax.ppermute(x, 'blk', [(i, i ^ (odd if i.bit_count() % 2 else even)) for...  15.4 us
    ppermute x10, waiting for transfers between devices, swap(): lax.ppermute(x, 'blk', [(i, i ^ (odd if i.bit_count() % 2 else even)) for...  6.34 us
    pallas_call x1, Pallas kernels, local(): pl.pallas_call(stage_kernel, out_shape=(jax.ShapeDtypeStruct((owned, widt...  1.35 us
    pallas_call x1, Pallas kernels, local(): pl.pallas_call(functools.partial(back_kernel, bits, owned, 0), out_shape=...  1.16 us
    pallas_call x1, Pallas kernels, local(): pl.pallas_call(early_kernel, out_shape=(jax.ShapeDtypeStruct((ROT, half,...  0.77 us
    pallas_call x1, Pallas kernels, local(): pl.pallas_call(functools.partial(back_kernel, bits, owned, half), out_sha...  0.72 us
    pallas_call x1, Pallas kernels, local(): pl.pallas_call(last_kernel, out_shape=(jax.ShapeDtypeStruct((owned, width...  0.63 us
    pallas_call x1, Pallas kernels, local(): pl.pallas_call(late_kernel, out_shape=(jax.ShapeDtypeStruct((ROT, half, b...  0.63 us
  transfers between devices with their start and end apart: 10, of which 6 were waited for; matrix products, arithmetic and copies ran while one was open for 0% of the time, Pallas kernels for 13%

profile of v9, /device:TPU:0, one launch (start us, length us, event | category | flops | bytes accessed | tf_op | source)
XLA Modules:
  0.0 28.3 jit_solution(2220611824280768215)
XLA Ops:
  0.6 3.5 %collective-permute-start = (bf16[2,4608]{1,0:T(2,128)(2,1)}, bf16[2,4608]{1,0:T(2,128)(2,1)S(1)}, u32[]{:S(2)}, u32[]{:S(2)}) collective-permute-start(bf16[2,4608]{1,0:T(2,128)(2,1)} %refs.1), channel_id=1, source_target_pairs={{0,9},{1,8},{2,11},{3,10},{4,13},{5,12},{6,15},{7,14},{8,1},{9,0},... | collective-permute-start | bytes 55304 | tf_op jit(solution)/shard_map/ppermute | solution.py:183
  4.2 0.7 %collective-permute-start.2 = (bf16[128,4608]{1,0:T(8,128)(2,1)}, bf16[128,4608]{1,0:T(8,128)(2,1)S(1)}, u32[]{:S(2)}, u32[]{:S(2)}) collective-permute-start(bf16[128,4608]{1,0:T(8,128)(2,1)} %particles.1), channel_id=1, source_target_pairs={{0,1},{1,0},{2,3},{3,2},{4,5},{5,4},{6,7},{7,6},{8,9},{9,8},{10,11... | collective-permute-start | bytes 3538952 | tf_op jit(solution)/shard_map/ppermute | solution.py:183
  4.8 1.4 %stage.1 = (bf16[2,4608]{1,0:T(2,128)(2,1)S(1)}, f32[3,128]{1,0:T(4,128)S(1)}, bf16[128,4608]{1,0:T(8,128)(2,1)S(1)}) custom-call(bf16[2,4608]{1,0:T(2,128)(2,1)} %refs.1, f32[1,128]{1,0:T(1,128)} %bitcast.4, s32[2,128]{1,0:T(2,128)} %bitcast.3, bf16[128,4608]{1,0:T(8,128)(2,1)} %particles.1), custom_call_target="tpu_custom_call" | custom-call | flops 4000000000 | bytes 12000000 | tf_op jit(solution)/shard_map/stage/pallas_call | solution.py:197
  6.2 1.6 %collective-permute-start.1 = (bf16[4,4608]{1,0:T(4,128)(2,1)S(1)}, bf16[4,4608]{1,0:T(4,128)(2,1)S(1)}, u32[]{:S(2)}, u32[]{:S(2)}) collective-permute-start(bf16[4,4608]{1,0:T(4,128)(2,1)S(1)} %join.3.held_ref), channel_id=1, source_target_pairs={{0,5},{1,2},{2,1},{3,6},{4,7},{5,0},{6,3},{7,4},{8,11},{9,12},{10,... | collective-permute-start | bytes 110600 | tf_op jit(solution)/shard_map/ppermute | solution.py:183
  7.8 0.3 %collective-permute-start.3 = (f32[3,128]{1,0:T(4,128)S(1)}, f32[3,128]{1,0:T(4,128)S(1)}, u32[]{:S(2)}, u32[]{:S(2)}) collective-permute-start(f32[3,128]{1,0:T(4,128)S(1)} %get-tuple-element.16.near_info), channel_id=1, source_target_pairs={{0,1},{1,0},{2,3},{3,2},{4,5},{5,4},{6,7},{7,6},{8,9},{9,8},{10,11... | collective-permute-start | bytes 4616 | tf_op jit(solution)/shard_map/ppermute | solution.py:183
  8.2 1.2 %collective-permute-start.4 = (bf16[4,4608]{1,0:T(4,128)(2,1)S(1)}, bf16[4,4608]{1,0:T(4,128)(2,1)S(1)}, u32[]{:S(2)}, u32[]{:S(2)}) collective-permute-start(bf16[4,4608]{1,0:T(4,128)(2,1)S(1)} %join.3.held_ref), channel_id=1, source_target_pairs={{0,3},{1,4},{2,7},{3,0},{4,1},{5,6},{6,5},{7,2},{8,13},{9,10},{10,... | collective-permute-start | bytes 110600 | tf_op jit(solution)/shard_map/ppermute | solution.py:183
  9.3 0.3 %collective-permute-done.1.got_ref = bf16[4,4608]{1,0:T(4,128)(2,1)S(1)} collective-permute-done((bf16[4,4608]{1,0:T(4,128)(2,1)S(1)}, bf16[4,4608]{1,0:T(4,128)(2,1)S(1)}, u32[]{:S(2)}, u32[]{:S(2)}) %collective-permute-start.1) | collective-permute-done | bytes 36896 | tf_op jit(solution)/shard_map/ppermute | solution.py:183
  9.7 1.5 %collective-permute-start.5 = (bf16[4,4608]{1,0:T(4,128)(2,1)S(1)}, bf16[4,4608]{1,0:T(4,128)(2,1)S(1)}, u32[]{:S(2)}, u32[]{:S(2)}) collective-permute-start(bf16[4,4608]{1,0:T(4,128)(2,1)S(1)} %collective-permute-done.1.got_ref), channel_id=1, source_target_pairs={{0,3},{1,4},{2,7},{3,0},{4,1},{5,6},{6,5},{7,2},{8,13},{9,10},{10,... | collective-permute-start | bytes 110600 | tf_op jit(solution)/shard_map/ppermute | solution.py:183
  11.2 0.4 %flip.1.own_flipped = bf16[4608,128]{1,0:T(8,128)(2,1)S(1)} custom-call(bf16[8,4608]{1,0:T(8,128)(2,1)S(1)} %join.4.after_ref.refs_ref, bf16[128,4608]{1,0:T(8,128)(2,1)S(1)} %get-tuple-element.15.p_ref.own_ref), custom_call_target="tpu_custom_call" | custom-call | flops 4000000000 | bytes 12000000 | tf_op jit(solution)/shard_map/flip/pallas_call | solution.py:216
  11.5 0.0 collective-permute-done.3.far_info
  11.5 0.8 %early.1 = (f32[12,8,256]{2,1,0:T(8,128)S(1)}, bf16[4608,128]{1,0:T(8,128)(2,1)S(1)}) custom-call(bf16[8,4608]{1,0:T(8,128)(2,1)S(1)} %join.4.after_ref.refs_ref, bf16[4608,128]{1,0:T(8,128)(2,1)S(1)} %flip.1.own_flipped, bf16[128,4608]{1,0:T(8,128)(2,1)S(1)} %collective-permute-done.2.far_ref, f32[3,128]{1,0:T(4,128)S(1)} %get-tuple-element.16.near_info, ...), custom_call_target="tpu_custom_call" | custom-call | flops 226492416 | bytes 4718592 | tf_op jit(solution)/shard_map/early/pallas_call | solution.py:225
  12.3 0.7 %collective-permute-done.5.got_ref = bf16[4,4608]{1,0:T(4,128)(2,1)S(1)} collective-permute-done((bf16[4,4608]{1,0:T(4,128)(2,1)S(1)}, bf16[4,4608]{1,0:T(4,128)(2,1)S(1)}, u32[]{:S(2)}, u32[]{:S(2)}) %collective-permute-start.5) | collective-permute-done | bytes 36896 | tf_op jit(solution)/shard_map/ppermute | solution.py:183
  13.1 0.6 %late.1 = (f32[12,8,256]{2,1,0:T(8,128)S(1)}, f32[1,256]{1,0:T(1,128)S(1)}) custom-call(bf16[8,4608]{1,0:T(8,128)(2,1)S(1)} %join.5.refs_ref, bf16[4608,128]{1,0:T(8,128)(2,1)S(1)} %flip.1.own_flipped, bf16[4608,128]{1,0:T(8,128)(2,1)S(1)} %get-tuple-element.18.rest_0_.far_flipped, f32[3,128]{1,0:T(4,128)S(1)} %get-tuple-element.16.near_info, ...), custom_call_target="tpu_custom_call" | custom-call | flops 226492416 | bytes 4718592 | tf_op jit(solution)/shard_map/late/pallas_call | solution.py:232
  13.7 0.3 %collective-permute-start.6 = (f32[1,256]{1,0:T(1,128)S(1)}, f32[1,256]{1,0:T(1,128)S(1)}, u32[]{:S(2)}, u32[]{:S(2)}) collective-permute-start(f32[1,256]{1,0:T(1,128)S(1)} %get-tuple-element.19.near_ref), channel_id=1, source_target_pairs={{0,1},{1,0},{2,3},{3,2},{4,5},{5,4},{6,7},{7,6},{8,9},{9,8},{10,11... | collective-permute-start | bytes 3080 | tf_op jit(solution)/shard_map/ppermute | solution.py:183
  14.1 0.9 %collective-permute-done.6.other_ref = f32[1,256]{1,0:T(1,128)S(1)} collective-permute-done((f32[1,256]{1,0:T(1,128)S(1)}, f32[1,256]{1,0:T(1,128)S(1)}, u32[]{:S(2)}, u32[]{:S(2)}) %collective-permute-start.6) | collective-permute-done | bytes 1056 | tf_op jit(solution)/shard_map/ppermute | solution.py:183
  14.9 0.7 %back_send.1 = bf16[8,4736]{1,0:T(8,128)(2,1)S(1)} custom-call(f32[12,8,256]{2,1,0:T(8,128)S(1)} %get-tuple-element.21.logits_ref, f32[1,256]{1,0:T(1,128)S(1)} %get-tuple-element.19.near_ref, f32[1,256]{1,0:T(1,128)S(1)} %collective-permute-done.6.other_ref, bf16[128,4608]{1,0:T(8,128)(2,1)S(1)} %get-tuple-element.15.p_ref.own_ref, ...), custom_call_target="tpu_custom_call" | custom-call | flops 226492416 | bytes 4718592 | tf_op jit(solution)/shard_map/back_send/pallas_call | solution.py:241
  15.7 1.6 %collective-permute-start.7 = (bf16[8,4736]{1,0:T(8,128)(2,1)S(1)}, bf16[8,4736]{1,0:T(8,128)(2,1)S(1)}, u32[]{:S(2)}, u32[]{:S(2)}) collective-permute-start(bf16[8,4736]{1,0:T(8,128)(2,1)S(1)} %back_send.1), channel_id=1, source_target_pairs={{0,3},{1,4},{2,7},{3,0},{4,1},{5,6},{6,5},{7,2},{8,13},{9,10},{10,... | collective-permute-start | bytes 227336 | tf_op jit(solution)/shard_map/ppermute | solution.py:183
  17.3 1.2 %back_keep.1 = (f32[8,4736]{1,0:T(8,128)S(1)}, f32[1,128]{1,0:T(1,128)}) custom-call(f32[12,8,256]{2,1,0:T(8,128)S(1)} %get-tuple-element.17.early_ref.logits_ref, f32[1,256]{1,0:T(1,128)S(1)} %get-tuple-element.19.near_ref, f32[1,256]{1,0:T(1,128)S(1)} %collective-permute-done.6.other_ref, bf16[128,4608]{1,0:T(8,128)(2,1)S(1)} %get-tuple-element.15.p_ref.own_ref, ...), custom_call_target="tpu_custom_call" | custom-call | flops 226492416 | bytes 4718592 | tf_op jit(solution)/shard_map/back_keep/pallas_call | solution.py:247
  18.4 1.1 %collective-permute-done.7 = bf16[8,4736]{1,0:T(8,128)(2,1)S(1)} collective-permute-done((bf16[8,4736]{1,0:T(8,128)(2,1)S(1)}, bf16[8,4736]{1,0:T(8,128)(2,1)S(1)}, u32[]{:S(2)}, u32[]{:S(2)}) %collective-permute-start.7) | collective-permute-done | bytes 75808 | tf_op jit(solution)/shard_map/ppermute | solution.py:183
  19.6 1.6 %collective-permute-start.8 = (bf16[4,4736]{1,0:T(4,128)(2,1)S(1)}, bf16[4,4736]{1,0:T(4,128)(2,1)S(1)}, u32[]{:S(2)}, u32[]{:S(2)}) collective-permute-start(bf16[4,4736]{1,0:T(4,128)(2,1)S(1)} %slice.25), channel_id=1, source_target_pairs={{0,5},{1,2},{2,1},{3,6},{4,7},{5,0},{6,3},{7,4},{8,11},{9,12},{10,... | collective-permute-start | bytes 113672 | tf_op jit(solution)/shard_map/ppermute | solution.py:183
  21.2 1.8 %collective-permute-done.8 = bf16[4,4736]{1,0:T(4,128)(2,1)S(1)} collective-permute-done((bf16[4,4736]{1,0:T(4,128)(2,1)S(1)}, bf16[4,4736]{1,0:T(4,128)(2,1)S(1)}, u32[]{:S(2)}, u32[]{:S(2)}) %collective-permute-start.8) | collective-permute-done | bytes 37920 | tf_op jit(solution)/shard_map/ppermute | solution.py:183
  23.1 3.1 %collective-permute-start.9 = (bf16[2,4736]{1,0:T(2,128)(2,1)S(1)}, bf16[2,4736]{1,0:T(2,128)(2,1)S(1)}, u32[]{:S(2)}, u32[]{:S(2)}) collective-permute-start(bf16[2,4736]{1,0:T(2,128)(2,1)S(1)} %slice.26), channel_id=1, source_target_pairs={{0,9},{1,8},{2,11},{3,10},{4,13},{5,12},{6,15},{7,14},{8,1},{9,0},... | collective-permute-start | bytes 56840 | tf_op jit(solution)/shard_map/ppermute | solution.py:183
  26.2 1.5 %collective-permute-done.9.got_ref = bf16[2,4736]{1,0:T(2,128)(2,1)S(1)} collective-permute-done((bf16[2,4736]{1,0:T(2,128)(2,1)S(1)}, bf16[2,4736]{1,0:T(2,128)(2,1)S(1)}, u32[]{:S(2)}, u32[]{:S(2)}) %collective-permute-start.9) | collective-permute-done | bytes 18976 | tf_op jit(solution)/shard_map/ppermute | solution.py:183
  27.6 0.6 %last.1 = (f32[2,4608]{1,0:T(2,128)}, f32[2]{0:T(128)}) custom-call(f32[2,4736]{1,0:T(2,128)S(1)} %slice.20.keep_ref, bf16[2,4736]{1,0:T(2,128)(2,1)S(1)} %collective-permute-done.9.got_ref), custom_call_target="tpu_custom_call" | custom-call | tf_op jit(solution)/shard_map/last/pallas_call | solution.py:260
  (11 shorter events, 0.2 us)
Async XLA Ops:
  0.6 5.6 %collective-permute-start = (bf16[2,4608]{1,0:T(2,128)(2,1)}, bf16[2,4608]{1,0:T(2,128)(2,1)S(1)}, u32[]{:S(2)}, u32[]{:S(2)}) collective-permute-start(bf16[2,4608]{1,0:T(2,128)(2,1)} %refs.1), channel_id=1, source_target_pairs={{0,9},{1,8},{2,11},{3,10},{4,13},{5,12},{6,15},{7,14},{8,1},{9,0},... | collective-permute-start | bytes 55304 | tf_op jit(solution)/shard_map/ppermute | solution.py:183
  4.2 7.4 %collective-permute-start.2 = (bf16[128,4608]{1,0:T(8,128)(2,1)}, bf16[128,4608]{1,0:T(8,128)(2,1)S(1)}, u32[]{:S(2)}, u32[]{:S(2)}) collective-permute-start(bf16[128,4608]{1,0:T(8,128)(2,1)} %particles.1), channel_id=1, source_target_pairs={{0,1},{1,0},{2,3},{3,2},{4,5},{5,4},{6,7},{7,6},{8,9},{9,8},{10,11... | collective-permute-start | bytes 3538952 | tf_op jit(solution)/shard_map/ppermute | solution.py:183
  6.2 3.4 %collective-permute-start.1 = (bf16[4,4608]{1,0:T(4,128)(2,1)S(1)}, bf16[4,4608]{1,0:T(4,128)(2,1)S(1)}, u32[]{:S(2)}, u32[]{:S(2)}) collective-permute-start(bf16[4,4608]{1,0:T(4,128)(2,1)S(1)} %join.3.held_ref), channel_id=1, source_target_pairs={{0,5},{1,2},{2,1},{3,6},{4,7},{5,0},{6,3},{7,4},{8,11},{9,12},{10,... | collective-permute-start | bytes 110600 | tf_op jit(solution)/shard_map/ppermute | solution.py:183
  7.8 3.7 %collective-permute-start.3 = (f32[3,128]{1,0:T(4,128)S(1)}, f32[3,128]{1,0:T(4,128)S(1)}, u32[]{:S(2)}, u32[]{:S(2)}) collective-permute-start(f32[3,128]{1,0:T(4,128)S(1)} %get-tuple-element.16.near_info), channel_id=1, source_target_pairs={{0,1},{1,0},{2,3},{3,2},{4,5},{5,4},{6,7},{7,6},{8,9},{9,8},{10,11... | collective-permute-start | bytes 4616 | tf_op jit(solution)/shard_map/ppermute | solution.py:183
  8.2 4.2 %collective-permute-start.4 = (bf16[4,4608]{1,0:T(4,128)(2,1)S(1)}, bf16[4,4608]{1,0:T(4,128)(2,1)S(1)}, u32[]{:S(2)}, u32[]{:S(2)}) collective-permute-start(bf16[4,4608]{1,0:T(4,128)(2,1)S(1)} %join.3.held_ref), channel_id=1, source_target_pairs={{0,3},{1,4},{2,7},{3,0},{4,1},{5,6},{6,5},{7,2},{8,13},{9,10},{10,... | collective-permute-start | bytes 110600 | tf_op jit(solution)/shard_map/ppermute | solution.py:183
  9.7 3.4 %collective-permute-start.5 = (bf16[4,4608]{1,0:T(4,128)(2,1)S(1)}, bf16[4,4608]{1,0:T(4,128)(2,1)S(1)}, u32[]{:S(2)}, u32[]{:S(2)}) collective-permute-start(bf16[4,4608]{1,0:T(4,128)(2,1)S(1)} %collective-permute-done.1.got_ref), channel_id=1, source_target_pairs={{0,3},{1,4},{2,7},{3,0},{4,1},{5,6},{6,5},{7,2},{8,13},{9,10},{10,... | collective-permute-start | bytes 110600 | tf_op jit(solution)/shard_map/ppermute | solution.py:183
  13.7 1.2 %collective-permute-start.6 = (f32[1,256]{1,0:T(1,128)S(1)}, f32[1,256]{1,0:T(1,128)S(1)}, u32[]{:S(2)}, u32[]{:S(2)}) collective-permute-start(f32[1,256]{1,0:T(1,128)S(1)} %get-tuple-element.19.near_ref), channel_id=1, source_target_pairs={{0,1},{1,0},{2,3},{3,2},{4,5},{5,4},{6,7},{7,6},{8,9},{9,8},{10,11... | collective-permute-start | bytes 3080 | tf_op jit(solution)/shard_map/ppermute | solution.py:183
  15.7 3.9 %collective-permute-start.7 = (bf16[8,4736]{1,0:T(8,128)(2,1)S(1)}, bf16[8,4736]{1,0:T(8,128)(2,1)S(1)}, u32[]{:S(2)}, u32[]{:S(2)}) collective-permute-start(bf16[8,4736]{1,0:T(8,128)(2,1)S(1)} %back_send.1), channel_id=1, source_target_pairs={{0,3},{1,4},{2,7},{3,0},{4,1},{5,6},{6,5},{7,2},{8,13},{9,10},{10,... | collective-permute-start | bytes 227336 | tf_op jit(solution)/shard_map/ppermute | solution.py:183
  19.6 3.5 %collective-permute-start.8 = (bf16[4,4736]{1,0:T(4,128)(2,1)S(1)}, bf16[4,4736]{1,0:T(4,128)(2,1)S(1)}, u32[]{:S(2)}, u32[]{:S(2)}) collective-permute-start(bf16[4,4736]{1,0:T(4,128)(2,1)S(1)} %slice.25), channel_id=1, source_target_pairs={{0,5},{1,2},{2,1},{3,6},{4,7},{5,0},{6,3},{7,4},{8,11},{9,12},{10,... | collective-permute-start | bytes 113672 | tf_op jit(solution)/shard_map/ppermute | solution.py:183
  23.1 4.5 %collective-permute-start.9 = (bf16[2,4736]{1,0:T(2,128)(2,1)S(1)}, bf16[2,4736]{1,0:T(2,128)(2,1)S(1)}, u32[]{:S(2)}, u32[]{:S(2)}) collective-permute-start(bf16[2,4736]{1,0:T(2,128)(2,1)S(1)} %slice.26), channel_id=1, source_target_pairs={{0,9},{1,8},{2,11},{3,10},{4,13},{5,12},{6,15},{7,14},{8,1},{9,0},... | collective-permute-start | bytes 56840 | tf_op jit(solution)/shard_map/ppermute | solution.py:183

commit v10 on v8

--- a/solution.py
+++ b/solution.py
@@ -141,9 +141,12 @@
     low = (post - high.astype(jnp.float32)).astype(jnp.bfloat16)
     both = jnp.concatenate([high, low], axis=0)
     group = FINE * classes
+    parts = []
     for c in range(0, CYCLES, 2):
         chunk = particles_of(own_ref, far_ref, c * ANGLES, 2 * ANGLES)
-        part = jnp.dot(both, chunk, preferred_element_type=jnp.float32)
+        parts.append(jnp.dot(both, chunk, preferred_element_type=jnp.float32))
+    for c in range(0, CYCLES, 2):
+        part = parts[c // 2]
         part = part[:count] + part[count:]
         for d in range(2):
             blocks = []

time: 28.4 us -> 28.4 us (level)
  no operation moved by 1% of the time
where the time goes in v10:
time: 28.4 us; the launch traced here: 28.3 us
  starting transfers between devices  15.4 us (54%)
  waiting for transfers between devices  6.27 us (22%)
  Pallas kernels  5.76 us (20%)
  between operations  0.74 us (3%)
    ppermute x10, starting transfers between devices, swap(): lax.ppermute(x, 'blk', [(i, i ^ (odd if i.bit_count() % 2 else even)) for...  15.4 us
    ppermute x10, waiting for transfers between devices, swap(): lax.ppermute(x, 'blk', [(i, i ^ (odd if i.bit_count() % 2 else even)) for...  6.27 us
    pallas_call x1, Pallas kernels, local(): pl.pallas_call(stage_kernel, out_shape=(jax.ShapeDtypeStruct((owned, widt...  1.35 us
    pallas_call x1, Pallas kernels, local(): pl.pallas_call(functools.partial(back_kernel, bits, owned, 0), out_shape=...  1.16 us
    pallas_call x1, Pallas kernels, local(): pl.pallas_call(early_kernel, out_shape=(jax.ShapeDtypeStruct((ROT, half,...  0.84 us
    pallas_call x1, Pallas kernels, local(): pl.pallas_call(functools.partial(back_kernel, bits, owned, half), out_sha...  0.72 us
    pallas_call x1, Pallas kernels, local(): pl.pallas_call(late_kernel, out_shape=(jax.ShapeDtypeStruct((ROT, half, b...  0.64 us
    pallas_call x1, Pallas kernels, local(): pl.pallas_call(last_kernel, out_shape=(jax.ShapeDtypeStruct((owned, width...  0.63 us
  transfers between devices with their start and end apart: 10, of which 6 were waited for; matrix products, arithmetic and copies ran while one was open for 0% of the time, Pallas kernels for 13%

profile of v10, /device:TPU:0, one launch (start us, length us, event | category | flops | bytes accessed | tf_op | source)
XLA Modules:
  0.0 28.3 jit_solution(16341649521477154757)
XLA Ops:
  0.6 3.5 %collective-permute-start = (bf16[2,4608]{1,0:T(2,128)(2,1)}, bf16[2,4608]{1,0:T(2,128)(2,1)S(1)}, u32[]{:S(2)}, u32[]{:S(2)}) collective-permute-start(bf16[2,4608]{1,0:T(2,128)(2,1)} %refs.1), channel_id=1, source_target_pairs={{0,9},{1,8},{2,11},{3,10},{4,13},{5,12},{6,15},{7,14},{8,1},{9,0},... | collective-permute-start | bytes 55304 | tf_op jit(solution)/shard_map/ppermute | solution.py:192
  4.2 0.7 %collective-permute-start.2 = (bf16[128,4608]{1,0:T(8,128)(2,1)}, bf16[128,4608]{1,0:T(8,128)(2,1)S(1)}, u32[]{:S(2)}, u32[]{:S(2)}) collective-permute-start(bf16[128,4608]{1,0:T(8,128)(2,1)} %particles.1), channel_id=1, source_target_pairs={{0,1},{1,0},{2,3},{3,2},{4,5},{5,4},{6,7},{7,6},{8,9},{9,8},{10,11... | collective-permute-start | bytes 3538952 | tf_op jit(solution)/shard_map/ppermute | solution.py:192
  4.8 1.4 %stage.1 = (bf16[2,4608]{1,0:T(2,128)(2,1)S(1)}, f32[3,128]{1,0:T(4,128)S(1)}, bf16[128,4608]{1,0:T(8,128)(2,1)S(1)}) custom-call(bf16[2,4608]{1,0:T(2,128)(2,1)} %refs.1, f32[1,128]{1,0:T(1,128)} %bitcast.4, s32[2,128]{1,0:T(2,128)} %bitcast.3, bf16[128,4608]{1,0:T(8,128)(2,1)} %particles.1), custom_call_target="tpu_custom_call" | custom-call | flops 4000000000 | bytes 12000000 | tf_op jit(solution)/shard_map/stage/pallas_call | solution.py:206
  6.2 1.6 %collective-permute-start.1 = (bf16[4,4608]{1,0:T(4,128)(2,1)S(1)}, bf16[4,4608]{1,0:T(4,128)(2,1)S(1)}, u32[]{:S(2)}, u32[]{:S(2)}) collective-permute-start(bf16[4,4608]{1,0:T(4,128)(2,1)S(1)} %join.3.held_ref), channel_id=1, source_target_pairs={{0,5},{1,2},{2,1},{3,6},{4,7},{5,0},{6,3},{7,4},{8,11},{9,12},{10,... | collective-permute-start | bytes 110600 | tf_op jit(solution)/shard_map/ppermute | solution.py:192
  7.8 0.3 %collective-permute-start.3 = (f32[3,128]{1,0:T(4,128)S(1)}, f32[3,128]{1,0:T(4,128)S(1)}, u32[]{:S(2)}, u32[]{:S(2)}) collective-permute-start(f32[3,128]{1,0:T(4,128)S(1)} %get-tuple-element.17.near_info), channel_id=1, source_target_pairs={{0,1},{1,0},{2,3},{3,2},{4,5},{5,4},{6,7},{7,6},{8,9},{9,8},{10,11... | collective-permute-start | bytes 4616 | tf_op jit(solution)/shard_map/ppermute | solution.py:192
  8.2 1.2 %collective-permute-start.4 = (bf16[4,4608]{1,0:T(4,128)(2,1)S(1)}, bf16[4,4608]{1,0:T(4,128)(2,1)S(1)}, u32[]{:S(2)}, u32[]{:S(2)}) collective-permute-start(bf16[4,4608]{1,0:T(4,128)(2,1)S(1)} %join.3.held_ref), channel_id=1, source_target_pairs={{0,3},{1,4},{2,7},{3,0},{4,1},{5,6},{6,5},{7,2},{8,13},{9,10},{10,... | collective-permute-start | bytes 110600 | tf_op jit(solution)/shard_map/ppermute | solution.py:192
  9.3 0.3 %collective-permute-done.1.got_ref = bf16[4,4608]{1,0:T(4,128)(2,1)S(1)} collective-permute-done((bf16[4,4608]{1,0:T(4,128)(2,1)S(1)}, bf16[4,4608]{1,0:T(4,128)(2,1)S(1)}, u32[]{:S(2)}, u32[]{:S(2)}) %collective-permute-start.1) | collective-permute-done | bytes 36896 | tf_op jit(solution)/shard_map/ppermute | solution.py:192
  9.7 1.5 %collective-permute-start.5 = (bf16[4,4608]{1,0:T(4,128)(2,1)S(1)}, bf16[4,4608]{1,0:T(4,128)(2,1)S(1)}, u32[]{:S(2)}, u32[]{:S(2)}) collective-permute-start(bf16[4,4608]{1,0:T(4,128)(2,1)S(1)} %collective-permute-done.1.got_ref), channel_id=1, source_target_pairs={{0,3},{1,4},{2,7},{3,0},{4,1},{5,6},{6,5},{7,2},{8,13},{9,10},{10,... | collective-permute-start | bytes 110600 | tf_op jit(solution)/shard_map/ppermute | solution.py:192
  11.2 0.4 %flip.1.own_flipped = bf16[4608,128]{1,0:T(8,128)(2,1)S(1)} custom-call(bf16[8,4608]{1,0:T(8,128)(2,1)S(1)} %join.4.after_ref.refs_ref, bf16[128,4608]{1,0:T(8,128)(2,1)S(1)} %get-tuple-element.16.p_ref.own_ref), custom_call_target="tpu_custom_call" | custom-call | flops 4000000000 | bytes 12000000 | tf_op jit(solution)/shard_map/flip/pallas_call | solution.py:225
  11.5 0.8 %early.1 = (f32[12,8,256]{2,1,0:T(8,128)S(1)}, bf16[4608,128]{1,0:T(8,128)(2,1)S(1)}, f32[2,256]{1,0:T(2,128)S(1)}) custom-call(bf16[8,4608]{1,0:T(8,128)(2,1)S(1)} %join.4.after_ref.refs_ref, bf16[4608,128]{1,0:T(8,128)(2,1)S(1)} %flip.1.own_flipped, bf16[128,4608]{1,0:T(8,128)(2,1)S(1)} %collective-permute-done.2.far_ref, ...), custom_call_target="tpu_custom_call" | custom-call | flops 226492416 | bytes 4718592 | tf_op jit(solution)/shard_map/early/pallas_call | solution.py:234
  12.4 0.0 collective-permute-done.4.held_ref
  12.4 0.7 %collective-permute-done.5.got_ref = bf16[4,4608]{1,0:T(4,128)(2,1)S(1)} collective-permute-done((bf16[4,4608]{1,0:T(4,128)(2,1)S(1)}, bf16[4,4608]{1,0:T(4,128)(2,1)S(1)}, u32[]{:S(2)}, u32[]{:S(2)}) %collective-permute-start.5) | collective-permute-done | bytes 36896 | tf_op jit(solution)/shard_map/ppermute | solution.py:192
  13.1 0.6 %late.1 = (f32[12,8,256]{2,1,0:T(8,128)S(1)}, f32[1,256]{1,0:T(1,128)S(1)}) custom-call(bf16[8,4608]{1,0:T(8,128)(2,1)S(1)} %join.5.refs_ref, bf16[4608,128]{1,0:T(8,128)(2,1)S(1)} %flip.1.own_flipped, bf16[4608,128]{1,0:T(8,128)(2,1)S(1)} %get-tuple-element.19.rest_0_.far_flipped, f32[3,128]{1,0:T(4,128)S(1)} %get-tuple-element.17.near_info, ...), custom_call_target="tpu_custom_call" | custom-call | flops 226492416 | bytes 4718592 | tf_op jit(solution)/shard_map/late/pallas_call | solution.py:245
  13.7 0.3 %collective-permute-start.6 = (f32[1,256]{1,0:T(1,128)S(1)}, f32[1,256]{1,0:T(1,128)S(1)}, u32[]{:S(2)}, u32[]{:S(2)}) collective-permute-start(f32[1,256]{1,0:T(1,128)S(1)} %get-tuple-element.21.near_ref), channel_id=1, source_target_pairs={{0,1},{1,0},{2,3},{3,2},{4,5},{5,4},{6,7},{7,6},{8,9},{9,8},{10,11... | collective-permute-start | bytes 3080 | tf_op jit(solution)/shard_map/ppermute | solution.py:192
  14.1 0.9 %collective-permute-done.6.other_ref = f32[1,256]{1,0:T(1,128)S(1)} collective-permute-done((f32[1,256]{1,0:T(1,128)S(1)}, f32[1,256]{1,0:T(1,128)S(1)}, u32[]{:S(2)}, u32[]{:S(2)}) %collective-permute-start.6) | collective-permute-done | bytes 1056 | tf_op jit(solution)/shard_map/ppermute | solution.py:192
  14.9 0.7 %back_send.1 = bf16[8,4736]{1,0:T(8,128)(2,1)S(1)} custom-call(f32[12,8,256]{2,1,0:T(8,128)S(1)} %get-tuple-element.23.logits_ref, f32[1,256]{1,0:T(1,128)S(1)} %get-tuple-element.21.near_ref, f32[1,256]{1,0:T(1,128)S(1)} %collective-permute-done.6.other_ref, bf16[128,4608]{1,0:T(8,128)(2,1)S(1)} %get-tuple-element.16.p_ref.own_ref, ...), custom_call_target="tpu_custom_call" | custom-call | flops 226492416 | bytes 4718592 | tf_op jit(solution)/shard_map/back_send/pallas_call | solution.py:254
  15.7 1.6 %collective-permute-start.7 = (bf16[8,4736]{1,0:T(8,128)(2,1)S(1)}, bf16[8,4736]{1,0:T(8,128)(2,1)S(1)}, u32[]{:S(2)}, u32[]{:S(2)}) collective-permute-start(bf16[8,4736]{1,0:T(8,128)(2,1)S(1)} %back_send.1), channel_id=1, source_target_pairs={{0,3},{1,4},{2,7},{3,0},{4,1},{5,6},{6,5},{7,2},{8,13},{9,10},{10,... | collective-permute-start | bytes 227336 | tf_op jit(solution)/shard_map/ppermute | solution.py:192
  17.3 1.2 %back_keep.1 = (f32[8,4736]{1,0:T(8,128)S(1)}, f32[1,128]{1,0:T(1,128)}) custom-call(f32[12,8,256]{2,1,0:T(8,128)S(1)} %get-tuple-element.18.logits_ref, f32[1,256]{1,0:T(1,128)S(1)} %get-tuple-element.21.near_ref, f32[1,256]{1,0:T(1,128)S(1)} %collective-permute-done.6.other_ref, bf16[128,4608]{1,0:T(8,128)(2,1)S(1)} %get-tuple-element.16.p_ref.own_ref, ...), custom_call_target="tpu_custom_call" | custom-call | flops 226492416 | bytes 4718592 | tf_op jit(solution)/shard_map/back_keep/pallas_call | solution.py:260
  18.4 1.1 %collective-permute-done.7 = bf16[8,4736]{1,0:T(8,128)(2,1)S(1)} collective-permute-done((bf16[8,4736]{1,0:T(8,128)(2,1)S(1)}, bf16[8,4736]{1,0:T(8,128)(2,1)S(1)}, u32[]{:S(2)}, u32[]{:S(2)}) %collective-permute-start.7) | collective-permute-done | bytes 75808 | tf_op jit(solution)/shard_map/ppermute | solution.py:192
  19.6 1.6 %collective-permute-start.8 = (bf16[4,4736]{1,0:T(4,128)(2,1)S(1)}, bf16[4,4736]{1,0:T(4,128)(2,1)S(1)}, u32[]{:S(2)}, u32[]{:S(2)}) collective-permute-start(bf16[4,4736]{1,0:T(4,128)(2,1)S(1)} %slice.25), channel_id=1, source_target_pairs={{0,5},{1,2},{2,1},{3,6},{4,7},{5,0},{6,3},{7,4},{8,11},{9,12},{10,... | collective-permute-start | bytes 113672 | tf_op jit(solution)/shard_map/ppermute | solution.py:192
  21.2 1.8 %collective-permute-done.8 = bf16[4,4736]{1,0:T(4,128)(2,1)S(1)} collective-permute-done((bf16[4,4736]{1,0:T(4,128)(2,1)S(1)}, bf16[4,4736]{1,0:T(4,128)(2,1)S(1)}, u32[]{:S(2)}, u32[]{:S(2)}) %collective-permute-start.8) | collective-permute-done | bytes 37920 | tf_op jit(solution)/shard_map/ppermute | solution.py:192
  23.1 3.1 %collective-permute-start.9 = (bf16[2,4736]{1,0:T(2,128)(2,1)S(1)}, bf16[2,4736]{1,0:T(2,128)(2,1)S(1)}, u32[]{:S(2)}, u32[]{:S(2)}) collective-permute-start(bf16[2,4736]{1,0:T(2,128)(2,1)S(1)} %slice.26), channel_id=1, source_target_pairs={{0,9},{1,8},{2,11},{3,10},{4,13},{5,12},{6,15},{7,14},{8,1},{9,0},... | collective-permute-start | bytes 56840 | tf_op jit(solution)/shard_map/ppermute | solution.py:192
  26.2 1.5 %collective-permute-done.9.got_ref = bf16[2,4736]{1,0:T(2,128)(2,1)S(1)} collective-permute-done((bf16[2,4736]{1,0:T(2,128)(2,1)S(1)}, bf16[2,4736]{1,0:T(2,128)(2,1)S(1)}, u32[]{:S(2)}, u32[]{:S(2)}) %collective-permute-start.9) | collective-permute-done | bytes 18976 | tf_op jit(solution)/shard_map/ppermute | solution.py:192
  27.6 0.6 %last.1 = (f32[2,4608]{1,0:T(2,128)}, f32[2]{0:T(128)}) custom-call(f32[2,4736]{1,0:T(2,128)S(1)} %slice.20.keep_ref, bf16[2,4736]{1,0:T(2,128)(2,1)S(1)} %collective-permute-done.9.got_ref), custom_call_target="tpu_custom_call" | custom-call | tf_op jit(solution)/shard_map/last/pallas_call | solution.py:273
  (11 shorter events, 0.2 us)
Async XLA Ops:
  0.6 5.6 %collective-permute-start = (bf16[2,4608]{1,0:T(2,128)(2,1)}, bf16[2,4608]{1,0:T(2,128)(2,1)S(1)}, u32[]{:S(2)}, u32[]{:S(2)}) collective-permute-start(bf16[2,4608]{1,0:T(2,128)(2,1)} %refs.1), channel_id=1, source_target_pairs={{0,9},{1,8},{2,11},{3,10},{4,13},{5,12},{6,15},{7,14},{8,1},{9,0},... | collective-permute-start | bytes 55304 | tf_op jit(solution)/shard_map/ppermute | solution.py:192
  4.2 7.4 %collective-permute-start.2 = (bf16[128,4608]{1,0:T(8,128)(2,1)}, bf16[128,4608]{1,0:T(8,128)(2,1)S(1)}, u32[]{:S(2)}, u32[]{:S(2)}) collective-permute-start(bf16[128,4608]{1,0:T(8,128)(2,1)} %particles.1), channel_id=1, source_target_pairs={{0,1},{1,0},{2,3},{3,2},{4,5},{5,4},{6,7},{7,6},{8,9},{9,8},{10,11... | collective-permute-start | bytes 3538952 | tf_op jit(solution)/shard_map/ppermute | solution.py:192
  6.2 3.4 %collective-permute-start.1 = (bf16[4,4608]{1,0:T(4,128)(2,1)S(1)}, bf16[4,4608]{1,0:T(4,128)(2,1)S(1)}, u32[]{:S(2)}, u32[]{:S(2)}) collective-permute-start(bf16[4,4608]{1,0:T(4,128)(2,1)S(1)} %join.3.held_ref), channel_id=1, source_target_pairs={{0,5},{1,2},{2,1},{3,6},{4,7},{5,0},{6,3},{7,4},{8,11},{9,12},{10,... | collective-permute-start | bytes 110600 | tf_op jit(solution)/shard_map/ppermute | solution.py:192
  7.8 3.7 %collective-permute-start.3 = (f32[3,128]{1,0:T(4,128)S(1)}, f32[3,128]{1,0:T(4,128)S(1)}, u32[]{:S(2)}, u32[]{:S(2)}) collective-permute-start(f32[3,128]{1,0:T(4,128)S(1)} %get-tuple-element.17.near_info), channel_id=1, source_target_pairs={{0,1},{1,0},{2,3},{3,2},{4,5},{5,4},{6,7},{7,6},{8,9},{9,8},{10,11... | collective-permute-start | bytes 4616 | tf_op jit(solution)/shard_map/ppermute | solution.py:192
  8.2 4.2 %collective-permute-start.4 = (bf16[4,4608]{1,0:T(4,128)(2,1)S(1)}, bf16[4,4608]{1,0:T(4,128)(2,1)S(1)}, u32[]{:S(2)}, u32[]{:S(2)}) collective-permute-start(bf16[4,4608]{1,0:T(4,128)(2,1)S(1)} %join.3.held_ref), channel_id=1, source_target_pairs={{0,3},{1,4},{2,7},{3,0},{4,1},{5,6},{6,5},{7,2},{8,13},{9,10},{10,... | collective-permute-start | bytes 110600 | tf_op jit(solution)/shard_map/ppermute | solution.py:192
  9.7 3.4 %collective-permute-start.5 = (bf16[4,4608]{1,0:T(4,128)(2,1)S(1)}, bf16[4,4608]{1,0:T(4,128)(2,1)S(1)}, u32[]{:S(2)}, u32[]{:S(2)}) collective-permute-start(bf16[4,4608]{1,0:T(4,128)(2,1)S(1)} %collective-permute-done.1.got_ref), channel_id=1, source_target_pairs={{0,3},{1,4},{2,7},{3,0},{4,1},{5,6},{6,5},{7,2},{8,13},{9,10},{10,... | collective-permute-start | bytes 110600 | tf_op jit(solution)/shard_map/ppermute | solution.py:192
  13.7 1.2 %collective-permute-start.6 = (f32[1,256]{1,0:T(1,128)S(1)}, f32[1,256]{1,0:T(1,128)S(1)}, u32[]{:S(2)}, u32[]{:S(2)}) collective-permute-start(f32[1,256]{1,0:T(1,128)S(1)} %get-tuple-element.21.near_ref), channel_id=1, source_target_pairs={{0,1},{1,0},{2,3},{3,2},{4,5},{5,4},{6,7},{7,6},{8,9},{9,8},{10,11... | collective-permute-start | bytes 3080 | tf_op jit(solution)/shard_map/ppermute | solution.py:192
  15.7 3.9 %collective-permute-start.7 = (bf16[8,4736]{1,0:T(8,128)(2,1)S(1)}, bf16[8,4736]{1,0:T(8,128)(2,1)S(1)}, u32[]{:S(2)}, u32[]{:S(2)}) collective-permute-start(bf16[8,4736]{1,0:T(8,128)(2,1)S(1)} %back_send.1), channel_id=1, source_target_pairs={{0,3},{1,4},{2,7},{3,0},{4,1},{5,6},{6,5},{7,2},{8,13},{9,10},{10,... | collective-permute-start | bytes 227336 | tf_op jit(solution)/shard_map/ppermute | solution.py:192
  19.6 3.5 %collective-permute-start.8 = (bf16[4,4736]{1,0:T(4,128)(2,1)S(1)}, bf16[4,4736]{1,0:T(4,128)(2,1)S(1)}, u32[]{:S(2)}, u32[]{:S(2)}) collective-permute-start(bf16[4,4736]{1,0:T(4,128)(2,1)S(1)} %slice.25), channel_id=1, source_target_pairs={{0,5},{1,2},{2,1},{3,6},{4,7},{5,0},{6,3},{7,4},{8,11},{9,12},{10,... | collective-permute-start | bytes 113672 | tf_op jit(solution)/shard_map/ppermute | solution.py:192
  23.1 4.5 %collective-permute-start.9 = (bf16[2,4736]{1,0:T(2,128)(2,1)S(1)}, bf16[2,4736]{1,0:T(2,128)(2,1)S(1)}, u32[]{:S(2)}, u32[]{:S(2)}) collective-permute-start(bf16[2,4736]{1,0:T(2,128)(2,1)S(1)} %slice.26), channel_id=1, source_target_pairs={{0,9},{1,8},{2,11},{3,10},{4,13},{5,12},{6,15},{7,14},{8,1},{9,0},... | collective-permute-start | bytes 56840 | tf_op jit(solution)/shard_map/ppermute | solution.py:192
